TPU v7x, 32 devices: a whole 2x2x4 slice. The times are simulated.
32 devices in a mesh: grp: 2 (over x), tp: 16 (over z, y, core).
Axes of the slice: x: 2, y: 2, z: 4, core: 2. Of those that a mesh axis runs over, the one named last changes fastest.
Arguments:
- attn_in: bfloat16 [2, 4096, 8192], P(None, 'tp', 'grp'), parts along dimension 2, may hold values from -6 to 6
- attn_grad: bfloat16 [2, 4096, 8192], P(None, 'tp', 'grp'), parts along dimension 2, may hold values from -6 to 6
- ffn_in: bfloat16 [2, 14336, 8192], P(None, 'tp', 'grp'), parts along dimension 2, may hold values from -6 to 6
- ffn_grad: bfloat16 [2, 4096, 8192], P(None, 'tp', 'grp'), parts along dimension 2, may hold values from -6 to 6
- proj_attn_in: bfloat16 [2, 4096, 64], P(None, 'tp'), may hold values from -0.09375 to 0.09375
- proj_attn_out: bfloat16 [2, 4096, 64], P(None, 'tp'), may hold values from -0.09375 to 0.09375
- proj_ffn_in: bfloat16 [2, 14336, 64], P(None, 'tp'), may hold values from -0.046875 to 0.046875
- proj_ffn_out: bfloat16 [2, 4096, 64], P(None, 'tp'), may hold values from -0.09375 to 0.09375
- test_grads: bfloat16 [1024, 16384], P(None, 'tp'), may hold values from -0.0009765625 to 0.0009765625
Outputs:
- scores: float32 [4, 1024], P('grp'), parts along dimension 0
There are 2 independent parts, one for each index of `grp`. A program takes and returns all parts, laid end to end along the dimension named above; an argument that names none is the same for every part. Nothing has to cross between parts.
All inputs are finite; a program needn't handle non-finite values.
Results may differ from a plain program's by a relative error of at most 0.0003.
Values may be sent and summed in bfloat16 or wider, within the bound.
No kernel may reach another device: no remote copies, remote signals or barrier semaphores. Data moves between devices by JAX's collectives and lax.ppermute only.
A program may use at most 192 MiB of HBM per device.

v0:
```python
import jax
import jax.numpy as jnp
from jax import lax
from jax.sharding import PartitionSpec as P

LEN = 2048
SEQS = 2


def project_all(acts, projs):
    layers = acts[0].shape[0]
    columns = []
    for layer in range(layers):
        for source, weight in zip(acts, projs):
            columns.append(
                lax.dot_general(
                    source[layer],
                    weight[layer],
                    (((0,), (0,)), ((), ())),
                    preferred_element_type=jnp.float32,
                )
            )
    return jnp.concatenate(columns, axis=1)


def shards(
    attn_in,
    attn_grad,
    ffn_in,
    ffn_grad,
    proj_attn_in,
    proj_attn_out,
    proj_ffn_in,
    proj_ffn_out,
    test_grads,
):
    layers = attn_in.shape[0]
    total = attn_in.shape[2]
    width_k = proj_attn_in.shape[2]
    devices = lax.axis_size("tp")
    rows = total // devices
    acts = (attn_in, attn_grad, ffn_in, ffn_grad)
    projs = (proj_attn_in, proj_attn_out, proj_ffn_in, proj_ffn_out)
    sliced = tuple((source for source in acts))
    projected = lax.psum_scatter(project_all(sliced, projs), "tp", scatter_dimension=0, tiled=True)
    first_token = lax.axis_index("tp") * rows
    token_index = first_token + jnp.arange(rows, dtype=jnp.int32)
    sequence = token_index // LEN
    onehot = (sequence[:, None] == jnp.arange(SEQS, dtype=jnp.int32)[None, :]).astype(jnp.float32)
    pieces = []
    for layer in range(layers):
        base = layer * 4 * width_k
        for module in range(2):
            inputs = projected[:, base + 2 * module * width_k : base + (2 * module + 1) * width_k]
            grads = projected[
                :, base + (2 * module + 1) * width_k : base + (2 * module + 2) * width_k
            ]
            outer = jnp.einsum(
                "ts,ta,tb->sab", onehot, grads, inputs, precision=lax.Precision.HIGHEST
            )
            pieces.append(outer.reshape(SEQS, width_k * width_k))
    flat = jnp.concatenate(pieces, axis=1)
    owned = lax.psum_scatter(flat, "tp", scatter_dimension=1, tiled=True)
    tests = test_grads.astype(jnp.float32)
    partial_scores = lax.dot_general(
        owned,
        tests,
        (((1,), (1,)), ((), ())),
        precision=lax.Precision.HIGHEST,
        preferred_element_type=jnp.float32,
    )
    return lax.psum(partial_scores, "tp")


def solution(mesh):
    placed = (
        P(None, "tp", "grp"),
        P(None, "tp", "grp"),
        P(None, "tp", "grp"),
        P(None, "tp", "grp"),
        P(None, "tp", None),
        P(None, "tp", None),
        P(None, "tp", None),
        P(None, "tp", None),
        P(None, "tp"),
    )
    return jax.shard_map(
        shards, mesh=mesh, in_specs=placed, out_specs=P("grp", None), check_vma=False
    )
```

profile of v0, /device:TPU:0, one launch (start us, length us, event | category | flops | bytes accessed | tf_op | source)
XLA Modules:
  0.0 293.6 jit_solution(12773371512289010979)
XLA Ops:
  6.5 0.0 copy-start
  6.5 0.0 copy-start.6
  6.5 0.0 reduce-scatter.5.cloned.1.call-start
  6.5 0.0 copy-start.3
  6.5 3.2 %convolution_dynamic-update-slice_fusion.5 = f32[4096,512]{0,1:T(8,128)} fusion(bf16[2,256,4096]{2,1,0:T(8,128)(2,1)} %param.9, bf16[2,256,64]{1,2,0:T(8,128)(2,1)} %param.13), kind=kOutput, calls=%fused_computation.11 | convolution fusion | flops 134217728 | bytes 3178496 | tf_op jit(solution)/shard_map/dot_general | solution.py:16
  9.8 0.0 copy-start.1
  9.8 0.0 copy-start.4
  9.8 3.3 %convolution_dynamic-update-slice_fusion.4 = f32[4096,512]{0,1:T(8,128)} fusion(f32[4096,512]{0,1:T(8,128)} %convolution_dynamic-update-slice_fusion.5, bf16[2,256,4096]{2,1,0:T(8,128)(2,1)} %param.10, bf16[2,256,64]{1,2,0:T(8,128)(2,1)} %param.14), kind=kOutput, calls=%fused_computation.10 | convolution fusion | flops 134217728 | bytes 3178496 | tf_op jit(solution)/shard_map/dot_general | solution.py:16
  13.0 0.0 copy-start.2
  13.1 0.0 copy-start.5
  13.1 0.0 copy-start.7
  13.1 5.7 %fusion.6 = f32[4096,512]{0,1:T(8,128)} fusion(f32[4096,512]{0,1:T(8,128)} %convolution_dynamic-update-slice_fusion.4, bf16[2,896,4096]{2,1,0:T(8,128)(2,1)} %param.11, bf16[2,896,64]{1,2,0:T(8,128)(2,1)} %param.15), kind=kOutput, calls=%fused_computation.12 | convolution fusion | flops 469762048 | bytes 8503296 | tf_op jit(solution)/shard_map/dot_general | solution.py:16
  18.8 0.0 copy-done.6
  18.8 0.0 copy-done.3
  18.8 1.5 convolution_dynamic-update-slice_fusion.3
  20.2 0.0 copy-done.1
  20.2 0.0 copy-done.4
  20.2 1.5 convolution_dynamic-update-slice_fusion.2
  21.7 0.0 copy-done.2
  21.7 0.0 copy-done.5
  21.7 1.5 convolution_dynamic-update-slice_fusion.1
  23.2 0.0 copy-done.7
  23.2 5.5 %fusion.9 = f32[4096,512]{0,1:T(8,128)} fusion(f32[4096,512]{0,1:T(8,128)} %convolution_dynamic-update-slice_fusion.1, bf16[2,896,4096]{2,1,0:T(8,128)(2,1)} %param.11, bf16[2,896,64]{1,2,0:T(8,128)(2,1)S(1)} %copy-done.7), kind=kOutput, calls=%fused_computation.13 | convolution fusion | flops 469762048 | bytes 8503296 | tf_op jit(solution)/shard_map/dot_general | solution.py:16
  28.7 1.5 convolution_dynamic-update-slice_fusion
  30.2 0.0 reduce-scatter.5.cloned.1.call-update
  30.2 0.0 reduce-scatter.7.cloned.1.call-start
  30.3 106.4 %reduce-scatter.5.cloned.1.call-done = f32[256,512]{0,1:T(8,128)} async-done(((f32[4096,512]{0,1:T(8,128)}), f32[256,512]{0,1:T(8,128)}) %reduce-scatter.5.cloned.1.call-update) | async-done | bytes 524304 | tf_op jit(solution)/shard_map/reduce_scatter | solution.py:45
  136.7 1.0 fusion.54
  137.6 1.1 convolution_bitcast_fusion.3
  138.7 0.1 reshape.31
  138.8 1.1 convolution_bitcast_fusion.2
  139.9 0.1 reshape.32
  140.0 1.1 convolution_bitcast_fusion.1
  141.1 0.1 reshape.33
  141.2 1.1 convolution_bitcast_fusion
  142.3 0.1 reshape.34
  142.4 0.1 pad_maximum_fusion
  142.5 5.0 %copy.10 = f32[2,16384]{0,1:T(8,128)} copy(f32[2,16384]{1,0:T(2,128)S(1)} %pad_maximum_fusion) | data formatting | bytes 262144
  147.5 0.0 reduce-scatter.7.cloned.1.call-update
  147.5 103.2 %reduce-scatter.7.cloned.1.call-done = f32[1024,2]{1,0:T(8,128)} async-done(((f32[16384,2]{1,0:T(8,128)}), f32[1024,2]{1,0:T(8,128)}) %reduce-scatter.7.cloned.1.call-update) | async-done | bytes 8208
  250.7 0.0 copy-done
  250.7 2.8 fusion.24
  253.5 33.2 %psum.7 = f32[2,1024]{1,0:T(2,128)} all-reduce(f32[2,1024]{1,0:T(2,128)S(1)} %fusion.24), channel_id=1, replica_groups=mesh['grp'=2,'tp'=16] {'tp'}, use_global_device_ids=true, to_apply=%region_2.3 | all-reduce | flops 2048 | bytes 16384 | tf_op jit(solution)/shard_map/psum | solution.py:72
  (2 shorter events, 0.0 us)
Async XLA Ops:
  6.5 244.2 %copy-start = (bf16[1024,1024]{1,0:T(8,128)(2,1)S(1)}, bf16[1024,1024]{1,0:T(8,128)(2,1)}, u32[]{:S(2)}) copy-start(bf16[1024,1024]{1,0:T(8,128)(2,1)} %param.17) | copy-start | bytes 6291460
  6.5 12.2 %copy-start.6 = (bf16[2,256,64]{1,2,0:T(8,128)(2,1)S(1)}, bf16[2,256,64]{1,2,0:T(8,128)(2,1)}, u32[]{:S(2)}) copy-start(bf16[2,256,64]{1,2,0:T(8,128)(2,1)} %param.16) | copy-start | bytes 196612
  6.5 130.1 %reduce-scatter.5.cloned.1.call-start = ((), (), s32[]{:S(2)}) async-start(), calls=%async_computation.2 | async-start | bytes 8912896 | tf_op jit(solution)/shard_map/reduce_scatter | solution.py:45
  6.5 12.2 %copy-start.3 = (bf16[2,256,4096]{2,1,0:T(8,128)(2,1)S(1)}, bf16[2,256,4096]{2,1,0:T(8,128)(2,1)}, u32[]{:S(2)}) copy-start(bf16[2,256,4096]{2,1,0:T(8,128)(2,1)} %param.12) | copy-start | bytes 12582916
  9.8 10.5 %copy-start.1 = (bf16[2,256,4096]{2,1,0:T(8,128)(2,1)S(1)}, bf16[2,256,4096]{2,1,0:T(8,128)(2,1)}, u32[]{:S(2)}) copy-start(bf16[2,256,4096]{2,1,0:T(8,128)(2,1)} %param.9) | copy-start | bytes 12582916
  9.8 10.5 %copy-start.4 = (bf16[2,256,64]{1,2,0:T(8,128)(2,1)S(1)}, bf16[2,256,64]{1,2,0:T(8,128)(2,1)}, u32[]{:S(2)}) copy-start(bf16[2,256,64]{1,2,0:T(8,128)(2,1)} %param.13) | copy-start | bytes 196612
  13.0 8.6 %copy-start.2 = (bf16[2,256,4096]{2,1,0:T(8,128)(2,1)S(1)}, bf16[2,256,4096]{2,1,0:T(8,128)(2,1)}, u32[]{:S(2)}) copy-start(bf16[2,256,4096]{2,1,0:T(8,128)(2,1)} %param.10) | copy-start | bytes 12582916
  13.1 8.6 %copy-start.5 = (bf16[2,256,64]{1,2,0:T(8,128)(2,1)S(1)}, bf16[2,256,64]{1,2,0:T(8,128)(2,1)}, u32[]{:S(2)}) copy-start(bf16[2,256,64]{1,2,0:T(8,128)(2,1)} %param.14) | copy-start | bytes 196612
  13.1 10.1 %copy-start.7 = (bf16[2,896,64]{1,2,0:T(8,128)(2,1)S(1)}, bf16[2,896,64]{1,2,0:T(8,128)(2,1)}, u32[]{:S(2)}) copy-start(bf16[2,896,64]{1,2,0:T(8,128)(2,1)} %param.15) | copy-start | bytes 688132
  30.2 220.5 %reduce-scatter.7.cloned.1.call-start = ((), (), s32[]{:S(2)}) async-start(), calls=%async_computation.3 | async-start | bytes 8912896
Sparse Core Ops, SparseCore 0:
  30.3 106.3 reduce-scatter.4
  147.6 103.0 reduce-scatter.6
where the time goes:
time: 294 us
  waiting for transfers between devices  210 us (71%)
  blocking collectives  33.2 us (11%)
  matrix products  30.8 us (10%)
  between operations  13.5 us (5%)
  local copies, waits for them, and re-layouts  6.31 us (2%)
    reduce_scatter x1, waiting for transfers between devices, shards(): lax.psum_scatter(project_all(sliced, projs), 'tp', scatter_dimension=0, t...  106 us
    unnamed x3, waiting for transfers between devices  103 us
    psum x1, blocking collectives, shards(): return lax.psum(partial_scores, 'tp')  33.2 us
    dot_general x8, matrix products, project_all(): lax.dot_general(source[layer], weight[layer], (((0,), (0,)), ((), ())), p...  23.6 us
  transfers between devices with their start and end apart: 2, of which 2 were waited for; matrix products, arithmetic and copies ran while one was open for 0% of the time, Pallas kernels for 0%

commit v1 on v0

v1 whole, which is shorter than its diff:
```python
import functools

import jax
import jax.numpy as jnp
from jax import lax
from jax.experimental import pallas as pl
from jax.experimental.pallas import tpu as pltpu
from jax.sharding import PartitionSpec as P

LEN = 2048
SEQS = 2
K = 64
F32 = jnp.float32
BF16 = jnp.bfloat16
SPAN = 250.0
HIGH = lax.Precision.HIGHEST


def encode(values, codes_ref, row, scales_ref, index):
    top = jnp.max(jnp.abs(values), axis=0, keepdims=True)
    scale = (top * 1.015625).astype(BF16).astype(F32)
    scales_ref[index : index + 1, :] = scale
    factor = jnp.where(scale > 2e-36, SPAN / jnp.maximum(scale, 2e-36), 0.0)
    power = jnp.exp2(jnp.abs(values) * factor - 0.5 * SPAN)
    codes_ref[row : row + K, :] = jnp.where(values < 0, -power, power).astype(BF16)


def decode(codes_ref, row, scales, index):
    codes = codes_ref[row : row + K, :].astype(F32)
    scale = scales[index : index + 1, :] * (1.0 / SPAN)
    size = (jnp.log2(jnp.abs(codes)) + 0.5 * SPAN) * scale
    return jnp.where(codes < 0, -size, size)


def encode_rows(pieces, codes_ref, scales_ref):
    scales_ref[...] = jnp.zeros_like(scales_ref)
    for index, piece in enumerate(pieces):
        encode(piece, codes_ref, index * K, scales_ref, index)
    base = len(pieces) * K
    codes_ref[base : base + 16, :] = scales_ref[...].astype(BF16)


def read_scales(codes_ref, groups):
    return codes_ref[groups * K : groups * K + 16, :].astype(F32)


def project(l, m, which, acts, projs):
    a = acts[m * 2 + which]
    w = projs[m * 2 + which]
    return jnp.dot(w[l], a[l], preferred_element_type=F32)


def send_kernel(where_ref, a0, a1, a2, a3, w0, w1, w2, w3, out_ref):
    acts, projs = (a0, a1, a2, a3), (w0, w1, w2, w3)
    for l in range(2):
        for m in range(2):
            for which in range(2):
                row = ((l * 2 + m) * 2 + which) * K
                out_ref[row : row + K, :] = project(l, m, which, acts, projs)


def keep_y_kernel(where_ref, a0, a1, a2, a3, w0, w1, w2, w3, got_ref, codes_ref, kept_ref, scales_ref):
    acts, projs = (a0, a1, a2, a3), (w0, w1, w2, w3)
    step = pl.program_id(0)

    def pieces():
        for l in range(2):
            for m in range(2):
                for which in range(2):
                    row = ((l * 2 + m) * 2 + which) * K
                    yield project(l, m, which, acts, projs) + got_ref[row : row + K, :]

    @pl.when(step == 0)
    def _():
        encode_rows(list(pieces()), codes_ref, scales_ref)

    @pl.when(step == 1)
    def _():
        for index, piece in enumerate(pieces()):
            kept_ref[index // 4, (index // 2) % 2, (index % 2) * K : (index % 2) * K + K, :] = piece


def keep_z_kernel(where_ref, a0, a1, a2, a3, w0, w1, w2, w3, got_ref, codes_ref, kept_ref, total_ref, scales_ref):
    acts, projs = (a0, a1, a2, a3), (w0, w1, w2, w3)
    for l in range(2):
        for m in range(2):
            for which in range(2):
                row = ((l * 2 + m) * 2 + which) * K
                total_ref[l, m, which * K : which * K + K, :] = (
                    project(l, m, which, acts, projs) + got_ref[row : row + K, :]
                )
    mine = where_ref[2]
    other = 1 - mine
    encode_rows([total_ref[l, other, w * K : w * K + K, :] for l in range(2) for w in range(2)], codes_ref, scales_ref)
    for l in range(2):
        kept_ref[l] = total_ref[l, mine]


def half_m_kernel(where_ref, codes_in, kept_ref, codes_ref, out_ref, scales_ref, total_ref):
    mine = where_ref[2]
    other = 1 - mine
    scales = read_scales(codes_in, 8)
    for l in range(2):
        for m in range(2):
            for w in range(2):
                index = (l * 2 + m) * 2 + w
                rows = slice(w * K, w * K + K)
                total_ref[l, m, rows, :] = kept_ref[l, m, rows, :] + decode(codes_in, index * K, scales, index)
    encode_rows([total_ref[l, other, w * K : w * K + K, :] for l in range(2) for w in range(2)], codes_ref, scales_ref)
    for l in range(2):
        out_ref[l] = total_ref[l, mine]


def half_l_kernel(where_ref, codes_in, kept_ref, codes_ref, out_ref, scales_ref, total_ref):
    mine = where_ref[3]
    other = 1 - mine
    scales = read_scales(codes_in, 4)
    for l in range(2):
        for w in range(2):
            index = l * 2 + w
            rows = slice(w * K, w * K + K)
            total_ref[l, rows, :] = kept_ref[l, rows, :] + decode(codes_in, index * K, scales, index)
    encode_rows([total_ref[other, w * K : w * K + K, :] for w in range(2)], codes_ref, scales_ref)
    out_ref[...] = total_ref[mine]


def half_s_kernel(where_ref, codes_in, kept_ref, codes_ref, out_ref, scales_ref):
    step = pl.program_id(0)
    scales = read_scales(codes_in, 2)
    total = [kept_ref[w * K : w * K + K, :] + decode(codes_in, w * K, scales, w) for w in range(2)]

    @pl.when(step == 0)
    def _():
        encode_rows(total, codes_ref, scales_ref)

    @pl.when(step == 1)
    def _():
        for w in range(2):
            out_ref[w * K : w * K + K, :] = total[w]


def outer_kernel(codes_a, kept_a, codes_b, kept_b, out_ref):
    total = None
    for codes, kept in ((codes_a, kept_a), (codes_b, kept_b)):
        scales = read_scales(codes, 2)
        g, x = [kept[w * K : w * K + K, :] + decode(codes, w * K, scales, w) for w in range(2)]
        part = lax.dot_general(g, x, (((1,), (1,)), ((), ())), precision=HIGH, preferred_element_type=F32)
        total = part if total is None else total + part
    out_ref[...] = total


def cube(
    attn_in, attn_grad, ffn_in, ffn_grad, proj_attn_in, proj_attn_out, proj_ffn_in, proj_ffn_out, test_grads
):
    acts = (attn_grad, attn_in, ffn_grad, ffn_in)
    projs = tuple(w.transpose(0, 2, 1) for w in (proj_attn_out, proj_attn_in, proj_ffn_out, proj_ffn_in))
    total_tokens = attn_in.shape[2]
    block = total_tokens // 8
    me = lax.axis_index("tp")
    core, y, z = me % 2, (me // 2) % 2, me // 4
    where = jnp.stack([core, y, z % 2, z // 2]).astype(jnp.int32)

    def swap(value, bit):
        return lax.ppermute(value, "tp", [(i, i ^ bit) for i in range(16)])

    act_bytes = sum(a.shape[0] * a.shape[1] for a in acts) * 2 * block * 2
    flops = sum(a.shape[0] * a.shape[1] for a in acts) * 2 * block * 2 * K

    def run_acts(kernel, chunk, own, order, extra, outs, out_specs, scratch, name):
        def index(step, where_ref):
            c = where_ref[0] if own else 1 - where_ref[0]
            s = jnp.where(step == 0, 1 - where_ref[1], where_ref[1]) if order else step
            return (0, 0, s * 4 + c * 2 + chunk)

        def got_index(step, where_ref):
            s = jnp.where(step == 0, 1 - where_ref[1], where_ref[1]) if order else step
            return (0, s)

        in_specs = [pl.BlockSpec((a.shape[0], a.shape[1], block), index) for a in acts]
        in_specs += [pl.BlockSpec(w.shape, lambda i, r: (0, 0, 0)) for w in projs]
        if extra:
            in_specs.append(pl.BlockSpec((8 * K, block), got_index))
        return pl.pallas_call(
            kernel,
            out_shape=outs,
            grid_spec=pltpu.PrefetchScalarGridSpec(
                num_scalar_prefetch=1, grid=(2,), in_specs=in_specs, out_specs=out_specs, scratch_shapes=scratch
            ),
            cost_estimate=pl.CostEstimate(flops=flops, bytes_accessed=act_bytes, transcendentals=0),
            name=name,
        )(where, *acts, *projs, *extra)

    def sds(shape, dtype=F32):
        return jax.ShapeDtypeStruct(shape, dtype)

    def send(chunk):
        return run_acts(
            send_kernel, chunk, False, False, (), sds((8 * K, 2 * block)),
            pl.BlockSpec((8 * K, block), lambda i, r: (0, i)), [], f"send{chunk}",
        )

    scales_scratch = pltpu.VMEM((16, block), F32)

    def small(kernel, ins, outs, name, grid=None, in_specs=None, out_specs=None, scratch=(scales_scratch,), wide=block):
        vmem = pl.BlockSpec(memory_space=pltpu.VMEM)
        if grid is None:
            in_specs = [pl.BlockSpec(memory_space=pltpu.SMEM)] + [vmem] * len(ins)
            return pl.pallas_call(
                kernel, out_shape=outs, in_specs=in_specs, out_specs=[vmem] * len(outs),
                scratch_shapes=[pltpu.VMEM((16, wide), F32), pltpu.VMEM(ins[1].shape, F32)], name=name,
                cost_estimate=pl.CostEstimate(flops=0, bytes_accessed=4 << 20, transcendentals=0),
            )(where, *ins)
        return pl.pallas_call(
            kernel, out_shape=outs,
            grid_spec=pltpu.PrefetchScalarGridSpec(
                num_scalar_prefetch=1, grid=grid, in_specs=in_specs, out_specs=out_specs, scratch_shapes=list(scratch)
            ),
            cost_estimate=pl.CostEstimate(flops=0, bytes_accessed=2 << 20, transcendentals=0),
            name=name,
        )(where, *ins)

    got_a = swap(send(0), 1)
    got_b = swap(send(1), 1)

    codes_a, kept_a = run_acts(
        keep_y_kernel, 0, True, True, (got_a,),
        (sds((8 * K + 16, block), BF16), sds((2, 2, 2 * K, block))),
        [pl.BlockSpec((8 * K + 16, block), lambda i, r: (0, 0)), pl.BlockSpec((2, 2, 2 * K, block), lambda i, r: (0, 0, 0, 0))],
        [scales_scratch], "keep_a",
    )
    in_a = swap(codes_a, 2)
    codes_b, kept_b = run_acts(
        keep_z_kernel, 1, True, False, (got_b,),
        (sds((4 * K + 16, 2 * block), BF16), sds((2, 2 * K, 2 * block))),
        [pl.BlockSpec((4 * K + 16, block), lambda i, r: (0, i)), pl.BlockSpec((2, 2 * K, block), lambda i, r: (0, 0, i))],
        [pltpu.VMEM((2, 2, 2 * K, block), F32), scales_scratch], "keep_b",
    )
    in_b = swap(codes_b, 4)

    codes_a, kept_a = small(
        half_m_kernel, (in_a, kept_a), (sds((4 * K + 16, block), BF16), sds((2, 2 * K, block))), "half_m_a"
    )
    in_a = swap(codes_a, 4)
    codes_b, kept_b = small(
        half_l_kernel, (in_b, kept_b), (sds((2 * K + 16, 2 * block), BF16), sds((2 * K, 2 * block))), "half_l_b", wide=2 * block
    )
    in_b = swap(codes_b, 8)

    codes_a, kept_a = small(
        half_l_kernel, (in_a, kept_a), (sds((2 * K + 16, block), BF16), sds((2 * K, block))), "half_l_a"
    )
    in_a = swap(codes_a, 8)

    def by_s(step, r):
        return (0, jnp.where(step == 0, 1 - r[1], r[1]))

    codes_b, kept_b = small(
        half_s_kernel, (in_b, kept_b), (sds((2 * K + 16, block), BF16), sds((2 * K, block))), "half_s_b", grid=(2,),
        in_specs=[pl.BlockSpec((2 * K + 16, block), by_s), pl.BlockSpec((2 * K, block), by_s)],
        out_specs=[pl.BlockSpec((2 * K + 16, block), lambda i, r: (0, 0)), pl.BlockSpec((2 * K, block), lambda i, r: (0, 0))],
    )
    in_b = swap(codes_b, 2)

    outer = pl.pallas_call(
        outer_kernel, out_shape=sds((K, K)), name="outer",
        in_specs=[pl.BlockSpec(memory_space=pltpu.VMEM)] * 4, out_specs=pl.BlockSpec(memory_space=pltpu.VMEM),
    )(in_a, kept_a, in_b, kept_b)

    rows = outer.reshape(2, 2, K // 4, K)
    mine = lax.dynamic_index_in_dim(rows, core, 1, keepdims=False)
    other = lax.dynamic_index_in_dim(rows, 1 - core, 1, keepdims=False)
    mine = mine + swap(other, 1)
    here = lax.dynamic_index_in_dim(mine, y, 0, keepdims=False)
    there = swap(lax.dynamic_index_in_dim(mine, 1 - y, 0, keepdims=False), 2)
    first = jnp.where(y == 0, here, there)
    second = jnp.where(y == 0, there, here)
    flat = jnp.stack([first, second]).reshape(2, K // 4 * K)
    scores = lax.dot_general(
        flat, test_grads.astype(F32), (((1,), (1,)), ((), ())), precision=HIGH, preferred_element_type=F32
    )
    for bit in (1, 2, 4, 8):
        scores = scores + swap(scores, bit)
    return scores


def shards(
    attn_in, attn_grad, ffn_in, ffn_grad, proj_attn_in, proj_attn_out, proj_ffn_in, proj_ffn_out, test_grads
):
    layers, _, total = attn_in.shape
    devices = lax.axis_size("tp")
    modules = ((attn_grad, proj_attn_out, attn_in, proj_attn_in), (ffn_grad, proj_ffn_out, ffn_in, proj_ffn_in))
    columns = []
    for layer in range(layers):
        for grad, out, source, into in modules:
            for act, weight in ((grad, out), (source, into)):
                columns.append(
                    lax.dot_general(
                        weight[layer], act[layer], (((0,), (0,)), ((), ())), preferred_element_type=F32
                    )
                )
    rows = total // devices
    projected = lax.psum_scatter(jnp.concatenate(columns), "tp", scatter_dimension=1, tiled=True)
    token = lax.axis_index("tp") * rows + jnp.arange(rows, dtype=jnp.int32)
    member = (token // LEN)[None, :] == jnp.arange(SEQS, dtype=jnp.int32)[:, None]
    pairs = projected.reshape(2 * layers, 2, K, rows)
    grads = jnp.where(member[:, None, None, :], pairs[None, :, 0], 0.0)
    outer = jnp.einsum("snat,nbt->snab", grads, pairs[:, 1], precision=HIGH)
    flat = outer.reshape(SEQS, devices, -1).transpose(1, 0, 2)
    flat = flat.reshape(devices, -1)
    owned = lax.psum_scatter(flat, "tp", scatter_dimension=0, tiled=True).reshape(SEQS, -1)
    scores = lax.dot_general(
        owned, test_grads.astype(F32), (((1,), (1,)), ((), ())), precision=HIGH, preferred_element_type=F32
    )
    return lax.psum(scores, "tp")


def solution(mesh):
    placed = (P(None, "tp", "grp"),) * 4 + (P(None, "tp", None),) * 4 + (P(None, "tp"),)
    body = cube if mesh.shape["tp"] == 16 else shards
    return jax.shard_map(body, mesh=mesh, in_specs=placed, out_specs=P("grp", None), check_vma=False)
```

time: 294 us -> 98.4 us (0.33)
  waiting for transfers between devices: 210 us -> 33.9 us
  Pallas kernels: 0 us -> 37.6 us
  blocking collectives: 33.2 us -> 0 us
  matrix products: 30.8 us -> 1.72 us
  starting transfers between devices: 0.04 us -> 18.1 us
  between operations: 13.5 us -> 0.03 us
    reduce_scatter x1 -> x0, waiting for transfers between devices: 106 us -> none  [shards(): lax.psum_scatter(project_all(sliced, projs), 'tp', scatter_dimension=0, t...]
    unnamed x3 -> x0, waiting for transfers between devices: 103 us -> none
    pallas_call x0 -> x9, Pallas kernels: none -> 37.6 us  [the longest x4 24.4 us: run_acts(): pl.pallas_call(kernel, out_shape=outs, grid_spec=pltpu.PrefetchScalarGrid...]
    ppermute x0 -> x14, waiting for transfers between devices: none -> 33.9 us  [swap(): return lax.ppermute(value, 'tp', [(i, i ^ bit) for i in range(16)])]
    psum x1 -> x0, blocking collectives: 33.2 us -> none  [shards(): return lax.psum(partial_scores, 'tp')]
    dot_general x13 -> x1, matrix products: 30.8 us -> 1.72 us  [cube(): lax.dot_general(flat, test_grads.astype(F32), (((1,), (1,)), ((), ())), p...]
    ppermute x0 -> x14, starting transfers between devices: none -> 18.1 us  [swap(): return lax.ppermute(value, 'tp', [(i, i ^ bit) for i in range(16)])]
  transfers between devices with their start and end apart: 2 -> 14, of which waited for: 2 -> 11; matrix products, arithmetic and copies ran while one was open for 0% -> 0% of each run, Pallas kernels for 0% -> 30%
where the time goes in v1:
time: 98.4 us; the launch traced here: 98 us
  Pallas kernels  37.6 us (38%)
  waiting for transfers between devices  33.9 us (34%)
  starting transfers between devices  18.1 us (18%)
  local copies, waits for them, and re-layouts  4.6 us (5%)
  other arithmetic  2.01 us (2%)
  matrix products  1.72 us (2%)
    ppermute x14, waiting for transfers between devices, swap(): return lax.ppermute(value, 'tp', [(i, i ^ bit) for i in range(16)])  33.9 us
    pallas_call x4, Pallas kernels, run_acts(): pl.pallas_call(kernel, out_shape=outs, grid_spec=pltpu.PrefetchScalarGrid...  24.4 us
    ppermute x14, starting transfers between devices, swap(): return lax.ppermute(value, 'tp', [(i, i ^ bit) for i in range(16)])  18.1 us
    pallas_call x3, Pallas kernels, small(): pl.pallas_call(kernel, out_shape=outs, in_specs=in_specs, out_specs=[vmem...  8.03 us
    unnamed x14, local copies, waits for them, and re-layouts  3.72 us
    pallas_call x1, Pallas kernels, small(): pl.pallas_call(kernel, out_shape=outs, grid_spec=pltpu.PrefetchScalarGrid...  2.85 us
    pallas_call x1, Pallas kernels, cube(): pl.pallas_call(outer_kernel, out_shape=sds((K, K)), name='outer', in_spec...  2.28 us
  transfers between devices with their start and end apart: 14, of which 11 were waited for; matrix products, arithmetic and copies ran while one was open for 0% of the time, Pallas kernels for 30%

profile of v1, /device:TPU:0, one launch (start us, length us, event | category | flops | bytes accessed | tf_op | source)
XLA Modules:
  0.0 98.0 jit_solution(223180349370208339)
XLA Ops:
  0.0 0.7 pad_add_fusion.where_ref
  0.7 5.7 %send1.1 = f32[512,1024]{1,0:T(8,128)} custom-call(s32[4]{0:T(128)} %pad_add_fusion.where_ref, bf16[2,256,4096]{2,1,0:T(8,128)(2,1)} %a0.7, bf16[2,256,4096]{2,1,0:T(8,128)(2,1)} %a1.7, bf16[2,256,4096]{2,1,0:T(8,128)(2,1)} %a2.7, bf16[2,896,4096]{2,1,0:T(8,128)(2,1)} %a3.7, bf16[2,64,256]{2,1,0:T(8,128)(2,1)} %bitcast.23, bf16[2,64,256]{2,1,0:T(8,128)(2,1)} %bitcast.27, ...), custom_call_target="tpu_custom_call" | custom-call | flops 436207616 | bytes 6815744 | tf_op jit(solution)/shard_map/send1/pallas_call | solution.py:183
  6.3 0.5 collective-permute-start.4
  6.8 5.6 %send0.1 = f32[512,1024]{1,0:T(8,128)} custom-call(s32[4]{0:T(128)} %pad_add_fusion.where_ref, bf16[2,256,4096]{2,1,0:T(8,128)(2,1)} %a0.7, bf16[2,256,4096]{2,1,0:T(8,128)(2,1)} %a1.7, bf16[2,256,4096]{2,1,0:T(8,128)(2,1)} %a2.7, bf16[2,896,4096]{2,1,0:T(8,128)(2,1)} %a3.7, bf16[2,64,256]{2,1,0:T(8,128)(2,1)} %bitcast.24, bf16[2,64,256]{2,1,0:T(8,128)(2,1)} %bitcast.28, ...), custom_call_target="tpu_custom_call" | custom-call | flops 436207616 | bytes 6815744 | tf_op jit(solution)/shard_map/send0/pallas_call | solution.py:183
  12.4 0.0 collective-permute-start
  12.5 0.0 collective-permute-done.4.got_ref
  12.5 6.6 %keep_b.1 = (bf16[272,1024]{1,0:T(8,128)(2,1)}, f32[2,128,1024]{2,1,0:T(8,128)}) custom-call(s32[4]{0:T(128)} %pad_add_fusion.where_ref, bf16[2,256,4096]{2,1,0:T(8,128)(2,1)} %a0.7, bf16[2,256,4096]{2,1,0:T(8,128)(2,1)} %a1.7, bf16[2,256,4096]{2,1,0:T(8,128)(2,1)} %a2.7, bf16[2,896,4096]{2,1,0:T(8,128)(2,1)} %a3.7, bf16[2,64,256]{2,1,0:T(8,128)(2,1)} %bitcast.25, ...), custom_call_target="tpu_custom_call" | custom-call | flops 436207616 | bytes 6815744 | tf_op jit(solution)/shard_map/keep_b/pallas_call | solution.py:183
  19.0 3.0 %collective-permute-start.5 = (bf16[272,1024]{1,0:T(8,128)(2,1)}, bf16[272,1024]{1,0:T(8,128)(2,1)S(1)}, u32[]{:S(2)}, u32[]{:S(2)}) collective-permute-start(bf16[272,1024]{1,0:T(8,128)(2,1)} %get-tuple-element.23), channel_id=1, source_target_pairs={{0,4},{1,5},{2,6},{3,7},{4,0},{5,1},{6,2},{7,3},{8,12},{9,13},{10,... | collective-permute-start | bytes 1671176 | tf_op jit(solution)/shard_map/ppermute | solution.py:164
  22.1 0.0 collective-permute-done.got_ref
  22.1 6.6 %keep_a.1 = (bf16[528,512]{1,0:T(8,128)(2,1)}, f32[2,2,128,512]{3,2,1,0:T(8,128)}) custom-call(s32[4]{0:T(128)} %pad_add_fusion.where_ref, bf16[2,256,4096]{2,1,0:T(8,128)(2,1)} %a0.7, bf16[2,256,4096]{2,1,0:T(8,128)(2,1)} %a1.7, bf16[2,256,4096]{2,1,0:T(8,128)(2,1)} %a2.7, bf16[2,896,4096]{2,1,0:T(8,128)(2,1)} %a3.7, bf16[2,64,256]{2,1,0:T(8,128)(2,1)} %bitcast.26, ...), custom_call_target="tpu_custom_call" | custom-call | flops 436207616 | bytes 6815744 | tf_op jit(solution)/shard_map/keep_a/pallas_call | solution.py:183
  28.6 1.5 %collective-permute-start.1 = (bf16[528,512]{1,0:T(8,128)(2,1)}, bf16[528,512]{1,0:T(8,128)(2,1)S(1)}, u32[]{:S(2)}, u32[]{:S(2)}) collective-permute-start(bf16[528,512]{1,0:T(8,128)(2,1)} %get-tuple-element.17), channel_id=1, source_target_pairs={{0,2},{1,3},{2,0},{3,1},{4,6},{5,7},{6,4},{7,5},{8,10},{9,11},{10,... | collective-permute-start | bytes 1622024 | tf_op jit(solution)/shard_map/ppermute | solution.py:164
  30.2 4.9 %collective-permute-done.5.codes_in = bf16[272,1024]{1,0:T(8,128)(2,1)S(1)} collective-permute-done((bf16[272,1024]{1,0:T(8,128)(2,1)}, bf16[272,1024]{1,0:T(8,128)(2,1)S(1)}, u32[]{:S(2)}, u32[]{:S(2)}) %collective-permute-start.5) | collective-permute-done | bytes 557088 | tf_op jit(solution)/shard_map/ppermute | solution.py:164
  35.1 0.8 copy-done.1
  35.9 3.0 %half_l_b.1 = (bf16[144,1024]{1,0:T(8,128)(2,1)}, f32[128,1024]{1,0:T(8,128)}) custom-call(s32[4]{0:T(128)} %pad_add_fusion.where_ref, bf16[272,1024]{1,0:T(8,128)(2,1)} %copy-done.1, f32[2,128,1024]{2,1,0:T(8,128)} %get-tuple-element.24.kept_ref), custom_call_target="tpu_custom_call" | custom-call | bytes 4194304 | tf_op jit(solution)/shard_map/half_l_b/pallas_call | solution.py:208
  38.9 2.8 %collective-permute-start.6 = (bf16[144,1024]{1,0:T(8,128)(2,1)}, bf16[144,1024]{1,0:T(8,128)(2,1)S(1)}, u32[]{:S(2)}, u32[]{:S(2)}) collective-permute-start(bf16[144,1024]{1,0:T(8,128)(2,1)} %get-tuple-element.25), channel_id=1, source_target_pairs={{0,8},{1,9},{2,10},{3,11},{4,12},{5,13},{6,14},{7,15},{8,0},{9,1},... | collective-permute-start | bytes 884744 | tf_op jit(solution)/shard_map/ppermute | solution.py:164
  41.7 1.1 %collective-permute-done.1.codes_in = bf16[528,512]{1,0:T(8,128)(2,1)S(1)} collective-permute-done((bf16[528,512]{1,0:T(8,128)(2,1)}, bf16[528,512]{1,0:T(8,128)(2,1)S(1)}, u32[]{:S(2)}, u32[]{:S(2)}) %collective-permute-start.1) | collective-permute-done | bytes 540704 | tf_op jit(solution)/shard_map/ppermute | solution.py:164
  42.8 0.8 copy-done.2
  43.6 2.9 %half_m_a.1 = (bf16[272,512]{1,0:T(8,128)(2,1)}, f32[2,128,512]{2,1,0:T(8,128)}) custom-call(s32[4]{0:T(128)} %pad_add_fusion.where_ref, bf16[528,512]{1,0:T(8,128)(2,1)} %copy-done.2, f32[2,2,128,512]{3,2,1,0:T(8,128)} %get-tuple-element.18.kept_ref), custom_call_target="tpu_custom_call" | custom-call | bytes 4194304 | tf_op jit(solution)/shard_map/half_m_a/pallas_call | solution.py:208
  46.5 0.5 collective-permute-start.2
  47.0 12.5 %collective-permute-done.2.codes_in = bf16[272,512]{1,0:T(8,128)(2,1)S(1)} collective-permute-done((bf16[272,512]{1,0:T(8,128)(2,1)}, bf16[272,512]{1,0:T(8,128)(2,1)S(1)}, u32[]{:S(2)}, u32[]{:S(2)}) %collective-permute-start.2) | collective-permute-done | bytes 278560 | tf_op jit(solution)/shard_map/ppermute | solution.py:164
  59.5 0.7 copy-done.4
  60.2 2.1 %half_l_a.1 = (bf16[144,512]{1,0:T(8,128)(2,1)}, f32[128,512]{1,0:T(8,128)}) custom-call(s32[4]{0:T(128)} %pad_add_fusion.where_ref, bf16[272,512]{1,0:T(8,128)(2,1)} %copy-done.4, f32[2,128,512]{2,1,0:T(8,128)} %get-tuple-element.20.kept_ref), custom_call_target="tpu_custom_call" | custom-call | bytes 4194304 | tf_op jit(solution)/shard_map/half_l_a/pallas_call | solution.py:208
  62.3 1.6 %collective-permute-start.3 = (bf16[144,512]{1,0:T(8,128)(2,1)}, bf16[144,512]{1,0:T(8,128)(2,1)S(1)}, u32[]{:S(2)}, u32[]{:S(2)}) collective-permute-start(bf16[144,512]{1,0:T(8,128)(2,1)} %get-tuple-element.21), channel_id=1, source_target_pairs={{0,8},{1,9},{2,10},{3,11},{4,12},{5,13},{6,14},{7,15},{8,0},{9,1},... | collective-permute-start | bytes 442376 | tf_op jit(solution)/shard_map/ppermute | solution.py:164
  63.9 0.0 collective-permute-done.6.codes_in
  63.9 0.7 copy-done.3
  64.6 2.8 %half_s_b.1 = (bf16[144,512]{1,0:T(8,128)(2,1)}, f32[128,512]{1,0:T(8,128)}) custom-call(s32[4]{0:T(128)} %pad_add_fusion.where_ref, bf16[144,1024]{1,0:T(8,128)(2,1)} %copy-done.3, f32[128,1024]{1,0:T(8,128)} %get-tuple-element.26.kept_ref), custom_call_target="tpu_custom_call" | custom-call | bytes 2097152 | tf_op jit(solution)/shard_map/half_s_b/pallas_call | solution.py:213
  67.5 1.6 %collective-permute-start.7 = (bf16[144,512]{1,0:T(8,128)(2,1)}, bf16[144,512]{1,0:T(8,128)(2,1)S(1)}, u32[]{:S(2)}, u32[]{:S(2)}) collective-permute-start(bf16[144,512]{1,0:T(8,128)(2,1)} %get-tuple-element.27), channel_id=1, source_target_pairs={{0,2},{1,3},{2,0},{3,1},{4,6},{5,7},{6,4},{7,5},{8,10},{9,11},{10,... | collective-permute-start | bytes 442376 | tf_op jit(solution)/shard_map/ppermute | solution.py:164
  69.1 2.1 %collective-permute-done.3.codes_a = bf16[144,512]{1,0:T(8,128)(2,1)S(1)} collective-permute-done((bf16[144,512]{1,0:T(8,128)(2,1)}, bf16[144,512]{1,0:T(8,128)(2,1)S(1)}, u32[]{:S(2)}, u32[]{:S(2)}) %collective-permute-start.3) | collective-permute-done | bytes 147488 | tf_op jit(solution)/shard_map/ppermute | solution.py:164
  71.2 1.6 %collective-permute-done.7.codes_b = bf16[144,512]{1,0:T(8,128)(2,1)S(1)} collective-permute-done((bf16[144,512]{1,0:T(8,128)(2,1)}, bf16[144,512]{1,0:T(8,128)(2,1)S(1)}, u32[]{:S(2)}, u32[]{:S(2)}) %collective-permute-start.7) | collective-permute-done | bytes 147488 | tf_op jit(solution)/shard_map/ppermute | solution.py:164
  72.8 0.6 copy-done.6
  73.5 2.3 %outer.1 = f32[64,64]{1,0:T(8,128)} custom-call(bf16[144,512]{1,0:T(8,128)(2,1)} %copy-done.5, f32[128,512]{1,0:T(8,128)} %get-tuple-element.22.kept_a, bf16[144,512]{1,0:T(8,128)(2,1)} %copy-done.6, f32[128,512]{1,0:T(8,128)} %get-tuple-element.28.kept_b), custom_call_target="tpu_custom_call" | custom-call | tf_op jit(solution)/shard_map/outer/pallas_call | solution.py:264
  75.8 0.7 dynamic-slice_bitcast_fusion
  76.5 0.0 collective-permute-start.8
  76.5 1.2 %collective-permute-done.8 = f32[2,16,64]{2,1,0:T(8,128)S(1)} collective-permute-done((f32[2,16,64]{2,1,0:T(8,128)S(1)}, f32[2,16,64]{2,1,0:T(8,128)S(1)}, u32[]{:S(2)}, u32[]{:S(2)}) %collective-permute-start.8) | collective-permute-done | bytes 8224 | tf_op jit(solution)/shard_map/ppermute | solution.py:164
  77.7 0.7 bitcast_add_fusion
  78.4 1.6 %collective-permute-start.9 = (f32[16,64]{1,0:T(8,128)S(1)}, f32[16,64]{1,0:T(8,128)S(1)}, u32[]{:S(2)}, u32[]{:S(2)}) collective-permute-start(f32[16,64]{1,0:T(8,128)S(1)} %dynamic-slice_bitcast_fusion.1), channel_id=1, source_target_pairs={{0,2},{1,3},{2,0},{3,1},{4,6},{5,7},{6,4},{7,5},{8,10},{9,11},{10,... | collective-permute-start | bytes 12296 | tf_op jit(solution)/shard_map/ppermute | solution.py:164
  80.0 2.0 %collective-permute-done.9 = f32[16,64]{1,0:T(8,128)S(1)} collective-permute-done((f32[16,64]{1,0:T(8,128)S(1)}, f32[16,64]{1,0:T(8,128)S(1)}, u32[]{:S(2)}, u32[]{:S(2)}) %collective-permute-start.9) | collective-permute-done | bytes 4128 | tf_op jit(solution)/shard_map/ppermute | solution.py:164
  82.1 0.1 stack.29
  82.1 0.1 stack.30
  82.2 1.7 %fusion = f32[2,1024]{1,0:T(2,128)S(1)} fusion(bf16[1024,1024]{1,0:T(8,128)(2,1)S(1)} %copy-done, f32[1,1024]{1,0:T(1,128)S(1)} %stack.30, f32[1,1024]{1,0:T(1,128)S(1)} %stack.29), kind=kOutput, calls=%fused_computation.2 | convolution fusion | flops 25167872 | bytes 2113536 | tf_op jit(solution)/shard_map/dot_general | solution.py:278
  83.9 1.2 %collective-permute-done.10 = f32[2,1024]{1,0:T(2,128)S(1)} collective-permute-done((f32[2,1024]{1,0:T(2,128)S(1)}, f32[2,1024]{1,0:T(2,128)S(1)}, u32[]{:S(2)}, u32[]{:S(2)}) %collective-permute-start.10) | collective-permute-done | bytes 8224 | tf_op jit(solution)/shard_map/ppermute | solution.py:164
  85.1 1.6 %collective-permute-start.11 = (f32[2,1024]{1,0:T(2,128)S(1)}, f32[2,1024]{1,0:T(2,128)S(1)}, u32[]{:S(2)}, u32[]{:S(2)}) collective-permute-start(f32[2,1024]{1,0:T(2,128)S(1)} %add.52), channel_id=1, source_target_pairs={{0,2},{1,3},{2,0},{3,1},{4,6},{5,7},{6,4},{7,5},{8,10},{9,11},{10,... | collective-permute-start | bytes 24584 | tf_op jit(solution)/shard_map/ppermute | solution.py:164
  86.8 2.0 %collective-permute-done.11 = f32[2,1024]{1,0:T(2,128)S(1)} collective-permute-done((f32[2,1024]{1,0:T(2,128)S(1)}, f32[2,1024]{1,0:T(2,128)S(1)}, u32[]{:S(2)}, u32[]{:S(2)}) %collective-permute-start.11) | collective-permute-done | bytes 8224 | tf_op jit(solution)/shard_map/ppermute | solution.py:164
  88.8 2.4 %collective-permute-start.12 = (f32[2,1024]{1,0:T(2,128)S(1)}, f32[2,1024]{1,0:T(2,128)S(1)}, u32[]{:S(2)}, u32[]{:S(2)}) collective-permute-start(f32[2,1024]{1,0:T(2,128)S(1)} %add.53), channel_id=1, source_target_pairs={{0,4},{1,5},{2,6},{3,7},{4,0},{5,1},{6,2},{7,3},{8,12},{9,13},{10,... | collective-permute-start | bytes 24584 | tf_op jit(solution)/shard_map/ppermute | solution.py:164
  91.2 1.6 %collective-permute-done.12 = f32[2,1024]{1,0:T(2,128)S(1)} collective-permute-done((f32[2,1024]{1,0:T(2,128)S(1)}, f32[2,1024]{1,0:T(2,128)S(1)}, u32[]{:S(2)}, u32[]{:S(2)}) %collective-permute-start.12) | collective-permute-done | bytes 8224 | tf_op jit(solution)/shard_map/ppermute | solution.py:164
  92.8 1.0 %collective-permute-start.13 = (f32[2,1024]{1,0:T(2,128)S(1)}, f32[2,1024]{1,0:T(2,128)S(1)}, u32[]{:S(2)}, u32[]{:S(2)}) collective-permute-start(f32[2,1024]{1,0:T(2,128)S(1)} %add.54), channel_id=1, source_target_pairs={{0,8},{1,9},{2,10},{3,11},{4,12},{5,13},{6,14},{7,15},{8,0},{9,1},... | collective-permute-start | bytes 24584 | tf_op jit(solution)/shard_map/ppermute | solution.py:164
  93.8 3.5 %collective-permute-done.13 = f32[2,1024]{1,0:T(2,128)S(1)} collective-permute-done((f32[2,1024]{1,0:T(2,128)S(1)}, f32[2,1024]{1,0:T(2,128)S(1)}, u32[]{:S(2)}, u32[]{:S(2)}) %collective-permute-start.13) | collective-permute-done | bytes 8224 | tf_op jit(solution)/shard_map/ppermute | solution.py:164
  97.4 0.6 add.55
  (15 shorter events, 0.0 us)
Async XLA Ops:
  0.0 82.2 %copy-start = (bf16[1024,1024]{1,0:T(8,128)(2,1)S(1)}, bf16[1024,1024]{1,0:T(8,128)(2,1)}, u32[]{:S(2)}) copy-start(bf16[1024,1024]{1,0:T(8,128)(2,1)} %param.17) | copy-start | bytes 6291460
  6.3 6.1 %collective-permute-start.4 = (f32[512,1024]{1,0:T(8,128)}, f32[512,1024]{1,0:T(8,128)}, u32[]{:S(2)}, u32[]{:S(2)}) collective-permute-start(f32[512,1024]{1,0:T(8,128)} %send1.1), channel_id=1, source_target_pairs={{0,1},{1,0},{2,3},{3,2},{4,5},{5,4},{6,7},{7,6},{8,9},{9,8},{10,11... | collective-permute-start | bytes 6291464 | tf_op jit(solution)/shard_map/ppermute | solution.py:164
  12.4 9.6 %collective-permute-start = (f32[512,1024]{1,0:T(8,128)}, f32[512,1024]{1,0:T(8,128)}, u32[]{:S(2)}, u32[]{:S(2)}) collective-permute-start(f32[512,1024]{1,0:T(8,128)} %send0.1), channel_id=1, source_target_pairs={{0,1},{1,0},{2,3},{3,2},{4,5},{5,4},{6,7},{7,6},{8,9},{9,8},{10,11... | collective-permute-start | bytes 6291464 | tf_op jit(solution)/shard_map/ppermute | solution.py:164
  19.0 16.1 %collective-permute-start.5 = (bf16[272,1024]{1,0:T(8,128)(2,1)}, bf16[272,1024]{1,0:T(8,128)(2,1)S(1)}, u32[]{:S(2)}, u32[]{:S(2)}) collective-permute-start(bf16[272,1024]{1,0:T(8,128)(2,1)} %get-tuple-element.23), channel_id=1, source_target_pairs={{0,4},{1,5},{2,6},{3,7},{4,0},{5,1},{6,2},{7,3},{8,12},{9,13},{10,... | collective-permute-start | bytes 1671176 | tf_op jit(solution)/shard_map/ppermute | solution.py:164
  28.6 14.1 %collective-permute-start.1 = (bf16[528,512]{1,0:T(8,128)(2,1)}, bf16[528,512]{1,0:T(8,128)(2,1)S(1)}, u32[]{:S(2)}, u32[]{:S(2)}) collective-permute-start(bf16[528,512]{1,0:T(8,128)(2,1)} %get-tuple-element.17), channel_id=1, source_target_pairs={{0,2},{1,3},{2,0},{3,1},{4,6},{5,7},{6,4},{7,5},{8,10},{9,11},{10,... | collective-permute-start | bytes 1622024 | tf_op jit(solution)/shard_map/ppermute | solution.py:164
  35.1 0.8 copy-start.1
  38.9 25.0 %collective-permute-start.6 = (bf16[144,1024]{1,0:T(8,128)(2,1)}, bf16[144,1024]{1,0:T(8,128)(2,1)S(1)}, u32[]{:S(2)}, u32[]{:S(2)}) collective-permute-start(bf16[144,1024]{1,0:T(8,128)(2,1)} %get-tuple-element.25), channel_id=1, source_target_pairs={{0,8},{1,9},{2,10},{3,11},{4,12},{5,13},{6,14},{7,15},{8,0},{9,1},... | collective-permute-start | bytes 884744 | tf_op jit(solution)/shard_map/ppermute | solution.py:164
  42.8 0.8 copy-start.2
  46.5 13.0 %collective-permute-start.2 = (bf16[272,512]{1,0:T(8,128)(2,1)}, bf16[272,512]{1,0:T(8,128)(2,1)S(1)}, u32[]{:S(2)}, u32[]{:S(2)}) collective-permute-start(bf16[272,512]{1,0:T(8,128)(2,1)} %get-tuple-element.19), channel_id=1, source_target_pairs={{0,4},{1,5},{2,6},{3,7},{4,0},{5,1},{6,2},{7,3},{8,12},{9,13},{10,... | collective-permute-start | bytes 835592 | tf_op jit(solution)/shard_map/ppermute | solution.py:164
  59.5 0.7 copy-start.4
  62.3 8.8 %collective-permute-start.3 = (bf16[144,512]{1,0:T(8,128)(2,1)}, bf16[144,512]{1,0:T(8,128)(2,1)S(1)}, u32[]{:S(2)}, u32[]{:S(2)}) collective-permute-start(bf16[144,512]{1,0:T(8,128)(2,1)} %get-tuple-element.21), channel_id=1, source_target_pairs={{0,8},{1,9},{2,10},{3,11},{4,12},{5,13},{6,14},{7,15},{8,0},{9,1},... | collective-permute-start | bytes 442376 | tf_op jit(solution)/shard_map/ppermute | solution.py:164
  63.9 0.7 copy-start.3
  67.5 5.4 %collective-permute-start.7 = (bf16[144,512]{1,0:T(8,128)(2,1)}, bf16[144,512]{1,0:T(8,128)(2,1)S(1)}, u32[]{:S(2)}, u32[]{:S(2)}) collective-permute-start(bf16[144,512]{1,0:T(8,128)(2,1)} %get-tuple-element.27), channel_id=1, source_target_pairs={{0,2},{1,3},{2,0},{3,1},{4,6},{5,7},{6,4},{7,5},{8,10},{9,11},{10,... | collective-permute-start | bytes 442376 | tf_op jit(solution)/shard_map/ppermute | solution.py:164
  71.2 1.7 %copy-start.5 = (bf16[144,512]{1,0:T(8,128)(2,1)}, bf16[144,512]{1,0:T(8,128)(2,1)S(1)}, u32[]{:S(2)}) copy-start(bf16[144,512]{1,0:T(8,128)(2,1)S(1)} %collective-permute-done.3.codes_a) | copy-start | bytes 442372
  72.8 0.7 copy-start.6
  76.5 1.2 %collective-permute-start.8 = (f32[2,16,64]{2,1,0:T(8,128)S(1)}, f32[2,16,64]{2,1,0:T(8,128)S(1)}, u32[]{:S(2)}, u32[]{:S(2)}) collective-permute-start(f32[2,16,64]{2,1,0:T(8,128)S(1)} %dynamic-slice_bitcast_fusion), channel_id=1, source_target_pairs={{0,1},{1,0},{2,3},{3,2},{4,5},{5,4},{6,7},{7,6},{8,9},{9,8},{10,11... | collective-permute-start | bytes 24584 | tf_op jit(solution)/shard_map/ppermute | solution.py:164
  78.4 3.7 %collective-permute-start.9 = (f32[16,64]{1,0:T(8,128)S(1)}, f32[16,64]{1,0:T(8,128)S(1)}, u32[]{:S(2)}, u32[]{:S(2)}) collective-permute-start(f32[16,64]{1,0:T(8,128)S(1)} %dynamic-slice_bitcast_fusion.1), channel_id=1, source_target_pairs={{0,2},{1,3},{2,0},{3,1},{4,6},{5,7},{6,4},{7,5},{8,10},{9,11},{10,... | collective-permute-start | bytes 12296 | tf_op jit(solution)/shard_map/ppermute | solution.py:164
  83.9 1.2 %collective-permute-start.10 = (f32[2,1024]{1,0:T(2,128)S(1)}, f32[2,1024]{1,0:T(2,128)S(1)}, u32[]{:S(2)}, u32[]{:S(2)}) collective-permute-start(f32[2,1024]{1,0:T(2,128)S(1)} %fusion), channel_id=1, source_target_pairs={{0,1},{1,0},{2,3},{3,2},{4,5},{5,4},{6,7},{7,6},{8,9},{9,8},{10,11... | collective-permute-start | bytes 24584 | tf_op jit(solution)/shard_map/ppermute | solution.py:164
  85.1 3.7 %collective-permute-start.11 = (f32[2,1024]{1,0:T(2,128)S(1)}, f32[2,1024]{1,0:T(2,128)S(1)}, u32[]{:S(2)}, u32[]{:S(2)}) collective-permute-start(f32[2,1024]{1,0:T(2,128)S(1)} %add.52), channel_id=1, source_target_pairs={{0,2},{1,3},{2,0},{3,1},{4,6},{5,7},{6,4},{7,5},{8,10},{9,11},{10,... | collective-permute-start | bytes 24584 | tf_op jit(solution)/shard_map/ppermute | solution.py:164
  88.8 4.0 %collective-permute-start.12 = (f32[2,1024]{1,0:T(2,128)S(1)}, f32[2,1024]{1,0:T(2,128)S(1)}, u32[]{:S(2)}, u32[]{:S(2)}) collective-permute-start(f32[2,1024]{1,0:T(2,128)S(1)} %add.53), channel_id=1, source_target_pairs={{0,4},{1,5},{2,6},{3,7},{4,0},{5,1},{6,2},{7,3},{8,12},{9,13},{10,... | collective-permute-start | bytes 24584 | tf_op jit(solution)/shard_map/ppermute | solution.py:164
  92.8 4.5 %collective-permute-start.13 = (f32[2,1024]{1,0:T(2,128)S(1)}, f32[2,1024]{1,0:T(2,128)S(1)}, u32[]{:S(2)}, u32[]{:S(2)}) collective-permute-start(f32[2,1024]{1,0:T(2,128)S(1)} %add.54), channel_id=1, source_target_pairs={{0,8},{1,9},{2,10},{3,11},{4,12},{5,13},{6,14},{7,15},{8,0},{9,1},... | collective-permute-start | bytes 24584 | tf_op jit(solution)/shard_map/ppermute | solution.py:164

commit v2 on v0

v2 whole, which is shorter than its diff:
```python
import functools

import jax
import jax.numpy as jnp
from jax import lax
from jax.experimental import pallas as pl
from jax.experimental.pallas import tpu as pltpu
from jax.sharding import PartitionSpec as P

LEN = 2048
SEQS = 2
K = 64
F32 = jnp.float32
BF16 = jnp.bfloat16
SPAN = 250.0
HIGH = lax.Precision.HIGHEST


def encode(values, codes_ref, row, scales_ref, index):
    top = jnp.max(jnp.abs(values), axis=0, keepdims=True)
    scale = (top * 1.015625).astype(BF16).astype(F32)
    scales_ref[index : index + 1, :] = scale
    factor = jnp.where(scale > 2e-36, SPAN / jnp.maximum(scale, 2e-36), 0.0)
    power = jnp.exp2(jnp.abs(values) * factor - 0.5 * SPAN)
    codes_ref[row : row + K, :] = jnp.where(values < 0, -power, power).astype(BF16)


def decode(codes_ref, row, scales, index):
    codes = codes_ref[row : row + K, :].astype(F32)
    scale = scales[index : index + 1, :] * (1.0 / SPAN)
    size = (jnp.log2(jnp.abs(codes)) + 0.5 * SPAN) * scale
    return jnp.where(codes < 0, -size, size)


def encode_groups(groups, codes_ref, scales_ref):
    scales_ref[...] = jnp.zeros_like(scales_ref)
    for index, values in enumerate(groups):
        encode(values, codes_ref, index * K, scales_ref, index)
    codes_ref[len(groups) * K :, :] = scales_ref[...].astype(BF16)


def split(dim, total_ref, codes_ref, kept_ref, scales_ref, where_ref):
    layers, modules, _, tokens = total_ref.shape
    mine = where_ref[" sml".index(dim)]
    other = 1 - mine
    if dim == "s":
        width = tokens // 2
        leave = pl.ds(pl.multiple_of(other * width, 128), width)
        stay = pl.ds(pl.multiple_of(mine * width, 128), width)
        groups = [(l, m, w, leave) for l in range(layers) for m in range(modules) for w in range(2)]
    elif dim == "m":
        groups = [(l, other, w, slice(None)) for l in range(layers) for w in range(2)]
    else:
        groups = [(other, m, w, slice(None)) for m in range(modules) for w in range(2)]
    encode_groups(
        [total_ref[l, m, w * K : w * K + K, lanes] for l, m, w, lanes in groups], codes_ref, scales_ref
    )
    if dim == "s":
        kept_ref[...] = total_ref[:, :, :, stay]
    elif dim == "m":
        for l in range(layers):
            kept_ref[l, 0] = total_ref[l, mine]
    else:
        kept_ref[0] = total_ref[mine]


def add_codes(codes_ref, kept_ref, total_ref):
    layers, modules, _, _ = kept_ref.shape
    rows = layers * modules * 2 * K
    scales = codes_ref[rows:, :].astype(F32)
    for l in range(layers):
        for m in range(modules):
            for w in range(2):
                index = (l * modules + m) * 2 + w
                part = slice(w * K, w * K + K)
                total_ref[l, m, part, :] = kept_ref[l, m, part, :] + decode(codes_ref, index * K, scales, index)


def split_kernel(dim, where_ref, codes_in, kept_in, codes_ref, kept_ref, scales_ref, total_ref):
    add_codes(codes_in, kept_in, total_ref)
    split(dim, total_ref, codes_ref, kept_ref, scales_ref, where_ref)


def outer_kernel(chunks, where_ref, *refs):
    ins, (leave_ref, stay_ref), totals = refs[: 2 * chunks], refs[2 * chunks : 2 * chunks + 2], refs[2 * chunks + 2 :]
    out_ref, totals = totals[0], totals[1:]
    total = None
    for chunk in range(chunks):
        sums = totals[chunk]
        add_codes(ins[2 * chunk], ins[2 * chunk + 1], sums)
        part = lax.dot_general(
            sums[0, 0, :K, :], sums[0, 0, K:, :], (((1,), (1,)), ((), ())), precision=HIGH, preferred_element_type=F32
        )
        total = part if total is None else total + part
    out_ref[...] = total
    core = where_ref[0]
    quarter = K // 4
    for y in range(2):
        leave_ref[y] = out_ref[pl.ds(pl.multiple_of((2 * y + 1 - core) * quarter, 8), quarter), :]
        stay_ref[y] = out_ref[pl.ds(pl.multiple_of((2 * y + core) * quarter, 8), quarter), :]


def scores_kernel(flat_ref, tests_ref, out_ref):
    rest = flat_ref[...]
    parts = []
    for _ in range(3):
        part = rest.astype(BF16)
        parts.append(part)
        rest = rest - part.astype(F32)
    total = None
    for part in reversed(parts):
        term = lax.dot_general(part, tests_ref[...], (((1,), (1,)), ((), ())), preferred_element_type=F32)
        total = term if total is None else total + term
    out_ref[...] = total


def project_kernel(own, where_ref, *refs):
    chunks = len(refs) - 17
    acts, projs, outs = refs[:4], refs[4:8], refs[8 : 8 + chunks]
    act_bufs, proj_bufs, sems = refs[8 + chunks : 12 + chunks], refs[12 + chunks : 16 + chunks], refs[16 + chunks]
    core = where_ref[0] if own else 1 - where_ref[0]
    layers, _, total = acts[0].shape
    quarter = total // 4
    pieces = [(s, l, i) for s in range(2) for l in range(layers) for i in range(4)]
    loads = [pltpu.make_async_copy(projs[i], proj_bufs[i], sems.at[len(pieces) + i]) for i in range(4)]
    copies = []
    for index, (s, l, i) in enumerate(pieces):
        lanes = pl.ds(pl.multiple_of(s * (total // 2) + core * quarter, 128), quarter)
        copies.append(pltpu.make_async_copy(acts[i].at[l, :, lanes], act_bufs[i].at[s, l], sems.at[index]))
    for copy in loads + copies:
        copy.start()
    for copy in loads:
        copy.wait()
    for index, (s, l, i) in enumerate(pieces):
        copies[index].wait()
        at = 0
        for out_ref in outs:
            width = out_ref.shape[-1] // 2
            out_ref[l, i // 2, i % 2 * K : i % 2 * K + K, s * width : (s + 1) * width] = jnp.dot(
                proj_bufs[i][l], act_bufs[i][s, l, :, at : at + width], preferred_element_type=F32
            )
            at += width


def join_kernel(dim, where_ref, own_ref, got_ref, codes_ref, kept_ref, scales_ref, total_ref):
    total_ref[...] = own_ref[...] + got_ref[...]
    split(dim, total_ref, codes_ref, kept_ref, scales_ref, where_ref)


CHUNKS = ((512, 'sml'), (512, 'msl'))
BITS = {"s": 2, "m": 4, "l": 8}


def cube(
    attn_in, attn_grad, ffn_in, ffn_grad, proj_attn_in, proj_attn_out, proj_ffn_in, proj_ffn_out, test_grads
):
    acts = (attn_grad, attn_in, ffn_grad, ffn_in)
    projs = tuple(w.transpose(0, 2, 1) for w in (proj_attn_out, proj_attn_in, proj_ffn_out, proj_ffn_in))
    acts = tuple(pltpu.with_memory_space_constraint(a, pltpu.HBM) for a in acts)
    projs = tuple(pltpu.with_memory_space_constraint(a, pltpu.HBM) for a in projs)
    quarter = attn_in.shape[2] // 4
    me = lax.axis_index("tp")
    core, y, z = me % 2, (me // 2) % 2, me // 4
    where = jnp.stack([core, y, z % 2, z // 2]).astype(jnp.int32)
    smem = pl.BlockSpec(memory_space=pltpu.SMEM)
    vmem = pl.BlockSpec(memory_space=pltpu.VMEM)
    hbm = pl.BlockSpec(memory_space=pltpu.HBM)

    def swap(value, bit):
        return lax.ppermute(value, "tp", [(i, i ^ bit) for i in range(16)])

    def sds(shape, dtype=F32):
        return jax.ShapeDtypeStruct(shape, dtype)

    def call(kernel, ins, in_specs, outs, scratch, name, cost, limit):
        nonlocal where

        def chained(where_ref, *refs):
            passed = refs[len(ins)]
            for i in range(4):
                passed[i] = where_ref[i]
            kernel(where_ref, *refs[: len(ins)], *refs[len(ins) + 1 :])

        where, *results = pl.pallas_call(
            chained, out_shape=(sds((4,), jnp.int32), *outs), in_specs=[smem] + in_specs,
            out_specs=[smem] + [vmem] * len(outs), scratch_shapes=scratch,
            name=name, cost_estimate=pl.CostEstimate(flops=0, bytes_accessed=cost, transcendentals=0),
            compiler_params=pltpu.CompilerParams(vmem_limit_bytes=limit << 20),
        )(where, *ins)
        return results

    def outputs(dim, shape):
        layers, modules, _, tokens = shape
        kept = {
            "s": (layers, modules, 2 * K, tokens // 2), "m": (layers, 1, 2 * K, tokens), "l": (1, modules, 2 * K, tokens)
        }[dim]
        groups = kept[0] * kept[1] * 2
        scales = max(8, groups)
        return (sds((groups * K + scales, kept[3]), BF16), sds(kept)), pltpu.VMEM((scales, kept[3]), F32)

    def project(name, own):
        scratch = [pltpu.VMEM((2, a.shape[0], a.shape[1], quarter), BF16) for a in acts]
        scratch += [pltpu.VMEM(w.shape, BF16) for w in projs] + [pltpu.SemaphoreType.DMA((8 * acts[0].shape[0] + 4,))]
        outs = tuple(sds((2, 2, 2 * K, 2 * width)) for width, _ in CHUNKS)
        return call(
            functools.partial(project_kernel, own), (*acts, *projs), [hbm] * 8, outs, scratch, name, 16 << 20, 24
        )

    def join(index, own, got, dim):
        outs, scales = outputs(dim, own.shape)
        return call(
            functools.partial(join_kernel, dim), (own, got), [vmem] * 2, outs, [scales, pltpu.VMEM(own.shape, F32)],
            f"join{index}{dim}", 4 << 20, 12,
        )

    def exchange(index, codes, kept, dim):
        outs, scales = outputs(dim, kept.shape)
        return call(
            functools.partial(split_kernel, dim), (codes, kept), [vmem] * 2, outs,
            [scales, pltpu.VMEM(kept.shape, F32)], f"split{index}{dim}", 4 << 20, 12,
        )

    sent = project("send", False)
    with jax.named_scope("cores"):
        got = [swap(value, 1) for value in sent]
    own = project("own", True)
    state = []
    for i, (_, order) in enumerate(CHUNKS):
        codes, kept = join(i, own[i], got[i], order[0])
        with jax.named_scope(f"x{i}{order[0]}"):
            state.append((swap(codes, BITS[order[0]]), kept))
    for stage in (1, 2):
        for i, (_, order) in enumerate(CHUNKS):
            codes, kept = exchange(i, *state[i], order[stage])
            with jax.named_scope(f"x{i}{order[stage]}"):
                state[i] = (swap(codes, BITS[order[stage]]), kept)


    leave, stay = call(
        functools.partial(outer_kernel, len(CHUNKS)), sum(((g, k) for g, k in state), ()), [vmem] * (2 * len(CHUNKS)),
        (sds((2, K // 4, K)), sds((2, K // 4, K))),
        [pltpu.VMEM((K, K), F32)] + [pltpu.VMEM(k.shape, F32) for _, k in state], "outer", 2 << 20, 12,
    )
    mine = stay + swap(leave, 1)
    here = lax.dynamic_index_in_dim(mine, y, 0, keepdims=False)
    there = swap(lax.dynamic_index_in_dim(mine, 1 - y, 0, keepdims=False), 2)
    first = jnp.where(y == 0, here, there)
    second = jnp.where(y == 0, there, here)
    flat = jnp.stack([first, second]).reshape(2, K // 4 * K)
    scores = pl.pallas_call(
        scores_kernel, out_shape=sds((2, test_grads.shape[0])), in_specs=[vmem] * 2, out_specs=vmem, name="scores",
        compiler_params=pltpu.CompilerParams(vmem_limit_bytes=12 << 20),
    )(flat, test_grads)
    for bit in (1, 2, 4, 8):
        scores = scores + swap(scores, bit)
    return scores


def shards(
    attn_in, attn_grad, ffn_in, ffn_grad, proj_attn_in, proj_attn_out, proj_ffn_in, proj_ffn_out, test_grads
):
    layers, _, total = attn_in.shape
    devices = lax.axis_size("tp")
    modules = ((attn_grad, proj_attn_out, attn_in, proj_attn_in), (ffn_grad, proj_ffn_out, ffn_in, proj_ffn_in))
    columns = []
    for layer in range(layers):
        for grad, out, source, into in modules:
            for act, weight in ((grad, out), (source, into)):
                columns.append(
                    lax.dot_general(
                        weight[layer], act[layer], (((0,), (0,)), ((), ())), preferred_element_type=F32
                    )
                )
    rows = total // devices
    projected = lax.psum_scatter(jnp.concatenate(columns), "tp", scatter_dimension=1, tiled=True)
    token = lax.axis_index("tp") * rows + jnp.arange(rows, dtype=jnp.int32)
    member = (token // LEN)[None, :] == jnp.arange(SEQS, dtype=jnp.int32)[:, None]
    pairs = projected.reshape(2 * layers, 2, K, rows)
    grads = jnp.where(member[:, None, None, :], pairs[None, :, 0], 0.0)
    outer = jnp.einsum("snat,nbt->snab", grads, pairs[:, 1], precision=HIGH)
    flat = outer.reshape(SEQS, devices, -1).transpose(1, 0, 2)
    flat = flat.reshape(devices, -1)
    owned = lax.psum_scatter(flat, "tp", scatter_dimension=0, tiled=True).reshape(SEQS, -1)
    scores = lax.dot_general(
        owned, test_grads.astype(F32), (((1,), (1,)), ((), ())), precision=HIGH, preferred_element_type=F32
    )
    return lax.psum(scores, "tp")


def solution(mesh):
    placed = (P(None, "tp", "grp"),) * 4 + (P(None, "tp", None),) * 4 + (P(None, "tp"),)
    body = cube if mesh.shape["tp"] == 16 else shards
    return jax.shard_map(body, mesh=mesh, in_specs=placed, out_specs=P("grp", None), check_vma=False)
```

time: 294 us -> 79.4 us (0.27)
  waiting for transfers between devices: 210 us -> 39.7 us
  blocking collectives: 33.2 us -> 0 us
  matrix products: 30.8 us -> 0 us
  Pallas kernels: 0 us -> 24.2 us
  starting transfers between devices: 0.04 us -> 14.3 us
  between operations: 13.5 us -> 0.15 us
  local copies, waits for them, and re-layouts: 6.31 us -> 0.17 us
    reduce_scatter x1 -> x0, waiting for transfers between devices: 106 us -> none  [shards(): lax.psum_scatter(project_all(sliced, projs), 'tp', scatter_dimension=0, t...]
    unnamed x3 -> x0, waiting for transfers between devices: 103 us -> none
    ppermute x0 -> x14, waiting for transfers between devices: none -> 39.7 us  [swap(): return lax.ppermute(value, 'tp', [(i, i ^ bit) for i in range(16)])]
    psum x1 -> x0, blocking collectives: 33.2 us -> none  [shards(): return lax.psum(partial_scores, 'tp')]
    dot_general x13 -> x0, matrix products: 30.8 us -> none  [the longest x8 23.6 us: project_all(): lax.dot_general(source[layer], weight[layer], (((0,), (0,)), ((), ())), p...]
    pallas_call x0 -> x10, Pallas kernels: none -> 24.2 us  [the longest x9 22.5 us: call(): pl.pallas_call(chained, out_shape=(sds((4,), jnp.int32), *outs), in_specs...]
    ppermute x0 -> x14, starting transfers between devices: none -> 14.3 us  [swap(): return lax.ppermute(value, 'tp', [(i, i ^ bit) for i in range(16)])]
    unnamed x17 -> x2, local copies, waits for them, and re-layouts: 4.98 us -> 0.01 us
  transfers between devices with their start and end apart: 2 -> 14, of which waited for: 2 -> 10; matrix products, arithmetic and copies ran while one was open for 0% -> 0% of each run, Pallas kernels for 0% -> 16%
where the time goes in v2:
time: 79.4 us; the launch traced here: 79.2 us
  waiting for transfers between devices  39.7 us (50%)
  Pallas kernels  24.2 us (30%)
  starting transfers between devices  14.3 us (18%)
    ppermute x14, waiting for transfers between devices, swap(): return lax.ppermute(value, 'tp', [(i, i ^ bit) for i in range(16)])  39.7 us
    pallas_call x9, Pallas kernels, call(): pl.pallas_call(chained, out_shape=(sds((4,), jnp.int32), *outs), in_specs...  22.5 us
    ppermute x14, starting transfers between devices, swap(): return lax.ppermute(value, 'tp', [(i, i ^ bit) for i in range(16)])  14.3 us
    pallas_call x1, Pallas kernels, cube(): pl.pallas_call(scores_kernel, out_shape=sds((2, test_grads.shape[0])), in...  1.72 us
  transfers between devices with their start and end apart: 14, of which 10 were waited for; matrix products, arithmetic and copies ran while one was open for 0% of the time, Pallas kernels for 16%

profile of v2, /device:TPU:0, one launch (start us, length us, event | category | flops | bytes accessed | tf_op | source)
XLA Modules:
  0.0 79.2 jit_solution(5207999662046465592)
XLA Ops:
  0.0 0.1 pad_add_fusion.where_ref
  0.1 6.7 %send.1 = (s32[4]{0:T(128)S(1)}, f32[2,2,128,1024]{3,2,1,0:T(8,128)S(1)}, f32[2,2,128,1024]{3,2,1,0:T(8,128)S(1)}) custom-call(s32[4]{0:T(128)S(1)} %pad_add_fusion.where_ref, bf16[2,256,4096]{2,1,0:T(8,128)(2,1)} %refs_0_.3, bf16[2,256,4096]{2,1,0:T(8,128)(2,1)} %refs_1_.3, bf16[2,256,4096]{2,1,0:T(8,128)(2,1)} %refs_2_.3, bf16[2,896,4096]{2,1,0:T(8,128)(2,1)} %refs_3_.3, ...), custom_call_target="tpu_custom_call" | custom-call | bytes 16777216 | tf_op jit(solution)/shard_map/send/pallas_call | solution.py:184
  6.8 0.6 collective-permute-start
  7.4 0.1 collective-permute-start.1
  7.5 6.7 %own.1 = (s32[4]{0:T(128)S(1)}, f32[2,2,128,1024]{3,2,1,0:T(8,128)S(1)}, f32[2,2,128,1024]{3,2,1,0:T(8,128)S(1)}) custom-call(s32[4]{0:T(128)S(1)} %get-tuple-element.31.where_ref, bf16[2,256,4096]{2,1,0:T(8,128)(2,1)} %refs_0_.3, bf16[2,256,4096]{2,1,0:T(8,128)(2,1)} %refs_1_.3, bf16[2,256,4096]{2,1,0:T(8,128)(2,1)} %refs_2_.3, ...), custom_call_target="tpu_custom_call" | custom-call | bytes 16777216 | tf_op jit(solution)/shard_map/own/pallas_call | solution.py:184
  14.2 0.0 collective-permute-done.refs_1_
  14.2 1.2 %join0s.1 = (s32[4]{0:T(128)S(1)}, bf16[520,512]{1,0:T(8,128)(2,1)S(1)}, f32[2,2,128,512]{3,2,1,0:T(8,128)S(1)}) custom-call(s32[4]{0:T(128)S(1)} %get-tuple-element.32.where_ref, f32[2,2,128,1024]{3,2,1,0:T(8,128)S(1)} %get-tuple-element.33.refs_0_, f32[2,2,128,1024]{3,2,1,0:T(8,128)S(1)} %collective-permute-done.refs_1_), custom_call_target="tpu_custom_call" | custom-call | bytes 4194304 | tf_op jit(solution)/shard_map/join0s/pallas_call | solution.py:184
  15.4 0.0 collective-permute-done.1.refs_1_
  15.4 1.3 %join1m.1 = (s32[4]{0:T(128)S(1)}, bf16[264,1024]{1,0:T(8,128)(2,1)S(1)}, f32[2,1,128,1024]{3,2,1,0:T(8,128)S(1)}) custom-call(s32[4]{0:T(128)S(1)} %get-tuple-element.35.where_ref, f32[2,2,128,1024]{3,2,1,0:T(8,128)S(1)} %get-tuple-element.36.refs_0_, f32[2,2,128,1024]{3,2,1,0:T(8,128)S(1)} %collective-permute-done.1.refs_1_), custom_call_target="tpu_custom_call" | custom-call | bytes 4194304 | tf_op jit(solution)/shard_map/join1m/pallas_call | solution.py:184
  16.8 3.1 %collective-permute-start.3 = (bf16[264,1024]{1,0:T(8,128)(2,1)S(1)}, bf16[264,1024]{1,0:T(8,128)(2,1)S(1)}, u32[]{:S(2)}, u32[]{:S(2)}) collective-permute-start(bf16[264,1024]{1,0:T(8,128)(2,1)S(1)} %get-tuple-element.42), channel_id=1, source_target_pairs={{0,4},{1,5},{2,6},{3,7},{4,0},{5,1},{6,2},{7,3},{8,12},{9,13},{10,... | collective-permute-start | bytes 1622024 | tf_op jit(solution)/shard_map/x1m/ppermute | solution.py:170
  19.8 1.5 %collective-permute-start.2 = (bf16[520,512]{1,0:T(8,128)(2,1)S(1)}, bf16[520,512]{1,0:T(8,128)(2,1)S(1)}, u32[]{:S(2)}, u32[]{:S(2)}) collective-permute-start(bf16[520,512]{1,0:T(8,128)(2,1)S(1)} %get-tuple-element.39), channel_id=1, source_target_pairs={{0,2},{1,3},{2,0},{3,1},{4,6},{5,7},{6,4},{7,5},{8,10},{9,11},{10,... | collective-permute-start | bytes 1597448 | tf_op jit(solution)/shard_map/x0s/ppermute | solution.py:170
  21.4 12.3 %collective-permute-done.2.refs_0_ = bf16[520,512]{1,0:T(8,128)(2,1)S(1)} collective-permute-done((bf16[520,512]{1,0:T(8,128)(2,1)S(1)}, bf16[520,512]{1,0:T(8,128)(2,1)S(1)}, u32[]{:S(2)}, u32[]{:S(2)}) %collective-permute-start.2) | collective-permute-done | bytes 532512 | tf_op jit(solution)/shard_map/x0s/ppermute | solution.py:170
  33.6 1.6 %split0m.1 = (s32[4]{0:T(128)S(1)}, bf16[264,512]{1,0:T(8,128)(2,1)S(1)}, f32[2,1,128,512]{3,2,1,0:T(8,128)S(1)}) custom-call(s32[4]{0:T(128)S(1)} %get-tuple-element.38.where_ref, bf16[520,512]{1,0:T(8,128)(2,1)S(1)} %collective-permute-done.2.refs_0_, f32[2,2,128,512]{3,2,1,0:T(8,128)S(1)} %get-tuple-element.40.refs_1_), custom_call_target="tpu_custom_call" | custom-call | bytes 4194304 | tf_op jit(solution)/shard_map/split0m/pallas_call | solution.py:184
  35.2 0.0 copy-start
  35.3 0.4 collective-permute-start.4
  35.7 0.0 collective-permute-done.3.refs_0_
  35.7 1.2 %split1s.1 = (s32[4]{0:T(128)S(1)}, bf16[264,512]{1,0:T(8,128)(2,1)S(1)}, f32[2,1,128,512]{3,2,1,0:T(8,128)S(1)}) custom-call(s32[4]{0:T(128)S(1)} %get-tuple-element.41.where_ref, bf16[264,1024]{1,0:T(8,128)(2,1)S(1)} %collective-permute-done.3.refs_0_, f32[2,1,128,1024]{3,2,1,0:T(8,128)S(1)} %get-tuple-element.43.refs_1_), custom_call_target="tpu_custom_call" | custom-call | bytes 4194304 | tf_op jit(solution)/shard_map/split1s/pallas_call | solution.py:184
  36.9 1.7 %collective-permute-start.5 = (bf16[264,512]{1,0:T(8,128)(2,1)S(1)}, bf16[264,512]{1,0:T(8,128)(2,1)S(1)}, u32[]{:S(2)}, u32[]{:S(2)}) collective-permute-start(bf16[264,512]{1,0:T(8,128)(2,1)S(1)} %get-tuple-element.48), channel_id=1, source_target_pairs={{0,2},{1,3},{2,0},{3,1},{4,6},{5,7},{6,4},{7,5},{8,10},{9,11},{10,... | collective-permute-start | bytes 811016 | tf_op jit(solution)/shard_map/x1s/ppermute | solution.py:170
  38.6 4.1 %collective-permute-done.4.refs_0_ = bf16[264,512]{1,0:T(8,128)(2,1)S(1)} collective-permute-done((bf16[264,512]{1,0:T(8,128)(2,1)S(1)}, bf16[264,512]{1,0:T(8,128)(2,1)S(1)}, u32[]{:S(2)}, u32[]{:S(2)}) %collective-permute-start.4) | collective-permute-done | bytes 270368 | tf_op jit(solution)/shard_map/x0m/ppermute | solution.py:170
  42.6 1.1 %split0l.1 = (s32[4]{0:T(128)S(1)}, bf16[136,512]{1,0:T(8,128)(2,1)S(1)}, f32[1,1,128,512]{3,2,1,0:T(8,128)S(1)}) custom-call(s32[4]{0:T(128)S(1)} %get-tuple-element.44.where_ref, bf16[264,512]{1,0:T(8,128)(2,1)S(1)} %collective-permute-done.4.refs_0_, f32[2,1,128,512]{3,2,1,0:T(8,128)S(1)} %get-tuple-element.46.refs_1_), custom_call_target="tpu_custom_call" | custom-call | bytes 4194304 | tf_op jit(solution)/shard_map/split0l/pallas_call | solution.py:184
  43.8 2.6 %collective-permute-start.6 = (bf16[136,512]{1,0:T(8,128)(2,1)S(1)}, bf16[136,512]{1,0:T(8,128)(2,1)S(1)}, u32[]{:S(2)}, u32[]{:S(2)}) collective-permute-start(bf16[136,512]{1,0:T(8,128)(2,1)S(1)} %get-tuple-element.51), channel_id=1, source_target_pairs={{0,8},{1,9},{2,10},{3,11},{4,12},{5,13},{6,14},{7,15},{8,0},{9,1},... | collective-permute-start | bytes 417800 | tf_op jit(solution)/shard_map/x0l/ppermute | solution.py:170
  46.4 0.0 collective-permute-done.5.refs_0_
  46.4 1.1 %split1l.1 = (s32[4]{0:T(128)S(1)}, bf16[136,512]{1,0:T(8,128)(2,1)S(1)}, f32[1,1,128,512]{3,2,1,0:T(8,128)S(1)}) custom-call(s32[4]{0:T(128)S(1)} %get-tuple-element.47.where_ref, bf16[264,512]{1,0:T(8,128)(2,1)S(1)} %collective-permute-done.5.refs_0_, f32[2,1,128,512]{3,2,1,0:T(8,128)S(1)} %get-tuple-element.49.refs_1_), custom_call_target="tpu_custom_call" | custom-call | bytes 4194304 | tf_op jit(solution)/shard_map/split1l/pallas_call | solution.py:184
  47.6 0.4 collective-permute-start.7
  48.0 7.8 %collective-permute-done.6.refs_0_ = bf16[136,512]{1,0:T(8,128)(2,1)S(1)} collective-permute-done((bf16[136,512]{1,0:T(8,128)(2,1)S(1)}, bf16[136,512]{1,0:T(8,128)(2,1)S(1)}, u32[]{:S(2)}, u32[]{:S(2)}) %collective-permute-start.6) | collective-permute-done | bytes 139296 | tf_op jit(solution)/shard_map/x0l/ppermute | solution.py:170
  55.8 1.6 %collective-permute-done.7.refs_2_ = bf16[136,512]{1,0:T(8,128)(2,1)S(1)} collective-permute-done((bf16[136,512]{1,0:T(8,128)(2,1)S(1)}, bf16[136,512]{1,0:T(8,128)(2,1)S(1)}, u32[]{:S(2)}, u32[]{:S(2)}) %collective-permute-start.7) | collective-permute-done | bytes 139296 | tf_op jit(solution)/shard_map/x1l/ppermute | solution.py:170
  57.4 1.4 %outer.1 = (s32[4]{0:T(128)}, f32[2,16,64]{2,1,0:T(8,128)S(1)}, f32[2,16,64]{2,1,0:T(8,128)S(1)}) custom-call(s32[4]{0:T(128)S(1)} %get-tuple-element.50.where_ref, bf16[136,512]{1,0:T(8,128)(2,1)S(1)} %collective-permute-done.6.refs_0_, f32[1,1,128,512]{3,2,1,0:T(8,128)S(1)} %get-tuple-element.52.refs_1_, ...), custom_call_target="tpu_custom_call" | custom-call | bytes 2097152 | tf_op jit(solution)/shard_map/outer/pallas_call | solution.py:184
  58.7 0.1 collective-permute-start.8
  58.8 1.2 %collective-permute-done.8 = f32[2,16,64]{2,1,0:T(8,128)S(1)} collective-permute-done((f32[2,16,64]{2,1,0:T(8,128)S(1)}, f32[2,16,64]{2,1,0:T(8,128)S(1)}, u32[]{:S(2)}, u32[]{:S(2)}) %collective-permute-start.8) | collective-permute-done | bytes 8224 | tf_op jit(solution)/shard_map/ppermute | solution.py:170
  60.0 1.4 %collective-permute-start.9 = (f32[16,64]{1,0:T(8,128)S(1)}, f32[16,64]{1,0:T(8,128)S(1)}, u32[]{:S(2)}, u32[]{:S(2)}) collective-permute-start(f32[16,64]{1,0:T(8,128)S(1)} %dynamic-slice_bitcast_fusion), channel_id=1, source_target_pairs={{0,2},{1,3},{2,0},{3,1},{4,6},{5,7},{6,4},{7,5},{8,10},{9,11},{10,... | collective-permute-start | bytes 12296 | tf_op jit(solution)/shard_map/ppermute | solution.py:170
  61.4 2.2 %collective-permute-done.9 = f32[16,64]{1,0:T(8,128)S(1)} collective-permute-done((f32[16,64]{1,0:T(8,128)S(1)}, f32[16,64]{1,0:T(8,128)S(1)}, u32[]{:S(2)}, u32[]{:S(2)}) %collective-permute-start.9) | collective-permute-done | bytes 4128 | tf_op jit(solution)/shard_map/ppermute | solution.py:170
  63.7 0.1 stack.29
  63.7 0.1 stack.30
  63.8 0.0 copy-done
  63.8 1.7 %scores.1 = f32[2,1024]{1,0:T(2,128)S(1)} custom-call(f32[2,1024]{1,0:T(2,128)S(1)} %pad_maximum_fusion.flat_ref, bf16[1024,1024]{1,0:T(8,128)(2,1)S(1)} %copy-done), custom_call_target="tpu_custom_call" | custom-call | tf_op jit(solution)/shard_map/scores/pallas_call | solution.py:250
  65.6 0.0 collective-permute-start.10
  65.6 1.2 %collective-permute-done.10 = f32[2,1024]{1,0:T(2,128)S(1)} collective-permute-done((f32[2,1024]{1,0:T(2,128)S(1)}, f32[2,1024]{1,0:T(2,128)S(1)}, u32[]{:S(2)}, u32[]{:S(2)}) %collective-permute-start.10) | collective-permute-done | bytes 8224 | tf_op jit(solution)/shard_map/ppermute | solution.py:170
  66.8 1.4 %collective-permute-start.11 = (f32[2,1024]{1,0:T(2,128)S(1)}, f32[2,1024]{1,0:T(2,128)S(1)}, u32[]{:S(2)}, u32[]{:S(2)}) collective-permute-start(f32[2,1024]{1,0:T(2,128)S(1)} %add.42), channel_id=1, source_target_pairs={{0,2},{1,3},{2,0},{3,1},{4,6},{5,7},{6,4},{7,5},{8,10},{9,11},{10,... | collective-permute-start | bytes 24584 | tf_op jit(solution)/shard_map/ppermute | solution.py:170
  68.2 2.2 %collective-permute-done.11 = f32[2,1024]{1,0:T(2,128)S(1)} collective-permute-done((f32[2,1024]{1,0:T(2,128)S(1)}, f32[2,1024]{1,0:T(2,128)S(1)}, u32[]{:S(2)}, u32[]{:S(2)}) %collective-permute-start.11) | collective-permute-done | bytes 8224 | tf_op jit(solution)/shard_map/ppermute | solution.py:170
  70.4 0.0 collective-permute-start.12
  70.4 3.6 %collective-permute-done.12 = f32[2,1024]{1,0:T(2,128)S(1)} collective-permute-done((f32[2,1024]{1,0:T(2,128)S(1)}, f32[2,1024]{1,0:T(2,128)S(1)}, u32[]{:S(2)}, u32[]{:S(2)}) %collective-permute-start.12) | collective-permute-done | bytes 8224 | tf_op jit(solution)/shard_map/ppermute | solution.py:170
  74.1 1.0 %collective-permute-start.13 = (f32[2,1024]{1,0:T(2,128)S(1)}, f32[2,1024]{1,0:T(2,128)S(1)}, u32[]{:S(2)}, u32[]{:S(2)}) collective-permute-start(f32[2,1024]{1,0:T(2,128)S(1)} %add.44), channel_id=1, source_target_pairs={{0,8},{1,9},{2,10},{3,11},{4,12},{5,13},{6,14},{7,15},{8,0},{9,1},... | collective-permute-start | bytes 24584 | tf_op jit(solution)/shard_map/ppermute | solution.py:170
  75.1 3.5 %collective-permute-done.13 = f32[2,1024]{1,0:T(2,128)S(1)} collective-permute-done((f32[2,1024]{1,0:T(2,128)S(1)}, f32[2,1024]{1,0:T(2,128)S(1)}, u32[]{:S(2)}, u32[]{:S(2)}) %collective-permute-start.13) | collective-permute-done | bytes 8224 | tf_op jit(solution)/shard_map/ppermute | solution.py:170
  78.6 0.6 add.45
  (7 shorter events, 0.0 us)
Async XLA Ops:
  6.8 7.4 %collective-permute-start = (f32[2,2,128,1024]{3,2,1,0:T(8,128)S(1)}, f32[2,2,128,1024]{3,2,1,0:T(8,128)S(1)}, u32[]{:S(2)}, u32[]{:S(2)}) collective-permute-start(f32[2,2,128,1024]{3,2,1,0:T(8,128)S(1)} %get-tuple-element.34), channel_id=1, source_target_pairs={{0,1},{1,0},{2,3},{3,2},{4,5},{5,4},{6,7},{7,6},{8,9},{9,8},{10,11... | collective-permute-start | bytes 6291464 | tf_op jit(solution)/shard_map/cores/ppermute | solution.py:170
  7.4 8.0 %collective-permute-start.1 = (f32[2,2,128,1024]{3,2,1,0:T(8,128)S(1)}, f32[2,2,128,1024]{3,2,1,0:T(8,128)S(1)}, u32[]{:S(2)}, u32[]{:S(2)}) collective-permute-start(f32[2,2,128,1024]{3,2,1,0:T(8,128)S(1)} %get-tuple-element.37), channel_id=1, source_target_pairs={{0,1},{1,0},{2,3},{3,2},{4,5},{5,4},{6,7},{7,6},{8,9},{9,8},{10,11... | collective-permute-start | bytes 6291464 | tf_op jit(solution)/shard_map/cores/ppermute | solution.py:170
  16.8 18.9 %collective-permute-start.3 = (bf16[264,1024]{1,0:T(8,128)(2,1)S(1)}, bf16[264,1024]{1,0:T(8,128)(2,1)S(1)}, u32[]{:S(2)}, u32[]{:S(2)}) collective-permute-start(bf16[264,1024]{1,0:T(8,128)(2,1)S(1)} %get-tuple-element.42), channel_id=1, source_target_pairs={{0,4},{1,5},{2,6},{3,7},{4,0},{5,1},{6,2},{7,3},{8,12},{9,13},{10,... | collective-permute-start | bytes 1622024 | tf_op jit(solution)/shard_map/x1m/ppermute | solution.py:170
  19.8 13.8 %collective-permute-start.2 = (bf16[520,512]{1,0:T(8,128)(2,1)S(1)}, bf16[520,512]{1,0:T(8,128)(2,1)S(1)}, u32[]{:S(2)}, u32[]{:S(2)}) collective-permute-start(bf16[520,512]{1,0:T(8,128)(2,1)S(1)} %get-tuple-element.39), channel_id=1, source_target_pairs={{0,2},{1,3},{2,0},{3,1},{4,6},{5,7},{6,4},{7,5},{8,10},{9,11},{10,... | collective-permute-start | bytes 1597448 | tf_op jit(solution)/shard_map/x0s/ppermute | solution.py:170
  35.2 28.6 %copy-start = (bf16[1024,1024]{1,0:T(8,128)(2,1)S(1)}, bf16[1024,1024]{1,0:T(8,128)(2,1)}, u32[]{:S(2)}) copy-start(bf16[1024,1024]{1,0:T(8,128)(2,1)} %tests_ref.1) | copy-start | bytes 6291460
  35.3 7.4 %collective-permute-start.4 = (bf16[264,512]{1,0:T(8,128)(2,1)S(1)}, bf16[264,512]{1,0:T(8,128)(2,1)S(1)}, u32[]{:S(2)}, u32[]{:S(2)}) collective-permute-start(bf16[264,512]{1,0:T(8,128)(2,1)S(1)} %get-tuple-element.45), channel_id=1, source_target_pairs={{0,4},{1,5},{2,6},{3,7},{4,0},{5,1},{6,2},{7,3},{8,12},{9,13},{10,... | collective-permute-start | bytes 811016 | tf_op jit(solution)/shard_map/x0m/ppermute | solution.py:170
  36.9 9.5 %collective-permute-start.5 = (bf16[264,512]{1,0:T(8,128)(2,1)S(1)}, bf16[264,512]{1,0:T(8,128)(2,1)S(1)}, u32[]{:S(2)}, u32[]{:S(2)}) collective-permute-start(bf16[264,512]{1,0:T(8,128)(2,1)S(1)} %get-tuple-element.48), channel_id=1, source_target_pairs={{0,2},{1,3},{2,0},{3,1},{4,6},{5,7},{6,4},{7,5},{8,10},{9,11},{10,... | collective-permute-start | bytes 811016 | tf_op jit(solution)/shard_map/x1s/ppermute | solution.py:170
  43.8 12.0 %collective-permute-start.6 = (bf16[136,512]{1,0:T(8,128)(2,1)S(1)}, bf16[136,512]{1,0:T(8,128)(2,1)S(1)}, u32[]{:S(2)}, u32[]{:S(2)}) collective-permute-start(bf16[136,512]{1,0:T(8,128)(2,1)S(1)} %get-tuple-element.51), channel_id=1, source_target_pairs={{0,8},{1,9},{2,10},{3,11},{4,12},{5,13},{6,14},{7,15},{8,0},{9,1},... | collective-permute-start | bytes 417800 | tf_op jit(solution)/shard_map/x0l/ppermute | solution.py:170
  47.6 9.8 %collective-permute-start.7 = (bf16[136,512]{1,0:T(8,128)(2,1)S(1)}, bf16[136,512]{1,0:T(8,128)(2,1)S(1)}, u32[]{:S(2)}, u32[]{:S(2)}) collective-permute-start(bf16[136,512]{1,0:T(8,128)(2,1)S(1)} %get-tuple-element.53), channel_id=1, source_target_pairs={{0,8},{1,9},{2,10},{3,11},{4,12},{5,13},{6,14},{7,15},{8,0},{9,1},... | collective-permute-start | bytes 417800 | tf_op jit(solution)/shard_map/x1l/ppermute | solution.py:170
  58.7 1.2 %collective-permute-start.8 = (f32[2,16,64]{2,1,0:T(8,128)S(1)}, f32[2,16,64]{2,1,0:T(8,128)S(1)}, u32[]{:S(2)}, u32[]{:S(2)}) collective-permute-start(f32[2,16,64]{2,1,0:T(8,128)S(1)} %get-tuple-element.56), channel_id=1, source_target_pairs={{0,1},{1,0},{2,3},{3,2},{4,5},{5,4},{6,7},{7,6},{8,9},{9,8},{10,11... | collective-permute-start | bytes 24584 | tf_op jit(solution)/shard_map/ppermute | solution.py:170
  60.0 3.7 %collective-permute-start.9 = (f32[16,64]{1,0:T(8,128)S(1)}, f32[16,64]{1,0:T(8,128)S(1)}, u32[]{:S(2)}, u32[]{:S(2)}) collective-permute-start(f32[16,64]{1,0:T(8,128)S(1)} %dynamic-slice_bitcast_fusion), channel_id=1, source_target_pairs={{0,2},{1,3},{2,0},{3,1},{4,6},{5,7},{6,4},{7,5},{8,10},{9,11},{10,... | collective-permute-start | bytes 12296 | tf_op jit(solution)/shard_map/ppermute | solution.py:170
  65.6 1.2 %collective-permute-start.10 = (f32[2,1024]{1,0:T(2,128)S(1)}, f32[2,1024]{1,0:T(2,128)S(1)}, u32[]{:S(2)}, u32[]{:S(2)}) collective-permute-start(f32[2,1024]{1,0:T(2,128)S(1)} %scores.1), channel_id=1, source_target_pairs={{0,1},{1,0},{2,3},{3,2},{4,5},{5,4},{6,7},{7,6},{8,9},{9,8},{10,11... | collective-permute-start | bytes 24584 | tf_op jit(solution)/shard_map/ppermute | solution.py:170
  66.8 3.7 %collective-permute-start.11 = (f32[2,1024]{1,0:T(2,128)S(1)}, f32[2,1024]{1,0:T(2,128)S(1)}, u32[]{:S(2)}, u32[]{:S(2)}) collective-permute-start(f32[2,1024]{1,0:T(2,128)S(1)} %add.42), channel_id=1, source_target_pairs={{0,2},{1,3},{2,0},{3,1},{4,6},{5,7},{6,4},{7,5},{8,10},{9,11},{10,... | collective-permute-start | bytes 24584 | tf_op jit(solution)/shard_map/ppermute | solution.py:170
  70.4 3.7 %collective-permute-start.12 = (f32[2,1024]{1,0:T(2,128)S(1)}, f32[2,1024]{1,0:T(2,128)S(1)}, u32[]{:S(2)}, u32[]{:S(2)}) collective-permute-start(f32[2,1024]{1,0:T(2,128)S(1)} %add.43), channel_id=1, source_target_pairs={{0,4},{1,5},{2,6},{3,7},{4,0},{5,1},{6,2},{7,3},{8,12},{9,13},{10,... | collective-permute-start | bytes 24584 | tf_op jit(solution)/shard_map/ppermute | solution.py:170
  74.1 4.5 %collective-permute-start.13 = (f32[2,1024]{1,0:T(2,128)S(1)}, f32[2,1024]{1,0:T(2,128)S(1)}, u32[]{:S(2)}, u32[]{:S(2)}) collective-permute-start(f32[2,1024]{1,0:T(2,128)S(1)} %add.44), channel_id=1, source_target_pairs={{0,8},{1,9},{2,10},{3,11},{4,12},{5,13},{6,14},{7,15},{8,0},{9,1},... | collective-permute-start | bytes 24584 | tf_op jit(solution)/shard_map/ppermute | solution.py:170

commit v3 on v2

--- a/solution.py
+++ b/solution.py
@@ -6,6 +6,7 @@
 from jax.experimental import pallas as pl
 from jax.experimental.pallas import tpu as pltpu
 from jax.sharding import PartitionSpec as P
+
 
 LEN = 2048
 SEQS = 2
@@ -81,18 +82,30 @@
     split(dim, total_ref, codes_ref, kept_ref, scales_ref, where_ref)
 
 
-def outer_kernel(chunks, where_ref, *refs):
-    ins, (leave_ref, stay_ref), totals = refs[: 2 * chunks], refs[2 * chunks : 2 * chunks + 2], refs[2 * chunks + 2 :]
-    out_ref, totals = totals[0], totals[1:]
+def products(ins, totals):
     total = None
-    for chunk in range(chunks):
-        sums = totals[chunk]
+    for chunk, sums in enumerate(totals):
         add_codes(ins[2 * chunk], ins[2 * chunk + 1], sums)
         part = lax.dot_general(
             sums[0, 0, :K, :], sums[0, 0, K:, :], (((1,), (1,)), ((), ())), precision=HIGH, preferred_element_type=F32
         )
         total = part if total is None else total + part
-    out_ref[...] = total
+    return total
+
+
+def early_kernel(where_ref, tests_in, *refs):
+    chunks = (len(refs) - 3) // 3
+    sum_ref, tests_ref, sem = refs[2 * chunks], refs[2 * chunks + 1], refs[-1]
+    copy = pltpu.make_async_copy(tests_in, tests_ref, sem)
+    copy.start()
+    sum_ref[...] = products(refs[: 2 * chunks], refs[2 * chunks + 2 : -1])
+    copy.wait()
+
+
+def outer_kernel(where_ref, early_ref, *refs):
+    chunks = (len(refs) - 3) // 3
+    leave_ref, stay_ref, out_ref = refs[2 * chunks : 2 * chunks + 3]
+    out_ref[...] = early_ref[...] + products(refs[: 2 * chunks], refs[2 * chunks + 3 :])
     core = where_ref[0]
     quarter = K // 4
     for y in range(2):
@@ -102,44 +115,58 @@
 
 def scores_kernel(flat_ref, tests_ref, out_ref):
     rest = flat_ref[...]
+    rows = rest.shape[0]
     parts = []
     for _ in range(3):
         part = rest.astype(BF16)
         parts.append(part)
         rest = rest - part.astype(F32)
-    total = None
-    for part in reversed(parts):
-        term = lax.dot_general(part, tests_ref[...], (((1,), (1,)), ((), ())), preferred_element_type=F32)
-        total = term if total is None else total + term
-    out_ref[...] = total
-
-
-def project_kernel(own, where_ref, *refs):
-    chunks = len(refs) - 17
-    acts, projs, outs = refs[:4], refs[4:8], refs[8 : 8 + chunks]
-    act_bufs, proj_bufs, sems = refs[8 + chunks : 12 + chunks], refs[12 + chunks : 16 + chunks], refs[16 + chunks]
-    core = where_ref[0] if own else 1 - where_ref[0]
+    terms = lax.dot_general(
+        jnp.concatenate(parts, axis=0), tests_ref[...], (((1,), (1,)), ((), ())), preferred_element_type=F32
+    )
+    out_ref[...] = terms[2 * rows :] + terms[rows : 2 * rows] + terms[:rows]
+
+
+def project_kernel(own, first, ahead, after, where_ref, *refs):
+    acts, projs, refs = refs[:4], refs[4:8], refs[8:]
+    given, refs = refs[:ahead], refs[ahead:]
+    proj_bufs, sems, act_bufs = refs[-5:-1], refs[-1], refs[-9:-5]
+    outs, fetched = refs[: -9 - after], refs[len(refs) - 9 - after : -9]
     layers, _, total = acts[0].shape
     quarter = total // 4
+    width = act_bufs[0].shape[-1]
     pieces = [(s, l, i) for s in range(2) for l in range(layers) for i in range(4)]
+
+    def fetch(index, core, target, sem):
+        s, l, i = pieces[index]
+        lanes = pl.ds(pl.multiple_of(s * (total // 2) + core * quarter + first, 128), width)
+        copy = pltpu.make_async_copy(acts[i].at[l, :, lanes], target, sem)
+        copy.start()
+        return copy
+
+    core = where_ref[0] if own else 1 - where_ref[0]
+    copies = {}
     loads = [pltpu.make_async_copy(projs[i], proj_bufs[i], sems.at[len(pieces) + i]) for i in range(4)]
-    copies = []
-    for index, (s, l, i) in enumerate(pieces):
-        lanes = pl.ds(pl.multiple_of(s * (total // 2) + core * quarter, 128), quarter)
-        copies.append(pltpu.make_async_copy(acts[i].at[l, :, lanes], act_bufs[i].at[s, l], sems.at[index]))
-    for copy in loads + copies:
+    for copy in loads:
         copy.start()
+    for index in range(ahead, len(pieces)):
+        s, l, i = pieces[index]
+        copies[index] = fetch(index, core, act_bufs[i].at[s, l], sems.at[index])
+    later = [fetch(j, where_ref[0], fetched[j], sems.at[len(pieces) + 4 + j]) for j in range(after)]
     for copy in loads:
         copy.wait()
     for index, (s, l, i) in enumerate(pieces):
-        copies[index].wait()
+        if index in copies:
+            copies[index].wait()
+        act = act_bufs[i][s, l] if index in copies else given[index][...]
+        value = jnp.dot(proj_bufs[i][l], act, preferred_element_type=F32)
         at = 0
         for out_ref in outs:
-            width = out_ref.shape[-1] // 2
-            out_ref[l, i // 2, i % 2 * K : i % 2 * K + K, s * width : (s + 1) * width] = jnp.dot(
-                proj_bufs[i][l], act_bufs[i][s, l, :, at : at + width], preferred_element_type=F32
-            )
-            at += width
+            span = out_ref.shape[-1] // 2
+            out_ref[l, i // 2, i % 2 * K : i % 2 * K + K, s * span : (s + 1) * span] = value[:, at : at + span]
+            at += span
+    for copy in later:
+        copy.wait()
 
 
 def join_kernel(dim, where_ref, own_ref, got_ref, codes_ref, kept_ref, scales_ref, total_ref):
@@ -147,18 +174,21 @@
     split(dim, total_ref, codes_ref, kept_ref, scales_ref, where_ref)
 
 
-CHUNKS = ((512, 'sml'), (512, 'msl'))
+CHUNKS = ((384, 'sml'), (384, 'msl'), (256, 'sml'))
+PLAN = (('send', 0, (0, 1, 2)), ('own', 0, (0, 1, 2)), ('k', 0, 0), ('x', 0, 0), ('k', 1, 0), ('x', 1, 0), ('k', 2, 0), ('x', 2, 0), ('k', 0, 1), ('x', 0, 1), ('k', 1, 1), ('x', 1, 1), ('k', 2, 1), ('x', 2, 1), ('k', 0, 2), ('x', 0, 2), ('k', 1, 2), ('x', 1, 2), ('k', 2, 2), ('x', 2, 2))
+AFTER = 4
+EARLY = 1
+FINISH = tuple(i for kind, i, stage in PLAN if kind == "x" and stage == 2)
 BITS = {"s": 2, "m": 4, "l": 8}
 
 
-def cube(
+def cube_body(
     attn_in, attn_grad, ffn_in, ffn_grad, proj_attn_in, proj_attn_out, proj_ffn_in, proj_ffn_out, test_grads
 ):
     acts = (attn_grad, attn_in, ffn_grad, ffn_in)
     projs = tuple(w.transpose(0, 2, 1) for w in (proj_attn_out, proj_attn_in, proj_ffn_out, proj_ffn_in))
     acts = tuple(pltpu.with_memory_space_constraint(a, pltpu.HBM) for a in acts)
     projs = tuple(pltpu.with_memory_space_constraint(a, pltpu.HBM) for a in projs)
-    quarter = attn_in.shape[2] // 4
     me = lax.axis_index("tp")
     core, y, z = me % 2, (me // 2) % 2, me // 4
     where = jnp.stack([core, y, z % 2, z // 2]).astype(jnp.int32)
@@ -172,22 +202,12 @@
     def sds(shape, dtype=F32):
         return jax.ShapeDtypeStruct(shape, dtype)
 
-    def call(kernel, ins, in_specs, outs, scratch, name, cost, limit):
-        nonlocal where
-
-        def chained(where_ref, *refs):
-            passed = refs[len(ins)]
-            for i in range(4):
-                passed[i] = where_ref[i]
-            kernel(where_ref, *refs[: len(ins)], *refs[len(ins) + 1 :])
-
-        where, *results = pl.pallas_call(
-            chained, out_shape=(sds((4,), jnp.int32), *outs), in_specs=[smem] + in_specs,
-            out_specs=[smem] + [vmem] * len(outs), scratch_shapes=scratch,
-            name=name, cost_estimate=pl.CostEstimate(flops=0, bytes_accessed=cost, transcendentals=0),
+    def call(kernel, ins, in_specs, outs, scratch, cost, limit):
+        return pl.pallas_call(
+            kernel, out_shape=outs, in_specs=[smem] + in_specs, out_specs=[vmem] * len(outs), scratch_shapes=scratch,
+            cost_estimate=pl.CostEstimate(flops=0, bytes_accessed=cost, transcendentals=0),
             compiler_params=pltpu.CompilerParams(vmem_limit_bytes=limit << 20),
         )(where, *ins)
-        return results
 
     def outputs(dim, shape):
         layers, modules, _, tokens = shape
@@ -198,48 +218,66 @@
         scales = max(8, groups)
         return (sds((groups * K + scales, kept[3]), BF16), sds(kept)), pltpu.VMEM((scales, kept[3]), F32)
 
-    def project(name, own):
-        scratch = [pltpu.VMEM((2, a.shape[0], a.shape[1], quarter), BF16) for a in acts]
-        scratch += [pltpu.VMEM(w.shape, BF16) for w in projs] + [pltpu.SemaphoreType.DMA((8 * acts[0].shape[0] + 4,))]
-        outs = tuple(sds((2, 2, 2 * K, 2 * width)) for width, _ in CHUNKS)
-        return call(
-            functools.partial(project_kernel, own), (*acts, *projs), [hbm] * 8, outs, scratch, name, 16 << 20, 24
+    def project(own, chunks, given=(), after=0):
+        widths = [CHUNKS[i][0] for i in chunks]
+        first = sum(width for width, _ in CHUNKS[: chunks[0]])
+        width = sum(widths)
+        layers = acts[0].shape[0]
+        scratch = [pltpu.VMEM((2, layers, a.shape[1], width), BF16) for a in acts]
+        scratch += [pltpu.VMEM(w.shape, BF16) for w in projs] + [pltpu.SemaphoreType.DMA((8 * layers + 4 + after,))]
+        outs = tuple(sds((2, 2, 2 * K, 2 * width)) for width in widths)
+        outs += tuple(sds((acts[i % 4].shape[1], width), BF16) for i in range(after))
+        results = call(
+            functools.partial(project_kernel, own, first, len(given), after), (*acts, *projs, *given),
+            [hbm] * 8 + [vmem] * len(given), outs, scratch, 16 << 20, 26,
         )
-
-    def join(index, own, got, dim):
+        return results[: len(widths)], results[len(widths) :]
+
+    def join(own, got, dim):
         outs, scales = outputs(dim, own.shape)
         return call(
             functools.partial(join_kernel, dim), (own, got), [vmem] * 2, outs, [scales, pltpu.VMEM(own.shape, F32)],
-            f"join{index}{dim}", 4 << 20, 12,
+            4 << 20, 12,
         )
 
-    def exchange(index, codes, kept, dim):
+    def exchange(codes, kept, dim):
         outs, scales = outputs(dim, kept.shape)
         return call(
             functools.partial(split_kernel, dim), (codes, kept), [vmem] * 2, outs,
-            [scales, pltpu.VMEM(kept.shape, F32)], f"split{index}{dim}", 4 << 20, 12,
+            [scales, pltpu.VMEM(kept.shape, F32)], 4 << 20, 12,
         )
 
-    sent = project("send", False)
-    with jax.named_scope("cores"):
-        got = [swap(value, 1) for value in sent]
-    own = project("own", True)
-    state = []
-    for i, (_, order) in enumerate(CHUNKS):
-        codes, kept = join(i, own[i], got[i], order[0])
-        with jax.named_scope(f"x{i}{order[0]}"):
-            state.append((swap(codes, BITS[order[0]]), kept))
-    for stage in (1, 2):
-        for i, (_, order) in enumerate(CHUNKS):
-            codes, kept = exchange(i, *state[i], order[stage])
-            with jax.named_scope(f"x{i}{order[stage]}"):
-                state[i] = (swap(codes, BITS[order[stage]]), kept)
-
-
+    got, own, state, ready = {}, {}, {}, ()
+    for step in PLAN:
+        kind, i, stage = step
+        if kind == "send":
+            sent, ready = project(False, stage, (), AFTER)
+            for j, value in zip(stage, sent):
+                got[j] = swap(value, 1)
+        elif kind == "own":
+            made, _ = project(True, stage, ready)
+            own.update(zip(stage, made))
+            ready = ()
+        elif kind == "k" and stage == 0:
+            state[i] = join(own[i], got[i], CHUNKS[i][1][0])
+        elif kind == "k":
+            state[i] = exchange(*state[i], CHUNKS[i][1][stage])
+        else:
+            dim = CHUNKS[i][1][stage]
+            state[i] = (swap(state[i][0], BITS[dim]), state[i][1])
+    state = [tuple(state[i]) for i in range(len(CHUNKS))]
+
+
+    before, last = [state[i] for i in FINISH[:EARLY]], [state[i] for i in FINISH[EARLY:]]
+    tests = pltpu.with_memory_space_constraint(test_grads, pltpu.HBM)
+    early, tests = call(
+        early_kernel, (tests, *sum(before, ())), [hbm] + [vmem] * (2 * len(before)),
+        (sds((K, K)), sds(tests.shape, tests.dtype)),
+        [pltpu.VMEM(k.shape, F32) for _, k in before] + [pltpu.SemaphoreType.DMA], 4 << 20, 12,
+    )
     leave, stay = call(
-        functools.partial(outer_kernel, len(CHUNKS)), sum(((g, k) for g, k in state), ()), [vmem] * (2 * len(CHUNKS)),
-        (sds((2, K // 4, K)), sds((2, K // 4, K))),
-        [pltpu.VMEM((K, K), F32)] + [pltpu.VMEM(k.shape, F32) for _, k in state], "outer", 2 << 20, 12,
+        outer_kernel, (early, *sum(last, ())), [vmem] * (1 + 2 * len(last)), (sds((2, K // 4, K)), sds((2, K // 4, K))),
+        [pltpu.VMEM((K, K), F32)] + [pltpu.VMEM(k.shape, F32) for _, k in last], 2 << 20, 12,
     )
     mine = stay + swap(leave, 1)
     here = lax.dynamic_index_in_dim(mine, y, 0, keepdims=False)
@@ -250,10 +288,14 @@
     scores = pl.pallas_call(
         scores_kernel, out_shape=sds((2, test_grads.shape[0])), in_specs=[vmem] * 2, out_specs=vmem, name="scores",
         compiler_params=pltpu.CompilerParams(vmem_limit_bytes=12 << 20),
-    )(flat, test_grads)
+    )(flat, tests)
     for bit in (1, 2, 4, 8):
         scores = scores + swap(scores, bit)
     return scores
+
+
+def cube(*args):
+    return cube_body(*args)
 
 
 def shards(
@@ -289,5 +331,7 @@
 
 def solution(mesh):
     placed = (P(None, "tp", "grp"),) * 4 + (P(None, "tp", None),) * 4 + (P(None, "tp"),)
-    body = cube if mesh.shape["tp"] == 16 else shards
-    return jax.shard_map(body, mesh=mesh, in_specs=placed, out_specs=P("grp", None), check_vma=False)
+    cubic = mesh.shape["tp"] == 16
+    return jax.shard_map(
+        cube if cubic else shards, mesh=mesh, in_specs=placed, out_specs=P("grp", None), check_vma=False
+    )

time: 79.4 us -> 73.2 us (0.922)
  waiting for transfers between devices: 39.7 us -> 28.6 us
  starting transfers between devices: 14.3 us -> 19.1 us
    ppermute x14 -> x18, waiting for transfers between devices: 39.7 us -> 28.6 us  [swap(): return lax.ppermute(value, 'tp', [(i, i ^ bit) for i in range(16)])]
    ppermute x14 -> x18, starting transfers between devices: 14.3 us -> 19.1 us  [swap(): return lax.ppermute(value, 'tp', [(i, i ^ bit) for i in range(16)])]
    pallas_call x10 -> x14, Pallas kernels: 24.2 us -> 24.4 us  [the longest x13 23.8 us: call(): pl.pallas_call(kernel, out_shape=outs, in_specs=[smem] + in_specs, out_sp...]
  transfers between devices with their start and end apart: 14 -> 18, of which waited for: 10 -> 11; matrix products, arithmetic and copies ran while one was open for 0% -> 0% of each run, Pallas kernels for 16% -> 22%
where the time goes in v3:
time: 73.2 us; the launch traced here: 73.1 us
  waiting for transfers between devices  28.6 us (39%)
  Pallas kernels  24.4 us (33%)
  starting transfers between devices  19.1 us (26%)
    ppermute x18, waiting for transfers between devices, swap(): return lax.ppermute(value, 'tp', [(i, i ^ bit) for i in range(16)])  28.6 us
    pallas_call x13, Pallas kernels, call(): pl.pallas_call(kernel, out_shape=outs, in_specs=[smem] + in_specs, out_sp...  23.8 us
    ppermute x18, starting transfers between devices, swap(): return lax.ppermute(value, 'tp', [(i, i ^ bit) for i in range(16)])  19.1 us
  transfers between devices with their start and end apart: 18, of which 11 were waited for; matrix products, arithmetic and copies ran while one was open for 0% of the time, Pallas kernels for 22%

profile of v3, /device:TPU:0, one launch (start us, length us, event | category | flops | bytes accessed | tf_op | source)
XLA Modules:
  0.0 73.1 jit_solution(8592888791415516092)
XLA Ops:
  0.0 0.1 pad_add_fusion.where_ref
  0.1 7.0 %shard_map.91 = (f32[2,2,128,768]{3,2,1,0:T(8,128)S(1)}, f32[2,2,128,768]{3,2,1,0:T(8,128)S(1)}, f32[2,2,128,512]{3,2,1,0:T(8,128)S(1)}, bf16[256,1024]{1,0:T(8,...) custom-call(s32[4]{0:T(128)S(1)} %pad_add_fusion.where_ref, ...), custom_call_target="tpu_custom_call" | custom-call | bytes 16777216 | tf_op jit(solution)/shard_map/pallas_call | solution.py:206
  7.0 0.6 collective-permute-start.4
  7.6 0.1 collective-permute-start
  7.7 0.4 collective-permute-start.8
  8.1 5.7 %shard_map.92 = (f32[2,2,128,768]{3,2,1,0:T(8,128)S(1)}, f32[2,2,128,768]{3,2,1,0:T(8,128)S(1)}, f32[2,2,128,512]{3,2,1,0:T(8,128)S(1)}) custom-call(s32[4]{0:T(128)S(1)} %pad_add_fusion.where_ref, bf16[2,256,4096]{2,1,0:T(8,128)(2,1)} %refs_0_.3, bf16[2,256,4096]{2,1,0:T(8,128)(2,1)} %refs_1_.3, bf16[2,256,4096]{2,1,0:T(8,128)(2,1)} %refs_2_.3, ...), custom_call_target="tpu_custom_call" | custom-call | bytes 16777216 | tf_op jit(solution)/shard_map/pallas_call | solution.py:206
  13.8 0.0 collective-permute-done.4.got_ref
  13.8 1.0 %shard_map.97 = (bf16[264,768]{1,0:T(8,128)(2,1)S(1)}, f32[2,1,128,768]{3,2,1,0:T(8,128)S(1)}) custom-call(s32[4]{0:T(128)S(1)} %pad_add_fusion.where_ref, f32[2,2,128,768]{3,2,1,0:T(8,128)S(1)} %get-tuple-element.50.own_ref, f32[2,2,128,768]{3,2,1,0:T(8,128)S(1)} %collective-permute-done.4.got_ref), custom_call_target="tpu_custom_call" | custom-call | bytes 4194304 | tf_op jit(solution)/shard_map/pallas_call | solution.py:206
  14.9 2.7 %collective-permute-start.5 = (bf16[264,768]{1,0:T(8,128)(2,1)S(1)}, bf16[264,768]{1,0:T(8,128)(2,1)S(1)}, u32[]{:S(2)}, u32[]{:S(2)}) collective-permute-start(bf16[264,768]{1,0:T(8,128)(2,1)S(1)} %get-tuple-element.52), channel_id=1, source_target_pairs={{0,4},{1,5},{2,6},{3,7},{4,0},{5,1},{6,2},{7,3},{8,12},{9,13},{10,... | collective-permute-start | bytes 1216520 | tf_op jit(solution)/shard_map/ppermute | solution.py:200
  17.6 1.0 %shard_map.93 = (bf16[520,384]{1,0:T(8,128)(2,1)S(1)}, f32[2,2,128,384]{3,2,1,0:T(8,128)S(1)}) custom-call(s32[4]{0:T(128)S(1)} %pad_add_fusion.where_ref, f32[2,2,128,768]{3,2,1,0:T(8,128)S(1)} %get-tuple-element.41.own_ref, f32[2,2,128,768]{3,2,1,0:T(8,128)S(1)} %collective-permute-done.got_ref), custom_call_target="tpu_custom_call" | custom-call | bytes 4194304 | tf_op jit(solution)/shard_map/pallas_call | solution.py:206
  18.6 1.6 %collective-permute-start.1 = (bf16[520,384]{1,0:T(8,128)(2,1)S(1)}, bf16[520,384]{1,0:T(8,128)(2,1)S(1)}, u32[]{:S(2)}, u32[]{:S(2)}) collective-permute-start(bf16[520,384]{1,0:T(8,128)(2,1)S(1)} %get-tuple-element.43), channel_id=1, source_target_pairs={{0,2},{1,3},{2,0},{3,1},{4,6},{5,7},{6,4},{7,5},{8,10},{9,11},{10,... | collective-permute-start | bytes 1198088 | tf_op jit(solution)/shard_map/ppermute | solution.py:200
  20.2 0.9 %shard_map.100 = (bf16[520,256]{1,0:T(8,128)(2,1)S(1)}, f32[2,2,128,256]{3,2,1,0:T(8,128)S(1)}) custom-call(s32[4]{0:T(128)S(1)} %pad_add_fusion.where_ref, f32[2,2,128,512]{3,2,1,0:T(8,128)S(1)} %get-tuple-element.58.own_ref, f32[2,2,128,512]{3,2,1,0:T(8,128)S(1)} %collective-permute-done.8.got_ref), custom_call_target="tpu_custom_call" | custom-call | bytes 4194304 | tf_op jit(solution)/shard_map/pallas_call | solution.py:206
  21.1 0.6 collective-permute-start.9
  21.6 9.2 %collective-permute-done.1.codes_in = bf16[520,384]{1,0:T(8,128)(2,1)S(1)} collective-permute-done((bf16[520,384]{1,0:T(8,128)(2,1)S(1)}, bf16[520,384]{1,0:T(8,128)(2,1)S(1)}, u32[]{:S(2)}, u32[]{:S(2)}) %collective-permute-start.1) | collective-permute-done | bytes 399392 | tf_op jit(solution)/shard_map/ppermute | solution.py:200
  30.8 1.0 %shard_map.94 = (bf16[264,384]{1,0:T(8,128)(2,1)S(1)}, f32[2,1,128,384]{3,2,1,0:T(8,128)S(1)}) custom-call(s32[4]{0:T(128)S(1)} %pad_add_fusion.where_ref, bf16[520,384]{1,0:T(8,128)(2,1)S(1)} %collective-permute-done.1.codes_in, f32[2,2,128,384]{3,2,1,0:T(8,128)S(1)} %get-tuple-element.44.kept_in), custom_call_target="tpu_custom_call" | custom-call | bytes 4194304 | tf_op jit(solution)/shard_map/pallas_call | solution.py:206
  31.8 0.1 collective-permute-start.2
  31.9 1.1 %shard_map.98 = (bf16[264,384]{1,0:T(8,128)(2,1)S(1)}, f32[2,1,128,384]{3,2,1,0:T(8,128)S(1)}) custom-call(s32[4]{0:T(128)S(1)} %pad_add_fusion.where_ref, bf16[264,768]{1,0:T(8,128)(2,1)S(1)} %collective-permute-done.5.codes_in, f32[2,1,128,768]{3,2,1,0:T(8,128)S(1)} %get-tuple-element.53.kept_in), custom_call_target="tpu_custom_call" | custom-call | bytes 4194304 | tf_op jit(solution)/shard_map/pallas_call | solution.py:206
  32.9 2.0 %collective-permute-start.6 = (bf16[264,384]{1,0:T(8,128)(2,1)S(1)}, bf16[264,384]{1,0:T(8,128)(2,1)S(1)}, u32[]{:S(2)}, u32[]{:S(2)}) collective-permute-start(bf16[264,384]{1,0:T(8,128)(2,1)S(1)} %get-tuple-element.54), channel_id=1, source_target_pairs={{0,2},{1,3},{2,0},{3,1},{4,6},{5,7},{6,4},{7,5},{8,10},{9,11},{10,... | collective-permute-start | bytes 608264 | tf_op jit(solution)/shard_map/ppermute | solution.py:200
  35.0 1.6 %collective-permute-done.9.codes_in = bf16[520,256]{1,0:T(8,128)(2,1)S(1)} collective-permute-done((bf16[520,256]{1,0:T(8,128)(2,1)S(1)}, bf16[520,256]{1,0:T(8,128)(2,1)S(1)}, u32[]{:S(2)}, u32[]{:S(2)}) %collective-permute-start.9) | collective-permute-done | bytes 266272 | tf_op jit(solution)/shard_map/ppermute | solution.py:200
  36.5 0.8 %shard_map.101 = (bf16[264,256]{1,0:T(8,128)(2,1)S(1)}, f32[2,1,128,256]{3,2,1,0:T(8,128)S(1)}) custom-call(s32[4]{0:T(128)S(1)} %pad_add_fusion.where_ref, bf16[520,256]{1,0:T(8,128)(2,1)S(1)} %collective-permute-done.9.codes_in, f32[2,2,128,256]{3,2,1,0:T(8,128)S(1)} %get-tuple-element.61.kept_in), custom_call_target="tpu_custom_call" | custom-call | bytes 4194304 | tf_op jit(solution)/shard_map/pallas_call | solution.py:206
  37.3 0.1 collective-permute-start.10
  37.4 0.2 collective-permute-done.2.codes_in
  37.6 0.8 %shard_map.95 = (bf16[136,384]{1,0:T(8,128)(2,1)S(1)}, f32[1,1,128,384]{3,2,1,0:T(8,128)S(1)}) custom-call(s32[4]{0:T(128)S(1)} %pad_add_fusion.where_ref, bf16[264,384]{1,0:T(8,128)(2,1)S(1)} %collective-permute-done.2.codes_in, f32[2,1,128,384]{3,2,1,0:T(8,128)S(1)} %get-tuple-element.46.kept_in), custom_call_target="tpu_custom_call" | custom-call | bytes 4194304 | tf_op jit(solution)/shard_map/pallas_call | solution.py:206
  38.4 2.6 %collective-permute-start.3 = (bf16[136,384]{1,0:T(8,128)(2,1)S(1)}, bf16[136,384]{1,0:T(8,128)(2,1)S(1)}, u32[]{:S(2)}, u32[]{:S(2)}) collective-permute-start(bf16[136,384]{1,0:T(8,128)(2,1)S(1)} %get-tuple-element.47), channel_id=1, source_target_pairs={{0,8},{1,9},{2,10},{3,11},{4,12},{5,13},{6,14},{7,15},{8,0},{9,1},... | collective-permute-start | bytes 313352 | tf_op jit(solution)/shard_map/ppermute | solution.py:200
  41.0 0.8 %shard_map.99 = (bf16[136,384]{1,0:T(8,128)(2,1)S(1)}, f32[1,1,128,384]{3,2,1,0:T(8,128)S(1)}) custom-call(s32[4]{0:T(128)S(1)} %pad_add_fusion.where_ref, bf16[264,384]{1,0:T(8,128)(2,1)S(1)} %collective-permute-done.6.codes_in, f32[2,1,128,384]{3,2,1,0:T(8,128)S(1)} %get-tuple-element.55.kept_in), custom_call_target="tpu_custom_call" | custom-call | bytes 4194304 | tf_op jit(solution)/shard_map/pallas_call | solution.py:206
  41.8 1.7 %collective-permute-start.7 = (bf16[136,384]{1,0:T(8,128)(2,1)S(1)}, bf16[136,384]{1,0:T(8,128)(2,1)S(1)}, u32[]{:S(2)}, u32[]{:S(2)}) collective-permute-start(bf16[136,384]{1,0:T(8,128)(2,1)S(1)} %get-tuple-element.56), channel_id=1, source_target_pairs={{0,8},{1,9},{2,10},{3,11},{4,12},{5,13},{6,14},{7,15},{8,0},{9,1},... | collective-permute-start | bytes 313352 | tf_op jit(solution)/shard_map/ppermute | solution.py:200
  43.5 0.7 shard_map.102
  44.1 1.7 %collective-permute-start.11 = (bf16[136,256]{1,0:T(8,128)(2,1)S(1)}, bf16[136,256]{1,0:T(8,128)(2,1)S(1)}, u32[]{:S(2)}, u32[]{:S(2)}) collective-permute-start(bf16[136,256]{1,0:T(8,128)(2,1)S(1)} %get-tuple-element.64), channel_id=1, source_target_pairs={{0,8},{1,9},{2,10},{3,11},{4,12},{5,13},{6,14},{7,15},{8,0},{9,1},... | collective-permute-start | bytes 208904 | tf_op jit(solution)/shard_map/ppermute | solution.py:200
  45.8 3.8 %collective-permute-done.3.refs_0_ = bf16[136,384]{1,0:T(8,128)(2,1)S(1)} collective-permute-done((bf16[136,384]{1,0:T(8,128)(2,1)S(1)}, bf16[136,384]{1,0:T(8,128)(2,1)S(1)}, u32[]{:S(2)}, u32[]{:S(2)}) %collective-permute-start.3) | collective-permute-done | bytes 104480 | tf_op jit(solution)/shard_map/ppermute | solution.py:200
  49.6 2.1 %shard_map.96 = (f32[64,64]{1,0:T(8,128)S(1)}, bf16[1024,1024]{1,0:T(8,128)(2,1)S(1)}) custom-call(s32[4]{0:T(128)S(1)} %pad_add_fusion.where_ref, bf16[1024,1024]{1,0:T(8,128)(2,1)} %tests_in.1, bf16[136,384]{1,0:T(8,128)(2,1)S(1)} %collective-permute-done.3.refs_0_, f32[1,1,128,384]{3,2,1,0:T(8,128)S(1)} %get-tuple-element.48.refs_1_), custom_call_target="tpu_custom_call" | custom-call | bytes 4194304 | tf_op jit(solution)/shard_map/pallas_call | solution.py:206
  51.7 1.0 %collective-permute-done.11.refs_2_ = bf16[136,256]{1,0:T(8,128)(2,1)S(1)} collective-permute-done((bf16[136,256]{1,0:T(8,128)(2,1)S(1)}, bf16[136,256]{1,0:T(8,128)(2,1)S(1)}, u32[]{:S(2)}, u32[]{:S(2)}) %collective-permute-start.11) | collective-permute-done | bytes 69664 | tf_op jit(solution)/shard_map/ppermute | solution.py:200
  52.7 0.9 %shard_map.103 = (f32[2,16,64]{2,1,0:T(8,128)S(1)}, f32[2,16,64]{2,1,0:T(8,128)S(1)}) custom-call(s32[4]{0:T(128)S(1)} %pad_add_fusion.where_ref, f32[64,64]{1,0:T(8,128)S(1)} %get-tuple-element.49.early_ref, bf16[136,384]{1,0:T(8,128)(2,1)S(1)} %collective-permute-done.7.refs_0_, f32[1,1,128,384]{3,2,1,0:T(8,128)S(1)} %get-tuple-element.57.refs_1_, ...), custom_call_target="tpu_custom_call" | custom-call | bytes 2097152 | tf_op jit(solution)/shard_map/pallas_call | solution.py:206
  53.7 0.1 collective-permute-start.12
  53.8 1.2 %collective-permute-done.12 = f32[2,16,64]{2,1,0:T(8,128)S(1)} collective-permute-done((f32[2,16,64]{2,1,0:T(8,128)S(1)}, f32[2,16,64]{2,1,0:T(8,128)S(1)}, u32[]{:S(2)}, u32[]{:S(2)}) %collective-permute-start.12) | collective-permute-done | bytes 8224 | tf_op jit(solution)/shard_map/ppermute | solution.py:200
  55.0 1.5 %collective-permute-start.13 = (f32[16,64]{1,0:T(8,128)S(1)}, f32[16,64]{1,0:T(8,128)S(1)}, u32[]{:S(2)}, u32[]{:S(2)}) collective-permute-start(f32[16,64]{1,0:T(8,128)S(1)} %dynamic-slice_bitcast_fusion), channel_id=1, source_target_pairs={{0,2},{1,3},{2,0},{3,1},{4,6},{5,7},{6,4},{7,5},{8,10},{9,11},{10,... | collective-permute-start | bytes 12296 | tf_op jit(solution)/shard_map/ppermute | solution.py:200
  56.5 2.1 %collective-permute-done.13 = f32[16,64]{1,0:T(8,128)S(1)} collective-permute-done((f32[16,64]{1,0:T(8,128)S(1)}, f32[16,64]{1,0:T(8,128)S(1)}, u32[]{:S(2)}, u32[]{:S(2)}) %collective-permute-start.13) | collective-permute-done | bytes 4128 | tf_op jit(solution)/shard_map/ppermute | solution.py:200
  58.6 0.1 stack.29
  58.7 0.1 stack.30
  58.8 0.7 scores.1
  59.4 0.0 collective-permute-start.14
  59.5 1.2 %collective-permute-done.14 = f32[2,1024]{1,0:T(2,128)S(1)} collective-permute-done((f32[2,1024]{1,0:T(2,128)S(1)}, f32[2,1024]{1,0:T(2,128)S(1)}, u32[]{:S(2)}, u32[]{:S(2)}) %collective-permute-start.14) | collective-permute-done | bytes 8224 | tf_op jit(solution)/shard_map/ppermute | solution.py:200
  60.6 1.5 %collective-permute-start.15 = (f32[2,1024]{1,0:T(2,128)S(1)}, f32[2,1024]{1,0:T(2,128)S(1)}, u32[]{:S(2)}, u32[]{:S(2)}) collective-permute-start(f32[2,1024]{1,0:T(2,128)S(1)} %add.42), channel_id=1, source_target_pairs={{0,2},{1,3},{2,0},{3,1},{4,6},{5,7},{6,4},{7,5},{8,10},{9,11},{10,... | collective-permute-start | bytes 24584 | tf_op jit(solution)/shard_map/ppermute | solution.py:200
  62.1 2.1 %collective-permute-done.15 = f32[2,1024]{1,0:T(2,128)S(1)} collective-permute-done((f32[2,1024]{1,0:T(2,128)S(1)}, f32[2,1024]{1,0:T(2,128)S(1)}, u32[]{:S(2)}, u32[]{:S(2)}) %collective-permute-start.15) | collective-permute-done | bytes 8224 | tf_op jit(solution)/shard_map/ppermute | solution.py:200
  64.3 0.3 collective-permute-start.16
  64.6 3.4 %collective-permute-done.16 = f32[2,1024]{1,0:T(2,128)S(1)} collective-permute-done((f32[2,1024]{1,0:T(2,128)S(1)}, f32[2,1024]{1,0:T(2,128)S(1)}, u32[]{:S(2)}, u32[]{:S(2)}) %collective-permute-start.16) | collective-permute-done | bytes 8224 | tf_op jit(solution)/shard_map/ppermute | solution.py:200
  67.9 1.6 %collective-permute-start.17 = (f32[2,1024]{1,0:T(2,128)S(1)}, f32[2,1024]{1,0:T(2,128)S(1)}, u32[]{:S(2)}, u32[]{:S(2)}) collective-permute-start(f32[2,1024]{1,0:T(2,128)S(1)} %add.44), channel_id=1, source_target_pairs={{0,8},{1,9},{2,10},{3,11},{4,12},{5,13},{6,14},{7,15},{8,0},{9,1},... | collective-permute-start | bytes 24584 | tf_op jit(solution)/shard_map/ppermute | solution.py:200
  69.6 2.9 %collective-permute-done.17 = f32[2,1024]{1,0:T(2,128)S(1)} collective-permute-done((f32[2,1024]{1,0:T(2,128)S(1)}, f32[2,1024]{1,0:T(2,128)S(1)}, u32[]{:S(2)}, u32[]{:S(2)}) %collective-permute-start.17) | collective-permute-done | bytes 8224 | tf_op jit(solution)/shard_map/ppermute | solution.py:200
  72.5 0.6 add.45
  (13 shorter events, 0.1 us)
Async XLA Ops:
  7.0 6.8 %collective-permute-start.4 = (f32[2,2,128,768]{3,2,1,0:T(8,128)S(1)}, f32[2,2,128,768]{3,2,1,0:T(8,128)S(1)}, u32[]{:S(2)}, u32[]{:S(2)}) collective-permute-start(f32[2,2,128,768]{3,2,1,0:T(8,128)S(1)} %get-tuple-element.51), channel_id=1, source_target_pairs={{0,1},{1,0},{2,3},{3,2},{4,5},{5,4},{6,7},{7,6},{8,9},{9,8},{10,11... | collective-permute-start | bytes 4718600 | tf_op jit(solution)/shard_map/ppermute | solution.py:200
  7.6 10.0 %collective-permute-start = (f32[2,2,128,768]{3,2,1,0:T(8,128)S(1)}, f32[2,2,128,768]{3,2,1,0:T(8,128)S(1)}, u32[]{:S(2)}, u32[]{:S(2)}) collective-permute-start(f32[2,2,128,768]{3,2,1,0:T(8,128)S(1)} %get-tuple-element.42), channel_id=1, source_target_pairs={{0,1},{1,0},{2,3},{3,2},{4,5},{5,4},{6,7},{7,6},{8,9},{9,8},{10,11... | collective-permute-start | bytes 4718600 | tf_op jit(solution)/shard_map/ppermute | solution.py:200
  7.7 12.5 %collective-permute-start.8 = (f32[2,2,128,512]{3,2,1,0:T(8,128)S(1)}, f32[2,2,128,512]{3,2,1,0:T(8,128)S(1)}, u32[]{:S(2)}, u32[]{:S(2)}) collective-permute-start(f32[2,2,128,512]{3,2,1,0:T(8,128)S(1)} %get-tuple-element.59), channel_id=1, source_target_pairs={{0,1},{1,0},{2,3},{3,2},{4,5},{5,4},{6,7},{7,6},{8,9},{9,8},{10,11... | collective-permute-start | bytes 3145736 | tf_op jit(solution)/shard_map/ppermute | solution.py:200
  14.9 17.0 %collective-permute-start.5 = (bf16[264,768]{1,0:T(8,128)(2,1)S(1)}, bf16[264,768]{1,0:T(8,128)(2,1)S(1)}, u32[]{:S(2)}, u32[]{:S(2)}) collective-permute-start(bf16[264,768]{1,0:T(8,128)(2,1)S(1)} %get-tuple-element.52), channel_id=1, source_target_pairs={{0,4},{1,5},{2,6},{3,7},{4,0},{5,1},{6,2},{7,3},{8,12},{9,13},{10,... | collective-permute-start | bytes 1216520 | tf_op jit(solution)/shard_map/ppermute | solution.py:200
  18.6 12.2 %collective-permute-start.1 = (bf16[520,384]{1,0:T(8,128)(2,1)S(1)}, bf16[520,384]{1,0:T(8,128)(2,1)S(1)}, u32[]{:S(2)}, u32[]{:S(2)}) collective-permute-start(bf16[520,384]{1,0:T(8,128)(2,1)S(1)} %get-tuple-element.43), channel_id=1, source_target_pairs={{0,2},{1,3},{2,0},{3,1},{4,6},{5,7},{6,4},{7,5},{8,10},{9,11},{10,... | collective-permute-start | bytes 1198088 | tf_op jit(solution)/shard_map/ppermute | solution.py:200
  21.1 15.4 %collective-permute-start.9 = (bf16[520,256]{1,0:T(8,128)(2,1)S(1)}, bf16[520,256]{1,0:T(8,128)(2,1)S(1)}, u32[]{:S(2)}, u32[]{:S(2)}) collective-permute-start(bf16[520,256]{1,0:T(8,128)(2,1)S(1)} %get-tuple-element.60), channel_id=1, source_target_pairs={{0,2},{1,3},{2,0},{3,1},{4,6},{5,7},{6,4},{7,5},{8,10},{9,11},{10,... | collective-permute-start | bytes 798728 | tf_op jit(solution)/shard_map/ppermute | solution.py:200
  31.8 5.8 %collective-permute-start.2 = (bf16[264,384]{1,0:T(8,128)(2,1)S(1)}, bf16[264,384]{1,0:T(8,128)(2,1)S(1)}, u32[]{:S(2)}, u32[]{:S(2)}) collective-permute-start(bf16[264,384]{1,0:T(8,128)(2,1)S(1)} %get-tuple-element.45), channel_id=1, source_target_pairs={{0,4},{1,5},{2,6},{3,7},{4,0},{5,1},{6,2},{7,3},{8,12},{9,13},{10,... | collective-permute-start | bytes 608264 | tf_op jit(solution)/shard_map/ppermute | solution.py:200
  32.9 8.1 %collective-permute-start.6 = (bf16[264,384]{1,0:T(8,128)(2,1)S(1)}, bf16[264,384]{1,0:T(8,128)(2,1)S(1)}, u32[]{:S(2)}, u32[]{:S(2)}) collective-permute-start(bf16[264,384]{1,0:T(8,128)(2,1)S(1)} %get-tuple-element.54), channel_id=1, source_target_pairs={{0,2},{1,3},{2,0},{3,1},{4,6},{5,7},{6,4},{7,5},{8,10},{9,11},{10,... | collective-permute-start | bytes 608264 | tf_op jit(solution)/shard_map/ppermute | solution.py:200
  37.3 6.1 %collective-permute-start.10 = (bf16[264,256]{1,0:T(8,128)(2,1)S(1)}, bf16[264,256]{1,0:T(8,128)(2,1)S(1)}, u32[]{:S(2)}, u32[]{:S(2)}) collective-permute-start(bf16[264,256]{1,0:T(8,128)(2,1)S(1)} %get-tuple-element.62), channel_id=1, source_target_pairs={{0,4},{1,5},{2,6},{3,7},{4,0},{5,1},{6,2},{7,3},{8,12},{9,13},{10,... | collective-permute-start | bytes 405512 | tf_op jit(solution)/shard_map/ppermute | solution.py:200
  38.4 11.2 %collective-permute-start.3 = (bf16[136,384]{1,0:T(8,128)(2,1)S(1)}, bf16[136,384]{1,0:T(8,128)(2,1)S(1)}, u32[]{:S(2)}, u32[]{:S(2)}) collective-permute-start(bf16[136,384]{1,0:T(8,128)(2,1)S(1)} %get-tuple-element.47), channel_id=1, source_target_pairs={{0,8},{1,9},{2,10},{3,11},{4,12},{5,13},{6,14},{7,15},{8,0},{9,1},... | collective-permute-start | bytes 313352 | tf_op jit(solution)/shard_map/ppermute | solution.py:200
  41.8 11.0 %collective-permute-start.7 = (bf16[136,384]{1,0:T(8,128)(2,1)S(1)}, bf16[136,384]{1,0:T(8,128)(2,1)S(1)}, u32[]{:S(2)}, u32[]{:S(2)}) collective-permute-start(bf16[136,384]{1,0:T(8,128)(2,1)S(1)} %get-tuple-element.56), channel_id=1, source_target_pairs={{0,8},{1,9},{2,10},{3,11},{4,12},{5,13},{6,14},{7,15},{8,0},{9,1},... | collective-permute-start | bytes 313352 | tf_op jit(solution)/shard_map/ppermute | solution.py:200
  44.1 8.6 %collective-permute-start.11 = (bf16[136,256]{1,0:T(8,128)(2,1)S(1)}, bf16[136,256]{1,0:T(8,128)(2,1)S(1)}, u32[]{:S(2)}, u32[]{:S(2)}) collective-permute-start(bf16[136,256]{1,0:T(8,128)(2,1)S(1)} %get-tuple-element.64), channel_id=1, source_target_pairs={{0,8},{1,9},{2,10},{3,11},{4,12},{5,13},{6,14},{7,15},{8,0},{9,1},... | collective-permute-start | bytes 208904 | tf_op jit(solution)/shard_map/ppermute | solution.py:200
  53.7 1.2 %collective-permute-start.12 = (f32[2,16,64]{2,1,0:T(8,128)S(1)}, f32[2,16,64]{2,1,0:T(8,128)S(1)}, u32[]{:S(2)}, u32[]{:S(2)}) collective-permute-start(f32[2,16,64]{2,1,0:T(8,128)S(1)} %get-tuple-element.67), channel_id=1, source_target_pairs={{0,1},{1,0},{2,3},{3,2},{4,5},{5,4},{6,7},{7,6},{8,9},{9,8},{10,11... | collective-permute-start | bytes 24584 | tf_op jit(solution)/shard_map/ppermute | solution.py:200
  55.0 3.7 %collective-permute-start.13 = (f32[16,64]{1,0:T(8,128)S(1)}, f32[16,64]{1,0:T(8,128)S(1)}, u32[]{:S(2)}, u32[]{:S(2)}) collective-permute-start(f32[16,64]{1,0:T(8,128)S(1)} %dynamic-slice_bitcast_fusion), channel_id=1, source_target_pairs={{0,2},{1,3},{2,0},{3,1},{4,6},{5,7},{6,4},{7,5},{8,10},{9,11},{10,... | collective-permute-start | bytes 12296 | tf_op jit(solution)/shard_map/ppermute | solution.py:200
  59.4 1.2 %collective-permute-start.14 = (f32[2,1024]{1,0:T(2,128)S(1)}, f32[2,1024]{1,0:T(2,128)S(1)}, u32[]{:S(2)}, u32[]{:S(2)}) collective-permute-start(f32[2,1024]{1,0:T(2,128)S(1)} %scores.1), channel_id=1, source_target_pairs={{0,1},{1,0},{2,3},{3,2},{4,5},{5,4},{6,7},{7,6},{8,9},{9,8},{10,11... | collective-permute-start | bytes 24584 | tf_op jit(solution)/shard_map/ppermute | solution.py:200
  60.6 3.7 %collective-permute-start.15 = (f32[2,1024]{1,0:T(2,128)S(1)}, f32[2,1024]{1,0:T(2,128)S(1)}, u32[]{:S(2)}, u32[]{:S(2)}) collective-permute-start(f32[2,1024]{1,0:T(2,128)S(1)} %add.42), channel_id=1, source_target_pairs={{0,2},{1,3},{2,0},{3,1},{4,6},{5,7},{6,4},{7,5},{8,10},{9,11},{10,... | collective-permute-start | bytes 24584 | tf_op jit(solution)/shard_map/ppermute | solution.py:200
  64.3 3.7 %collective-permute-start.16 = (f32[2,1024]{1,0:T(2,128)S(1)}, f32[2,1024]{1,0:T(2,128)S(1)}, u32[]{:S(2)}, u32[]{:S(2)}) collective-permute-start(f32[2,1024]{1,0:T(2,128)S(1)} %add.43), channel_id=1, source_target_pairs={{0,4},{1,5},{2,6},{3,7},{4,0},{5,1},{6,2},{7,3},{8,12},{9,13},{10,... | collective-permute-start | bytes 24584 | tf_op jit(solution)/shard_map/ppermute | solution.py:200
  67.9 4.5 %collective-permute-start.17 = (f32[2,1024]{1,0:T(2,128)S(1)}, f32[2,1024]{1,0:T(2,128)S(1)}, u32[]{:S(2)}, u32[]{:S(2)}) collective-permute-start(f32[2,1024]{1,0:T(2,128)S(1)} %add.44), channel_id=1, source_target_pairs={{0,8},{1,9},{2,10},{3,11},{4,12},{5,13},{6,14},{7,15},{8,0},{9,1},... | collective-permute-start | bytes 24584 | tf_op jit(solution)/shard_map/ppermute | solution.py:200

commit v4 on v3

--- a/solution.py
+++ b/solution.py
@@ -169,13 +169,17 @@
         copy.wait()
 
 
-def join_kernel(dim, where_ref, own_ref, got_ref, codes_ref, kept_ref, scales_ref, total_ref):
-    total_ref[...] = own_ref[...] + got_ref[...]
+def join_kernel(dim, at, where_ref, own_ref, got_ref, codes_ref, kept_ref, scales_ref, total_ref):
+    span, width = own_ref.shape[-1] // 2, total_ref.shape[-1] // 2
+    for s in range(2):
+        lanes = slice(s * span + at, s * span + at + width)
+        total_ref[:, :, :, s * width : (s + 1) * width] = own_ref[:, :, :, lanes] + got_ref[:, :, :, lanes]
     split(dim, total_ref, codes_ref, kept_ref, scales_ref, where_ref)
 
 
 CHUNKS = ((384, 'sml'), (384, 'msl'), (256, 'sml'))
-PLAN = (('send', 0, (0, 1, 2)), ('own', 0, (0, 1, 2)), ('k', 0, 0), ('x', 0, 0), ('k', 1, 0), ('x', 1, 0), ('k', 2, 0), ('x', 2, 0), ('k', 0, 1), ('x', 0, 1), ('k', 1, 1), ('x', 1, 1), ('k', 2, 1), ('x', 2, 1), ('k', 0, 2), ('x', 0, 2), ('k', 1, 2), ('x', 1, 2), ('k', 2, 2), ('x', 2, 2))
+GROUPS = ((0,), (1, 2))
+PLAN = (('send', 0, (0, 1, 2)), ('own', 0, (0, 1, 2)), ('k', 0, 0), ('x', 0, 0), ('k', 1, 0), ('x', 1, 0), ('k', 2, 0), ('x', 2, 0), ('k', 0, 1), ('x', 0, 1), ('k', 1, 1), ('x', 1, 1), ('k', 2, 1), ('x', 2, 1), ('k', 0, 2), ('x', 0, 2), ('k', 2, 2), ('x', 2, 2), ('k', 1, 2), ('x', 1, 2))
 AFTER = 4
 EARLY = 1
 FINISH = tuple(i for kind, i, stage in PLAN if kind == "x" and stage == 2)
@@ -219,7 +223,7 @@
         return (sds((groups * K + scales, kept[3]), BF16), sds(kept)), pltpu.VMEM((scales, kept[3]), F32)
 
     def project(own, chunks, given=(), after=0):
-        widths = [CHUNKS[i][0] for i in chunks]
+        widths = [sum(CHUNKS[i][0] for i in group) for group in GROUPS]
         first = sum(width for width, _ in CHUNKS[: chunks[0]])
         width = sum(widths)
         layers = acts[0].shape[0]
@@ -233,10 +237,13 @@
         )
         return results[: len(widths)], results[len(widths) :]
 
-    def join(own, got, dim):
-        outs, scales = outputs(dim, own.shape)
+    def join(index, own, got, dim):
+        group = next(g for g in GROUPS if index in g)
+        at = sum(CHUNKS[j][0] for j in group if j < index)
+        shape = (*own.shape[:3], 2 * CHUNKS[index][0])
+        outs, scales = outputs(dim, shape)
         return call(
-            functools.partial(join_kernel, dim), (own, got), [vmem] * 2, outs, [scales, pltpu.VMEM(own.shape, F32)],
+            functools.partial(join_kernel, dim, at), (own, got), [vmem] * 2, outs, [scales, pltpu.VMEM(shape, F32)],
             4 << 20, 12,
         )
 
@@ -252,14 +259,15 @@
         kind, i, stage = step
         if kind == "send":
             sent, ready = project(False, stage, (), AFTER)
-            for j, value in zip(stage, sent):
-                got[j] = swap(value, 1)
+            for group, value in zip(GROUPS, sent):
+                value = swap(value, 1)
+                got.update({j: value for j in group})
         elif kind == "own":
             made, _ = project(True, stage, ready)
-            own.update(zip(stage, made))
+            own.update({j: value for group, value in zip(GROUPS, made) for j in group})
             ready = ()
         elif kind == "k" and stage == 0:
-            state[i] = join(own[i], got[i], CHUNKS[i][1][0])
+            state[i] = join(i, own[i], got[i], CHUNKS[i][1][0])
         elif kind == "k":
             state[i] = exchange(*state[i], CHUNKS[i][1][stage])
         else:

time: 73.2 us -> 72.9 us (level)
    ppermute x18 -> x17, starting transfers between devices: 19.1 us -> 18.8 us  [swap(): return lax.ppermute(value, 'tp', [(i, i ^ bit) for i in range(16)])]
    ppermute x18 -> x17, waiting for transfers between devices: 28.6 us -> 28.6 us  [swap(): return lax.ppermute(value, 'tp', [(i, i ^ bit) for i in range(16)])]
  transfers between devices with their start and end apart: 18 -> 17, of which waited for: 11 -> 11; matrix products, arithmetic and copies ran while one was open for 0% -> 0% of each run, Pallas kernels for 22% -> 22%
where the time goes in v4:
time: 72.9 us; the launch traced here: 72.8 us
  waiting for transfers between devices  28.6 us (39%)
  Pallas kernels  24.4 us (33%)
  starting transfers between devices  18.8 us (26%)
    ppermute x17, waiting for transfers between devices, swap(): return lax.ppermute(value, 'tp', [(i, i ^ bit) for i in range(16)])  28.6 us
    pallas_call x13, Pallas kernels, call(): pl.pallas_call(kernel, out_shape=outs, in_specs=[smem] + in_specs, out_sp...  23.7 us
    ppermute x17, starting transfers between devices, swap(): return lax.ppermute(value, 'tp', [(i, i ^ bit) for i in range(16)])  18.8 us
  transfers between devices with their start and end apart: 17, of which 11 were waited for; matrix products, arithmetic and copies ran while one was open for 0% of the time, Pallas kernels for 22%

profile of v4, /device:TPU:0, one launch (start us, length us, event | category | flops | bytes accessed | tf_op | source)
XLA Modules:
  0.0 72.8 jit_solution(18251038020642048173)
XLA Ops:
  0.0 0.1 pad_add_fusion.where_ref
  0.1 7.0 %shard_map.91 = (f32[2,2,128,768]{3,2,1,0:T(8,128)S(1)}, f32[2,2,128,1280]{3,2,1,0:T(8,128)S(1)}, bf16[256,1024]{1,0:T(8,128)(2,1)S(1)}, bf16[256,1024]{1,0:T(8,...) custom-call(s32[4]{0:T(128)S(1)} %pad_add_fusion.where_ref, bf16[2,256,4096]{2,1,0:T(8,128)(2,1)} %refs_0_.3, ...), custom_call_target="tpu_custom_call" | custom-call | bytes 16777216 | tf_op jit(solution)/shard_map/pallas_call | solution.py:210
  7.0 0.6 collective-permute-start.4
  7.6 0.1 collective-permute-start
  7.7 5.7 %shard_map.92 = (f32[2,2,128,768]{3,2,1,0:T(8,128)S(1)}, f32[2,2,128,1280]{3,2,1,0:T(8,128)S(1)}) custom-call(s32[4]{0:T(128)S(1)} %pad_add_fusion.where_ref, bf16[2,256,4096]{2,1,0:T(8,128)(2,1)} %refs_0_.3, bf16[2,256,4096]{2,1,0:T(8,128)(2,1)} %refs_1_.3, bf16[2,256,4096]{2,1,0:T(8,128)(2,1)} %refs_2_.3, bf16[2,896,4096]{2,1,0:T(8,128)(2,1)} %refs_3_.3, ...), custom_call_target="tpu_custom_call" | custom-call | bytes 16777216 | tf_op jit(solution)/shard_map/pallas_call | solution.py:210
  13.4 0.0 collective-permute-done.4.got_ref
  13.4 1.0 %shard_map.100 = (bf16[264,768]{1,0:T(8,128)(2,1)S(1)}, f32[2,1,128,768]{3,2,1,0:T(8,128)S(1)}) custom-call(s32[4]{0:T(128)S(1)} %pad_add_fusion.where_ref, f32[2,2,128,1280]{3,2,1,0:T(8,128)S(1)} %get-tuple-element.48.own_ref, f32[2,2,128,1280]{3,2,1,0:T(8,128)S(1)} %collective-permute-done.4.got_ref), custom_call_target="tpu_custom_call" | custom-call | bytes 4194304 | tf_op jit(solution)/shard_map/pallas_call | solution.py:210
  14.4 3.1 %collective-permute-start.8 = (bf16[264,768]{1,0:T(8,128)(2,1)S(1)}, bf16[264,768]{1,0:T(8,128)(2,1)S(1)}, u32[]{:S(2)}, u32[]{:S(2)}) collective-permute-start(bf16[264,768]{1,0:T(8,128)(2,1)S(1)} %get-tuple-element.56), channel_id=1, source_target_pairs={{0,4},{1,5},{2,6},{3,7},{4,0},{5,1},{6,2},{7,3},{8,12},{9,13},{10,... | collective-permute-start | bytes 1216520 | tf_op jit(solution)/shard_map/ppermute | solution.py:204
  17.5 1.0 %shard_map.93 = (bf16[520,384]{1,0:T(8,128)(2,1)S(1)}, f32[2,2,128,384]{3,2,1,0:T(8,128)S(1)}) custom-call(s32[4]{0:T(128)S(1)} %pad_add_fusion.where_ref, f32[2,2,128,768]{3,2,1,0:T(8,128)S(1)} %get-tuple-element.39.own_ref, f32[2,2,128,768]{3,2,1,0:T(8,128)S(1)} %collective-permute-done.got_ref), custom_call_target="tpu_custom_call" | custom-call | bytes 4194304 | tf_op jit(solution)/shard_map/pallas_call | solution.py:210
  18.5 1.6 %collective-permute-start.1 = (bf16[520,384]{1,0:T(8,128)(2,1)S(1)}, bf16[520,384]{1,0:T(8,128)(2,1)S(1)}, u32[]{:S(2)}, u32[]{:S(2)}) collective-permute-start(bf16[520,384]{1,0:T(8,128)(2,1)S(1)} %get-tuple-element.41), channel_id=1, source_target_pairs={{0,2},{1,3},{2,0},{3,1},{4,6},{5,7},{6,4},{7,5},{8,10},{9,11},{10,... | collective-permute-start | bytes 1198088 | tf_op jit(solution)/shard_map/ppermute | solution.py:204
  20.1 0.9 %shard_map.97 = (bf16[520,256]{1,0:T(8,128)(2,1)S(1)}, f32[2,2,128,256]{3,2,1,0:T(8,128)S(1)}) custom-call(s32[4]{0:T(128)S(1)} %pad_add_fusion.where_ref, f32[2,2,128,1280]{3,2,1,0:T(8,128)S(1)} %get-tuple-element.48.own_ref, f32[2,2,128,1280]{3,2,1,0:T(8,128)S(1)} %collective-permute-done.4.got_ref), custom_call_target="tpu_custom_call" | custom-call | bytes 4194304 | tf_op jit(solution)/shard_map/pallas_call | solution.py:210
  21.0 0.6 collective-permute-start.5
  21.6 9.2 %collective-permute-done.1.codes_in = bf16[520,384]{1,0:T(8,128)(2,1)S(1)} collective-permute-done((bf16[520,384]{1,0:T(8,128)(2,1)S(1)}, bf16[520,384]{1,0:T(8,128)(2,1)S(1)}, u32[]{:S(2)}, u32[]{:S(2)}) %collective-permute-start.1) | collective-permute-done | bytes 399392 | tf_op jit(solution)/shard_map/ppermute | solution.py:204
  30.7 1.0 %shard_map.94 = (bf16[264,384]{1,0:T(8,128)(2,1)S(1)}, f32[2,1,128,384]{3,2,1,0:T(8,128)S(1)}) custom-call(s32[4]{0:T(128)S(1)} %pad_add_fusion.where_ref, bf16[520,384]{1,0:T(8,128)(2,1)S(1)} %collective-permute-done.1.codes_in, f32[2,2,128,384]{3,2,1,0:T(8,128)S(1)} %get-tuple-element.42.kept_in), custom_call_target="tpu_custom_call" | custom-call | bytes 4194304 | tf_op jit(solution)/shard_map/pallas_call | solution.py:210
  31.7 0.1 collective-permute-start.2
  31.8 0.0 collective-permute-done.8.codes_in
  31.8 1.1 %shard_map.101 = (bf16[264,384]{1,0:T(8,128)(2,1)S(1)}, f32[2,1,128,384]{3,2,1,0:T(8,128)S(1)}) custom-call(s32[4]{0:T(128)S(1)} %pad_add_fusion.where_ref, bf16[264,768]{1,0:T(8,128)(2,1)S(1)} %collective-permute-done.8.codes_in, f32[2,1,128,768]{3,2,1,0:T(8,128)S(1)} %get-tuple-element.57.kept_in), custom_call_target="tpu_custom_call" | custom-call | bytes 4194304 | tf_op jit(solution)/shard_map/pallas_call | solution.py:210
  32.9 2.0 %collective-permute-start.9 = (bf16[264,384]{1,0:T(8,128)(2,1)S(1)}, bf16[264,384]{1,0:T(8,128)(2,1)S(1)}, u32[]{:S(2)}, u32[]{:S(2)}) collective-permute-start(bf16[264,384]{1,0:T(8,128)(2,1)S(1)} %get-tuple-element.58), channel_id=1, source_target_pairs={{0,2},{1,3},{2,0},{3,1},{4,6},{5,7},{6,4},{7,5},{8,10},{9,11},{10,... | collective-permute-start | bytes 608264 | tf_op jit(solution)/shard_map/ppermute | solution.py:204
  34.9 1.5 %collective-permute-done.5.codes_in = bf16[520,256]{1,0:T(8,128)(2,1)S(1)} collective-permute-done((bf16[520,256]{1,0:T(8,128)(2,1)S(1)}, bf16[520,256]{1,0:T(8,128)(2,1)S(1)}, u32[]{:S(2)}, u32[]{:S(2)}) %collective-permute-start.5) | collective-permute-done | bytes 266272 | tf_op jit(solution)/shard_map/ppermute | solution.py:204
  36.4 0.8 %shard_map.98 = (bf16[264,256]{1,0:T(8,128)(2,1)S(1)}, f32[2,1,128,256]{3,2,1,0:T(8,128)S(1)}) custom-call(s32[4]{0:T(128)S(1)} %pad_add_fusion.where_ref, bf16[520,256]{1,0:T(8,128)(2,1)S(1)} %collective-permute-done.5.codes_in, f32[2,2,128,256]{3,2,1,0:T(8,128)S(1)} %get-tuple-element.51.kept_in), custom_call_target="tpu_custom_call" | custom-call | bytes 4194304 | tf_op jit(solution)/shard_map/pallas_call | solution.py:210
  37.2 0.1 collective-permute-start.6
  37.3 0.2 collective-permute-done.2.codes_in
  37.5 0.8 %shard_map.95 = (bf16[136,384]{1,0:T(8,128)(2,1)S(1)}, f32[1,1,128,384]{3,2,1,0:T(8,128)S(1)}) custom-call(s32[4]{0:T(128)S(1)} %pad_add_fusion.where_ref, bf16[264,384]{1,0:T(8,128)(2,1)S(1)} %collective-permute-done.2.codes_in, f32[2,1,128,384]{3,2,1,0:T(8,128)S(1)} %get-tuple-element.44.kept_in), custom_call_target="tpu_custom_call" | custom-call | bytes 4194304 | tf_op jit(solution)/shard_map/pallas_call | solution.py:210
  38.3 2.6 %collective-permute-start.3 = (bf16[136,384]{1,0:T(8,128)(2,1)S(1)}, bf16[136,384]{1,0:T(8,128)(2,1)S(1)}, u32[]{:S(2)}, u32[]{:S(2)}) collective-permute-start(bf16[136,384]{1,0:T(8,128)(2,1)S(1)} %get-tuple-element.45), channel_id=1, source_target_pairs={{0,8},{1,9},{2,10},{3,11},{4,12},{5,13},{6,14},{7,15},{8,0},{9,1},... | collective-permute-start | bytes 313352 | tf_op jit(solution)/shard_map/ppermute | solution.py:204
  40.9 0.0 collective-permute-done.9.codes_in
  40.9 0.8 %shard_map.102 = (bf16[136,384]{1,0:T(8,128)(2,1)S(1)}, f32[1,1,128,384]{3,2,1,0:T(8,128)S(1)}) custom-call(s32[4]{0:T(128)S(1)} %pad_add_fusion.where_ref, bf16[264,384]{1,0:T(8,128)(2,1)S(1)} %collective-permute-done.9.codes_in, f32[2,1,128,384]{3,2,1,0:T(8,128)S(1)} %get-tuple-element.59.kept_in), custom_call_target="tpu_custom_call" | custom-call | bytes 4194304 | tf_op jit(solution)/shard_map/pallas_call | solution.py:210
  41.7 1.3 %collective-permute-start.10 = (bf16[136,384]{1,0:T(8,128)(2,1)S(1)}, bf16[136,384]{1,0:T(8,128)(2,1)S(1)}, u32[]{:S(2)}, u32[]{:S(2)}) collective-permute-start(bf16[136,384]{1,0:T(8,128)(2,1)S(1)} %get-tuple-element.60), channel_id=1, source_target_pairs={{0,8},{1,9},{2,10},{3,11},{4,12},{5,13},{6,14},{7,15},{8,0},{9,1},... | collective-permute-start | bytes 313352 | tf_op jit(solution)/shard_map/ppermute | solution.py:204
  43.0 0.7 shard_map.99
  43.7 2.5 %collective-permute-start.7 = (bf16[136,256]{1,0:T(8,128)(2,1)S(1)}, bf16[136,256]{1,0:T(8,128)(2,1)S(1)}, u32[]{:S(2)}, u32[]{:S(2)}) collective-permute-start(bf16[136,256]{1,0:T(8,128)(2,1)S(1)} %get-tuple-element.54), channel_id=1, source_target_pairs={{0,8},{1,9},{2,10},{3,11},{4,12},{5,13},{6,14},{7,15},{8,0},{9,1},... | collective-permute-start | bytes 208904 | tf_op jit(solution)/shard_map/ppermute | solution.py:204
  46.2 3.7 %collective-permute-done.3.refs_0_ = bf16[136,384]{1,0:T(8,128)(2,1)S(1)} collective-permute-done((bf16[136,384]{1,0:T(8,128)(2,1)S(1)}, bf16[136,384]{1,0:T(8,128)(2,1)S(1)}, u32[]{:S(2)}, u32[]{:S(2)}) %collective-permute-start.3) | collective-permute-done | bytes 104480 | tf_op jit(solution)/shard_map/ppermute | solution.py:204
  49.9 2.1 %shard_map.96 = (f32[64,64]{1,0:T(8,128)S(1)}, bf16[1024,1024]{1,0:T(8,128)(2,1)S(1)}) custom-call(s32[4]{0:T(128)S(1)} %pad_add_fusion.where_ref, bf16[1024,1024]{1,0:T(8,128)(2,1)} %tests_in.1, bf16[136,384]{1,0:T(8,128)(2,1)S(1)} %collective-permute-done.3.refs_0_, f32[1,1,128,384]{3,2,1,0:T(8,128)S(1)} %get-tuple-element.46.refs_1_), custom_call_target="tpu_custom_call" | custom-call | bytes 4194304 | tf_op jit(solution)/shard_map/pallas_call | solution.py:210
  52.0 0.4 collective-permute-done.7.refs_0_
  52.5 0.9 %shard_map.103 = (f32[2,16,64]{2,1,0:T(8,128)S(1)}, f32[2,16,64]{2,1,0:T(8,128)S(1)}) custom-call(s32[4]{0:T(128)S(1)} %pad_add_fusion.where_ref, f32[64,64]{1,0:T(8,128)S(1)} %get-tuple-element.47.early_ref, bf16[136,256]{1,0:T(8,128)(2,1)S(1)} %collective-permute-done.7.refs_0_, f32[1,1,128,256]{3,2,1,0:T(8,128)S(1)} %get-tuple-element.55.refs_1_, ...), custom_call_target="tpu_custom_call" | custom-call | bytes 2097152 | tf_op jit(solution)/shard_map/pallas_call | solution.py:210
  53.4 0.1 collective-permute-start.11
  53.5 1.2 %collective-permute-done.11 = f32[2,16,64]{2,1,0:T(8,128)S(1)} collective-permute-done((f32[2,16,64]{2,1,0:T(8,128)S(1)}, f32[2,16,64]{2,1,0:T(8,128)S(1)}, u32[]{:S(2)}, u32[]{:S(2)}) %collective-permute-start.11) | collective-permute-done | bytes 8224 | tf_op jit(solution)/shard_map/ppermute | solution.py:204
  54.7 1.5 %collective-permute-start.12 = (f32[16,64]{1,0:T(8,128)S(1)}, f32[16,64]{1,0:T(8,128)S(1)}, u32[]{:S(2)}, u32[]{:S(2)}) collective-permute-start(f32[16,64]{1,0:T(8,128)S(1)} %dynamic-slice_bitcast_fusion), channel_id=1, source_target_pairs={{0,2},{1,3},{2,0},{3,1},{4,6},{5,7},{6,4},{7,5},{8,10},{9,11},{10,... | collective-permute-start | bytes 12296 | tf_op jit(solution)/shard_map/ppermute | solution.py:204
  56.1 2.2 %collective-permute-done.12 = f32[16,64]{1,0:T(8,128)S(1)} collective-permute-done((f32[16,64]{1,0:T(8,128)S(1)}, f32[16,64]{1,0:T(8,128)S(1)}, u32[]{:S(2)}, u32[]{:S(2)}) %collective-permute-start.12) | collective-permute-done | bytes 4128 | tf_op jit(solution)/shard_map/ppermute | solution.py:204
  58.3 0.1 stack.29
  58.4 0.1 stack.30
  58.5 0.7 scores.1
  59.1 0.0 collective-permute-start.13
  59.2 1.2 %collective-permute-done.13 = f32[2,1024]{1,0:T(2,128)S(1)} collective-permute-done((f32[2,1024]{1,0:T(2,128)S(1)}, f32[2,1024]{1,0:T(2,128)S(1)}, u32[]{:S(2)}, u32[]{:S(2)}) %collective-permute-start.13) | collective-permute-done | bytes 8224 | tf_op jit(solution)/shard_map/ppermute | solution.py:204
  60.3 1.5 %collective-permute-start.14 = (f32[2,1024]{1,0:T(2,128)S(1)}, f32[2,1024]{1,0:T(2,128)S(1)}, u32[]{:S(2)}, u32[]{:S(2)}) collective-permute-start(f32[2,1024]{1,0:T(2,128)S(1)} %add.42), channel_id=1, source_target_pairs={{0,2},{1,3},{2,0},{3,1},{4,6},{5,7},{6,4},{7,5},{8,10},{9,11},{10,... | collective-permute-start | bytes 24584 | tf_op jit(solution)/shard_map/ppermute | solution.py:204
  61.8 2.2 %collective-permute-done.14 = f32[2,1024]{1,0:T(2,128)S(1)} collective-permute-done((f32[2,1024]{1,0:T(2,128)S(1)}, f32[2,1024]{1,0:T(2,128)S(1)}, u32[]{:S(2)}, u32[]{:S(2)}) %collective-permute-start.14) | collective-permute-done | bytes 8224 | tf_op jit(solution)/shard_map/ppermute | solution.py:204
  64.0 3.6 %collective-permute-done.15 = f32[2,1024]{1,0:T(2,128)S(1)} collective-permute-done((f32[2,1024]{1,0:T(2,128)S(1)}, f32[2,1024]{1,0:T(2,128)S(1)}, u32[]{:S(2)}, u32[]{:S(2)}) %collective-permute-start.15) | collective-permute-done | bytes 8224 | tf_op jit(solution)/shard_map/ppermute | solution.py:204
  67.7 1.3 %collective-permute-start.16 = (f32[2,1024]{1,0:T(2,128)S(1)}, f32[2,1024]{1,0:T(2,128)S(1)}, u32[]{:S(2)}, u32[]{:S(2)}) collective-permute-start(f32[2,1024]{1,0:T(2,128)S(1)} %add.44), channel_id=1, source_target_pairs={{0,8},{1,9},{2,10},{3,11},{4,12},{5,13},{6,14},{7,15},{8,0},{9,1},... | collective-permute-start | bytes 24584 | tf_op jit(solution)/shard_map/ppermute | solution.py:204
  68.9 3.3 %collective-permute-done.16 = f32[2,1024]{1,0:T(2,128)S(1)} collective-permute-done((f32[2,1024]{1,0:T(2,128)S(1)}, f32[2,1024]{1,0:T(2,128)S(1)}, u32[]{:S(2)}, u32[]{:S(2)}) %collective-permute-start.16) | collective-permute-done | bytes 8224 | tf_op jit(solution)/shard_map/ppermute | solution.py:204
  72.2 0.6 add.45
  (11 shorter events, 0.1 us)
Async XLA Ops:
  7.0 6.3 %collective-permute-start.4 = (f32[2,2,128,1280]{3,2,1,0:T(8,128)S(1)}, f32[2,2,128,1280]{3,2,1,0:T(8,128)S(1)}, u32[]{:S(2)}, u32[]{:S(2)}) collective-permute-start(f32[2,2,128,1280]{3,2,1,0:T(8,128)S(1)} %get-tuple-element.49), channel_id=1, source_target_pairs={{0,1},{1,0},{2,3},{3,2},{4,5},{5,4},{6,7},{7,6},{8,9},{9,8},{10,11... | collective-permute-start | bytes 7864328 | tf_op jit(solution)/shard_map/ppermute | solution.py:204
  7.6 9.9 %collective-permute-start = (f32[2,2,128,768]{3,2,1,0:T(8,128)S(1)}, f32[2,2,128,768]{3,2,1,0:T(8,128)S(1)}, u32[]{:S(2)}, u32[]{:S(2)}) collective-permute-start(f32[2,2,128,768]{3,2,1,0:T(8,128)S(1)} %get-tuple-element.40), channel_id=1, source_target_pairs={{0,1},{1,0},{2,3},{3,2},{4,5},{5,4},{6,7},{7,6},{8,9},{9,8},{10,11... | collective-permute-start | bytes 4718600 | tf_op jit(solution)/shard_map/ppermute | solution.py:204
  14.4 17.4 %collective-permute-start.8 = (bf16[264,768]{1,0:T(8,128)(2,1)S(1)}, bf16[264,768]{1,0:T(8,128)(2,1)S(1)}, u32[]{:S(2)}, u32[]{:S(2)}) collective-permute-start(bf16[264,768]{1,0:T(8,128)(2,1)S(1)} %get-tuple-element.56), channel_id=1, source_target_pairs={{0,4},{1,5},{2,6},{3,7},{4,0},{5,1},{6,2},{7,3},{8,12},{9,13},{10,... | collective-permute-start | bytes 1216520 | tf_op jit(solution)/shard_map/ppermute | solution.py:204
  18.5 12.2 %collective-permute-start.1 = (bf16[520,384]{1,0:T(8,128)(2,1)S(1)}, bf16[520,384]{1,0:T(8,128)(2,1)S(1)}, u32[]{:S(2)}, u32[]{:S(2)}) collective-permute-start(bf16[520,384]{1,0:T(8,128)(2,1)S(1)} %get-tuple-element.41), channel_id=1, source_target_pairs={{0,2},{1,3},{2,0},{3,1},{4,6},{5,7},{6,4},{7,5},{8,10},{9,11},{10,... | collective-permute-start | bytes 1198088 | tf_op jit(solution)/shard_map/ppermute | solution.py:204
  21.0 15.5 %collective-permute-start.5 = (bf16[520,256]{1,0:T(8,128)(2,1)S(1)}, bf16[520,256]{1,0:T(8,128)(2,1)S(1)}, u32[]{:S(2)}, u32[]{:S(2)}) collective-permute-start(bf16[520,256]{1,0:T(8,128)(2,1)S(1)} %get-tuple-element.50), channel_id=1, source_target_pairs={{0,2},{1,3},{2,0},{3,1},{4,6},{5,7},{6,4},{7,5},{8,10},{9,11},{10,... | collective-permute-start | bytes 798728 | tf_op jit(solution)/shard_map/ppermute | solution.py:204
  31.7 5.8 %collective-permute-start.2 = (bf16[264,384]{1,0:T(8,128)(2,1)S(1)}, bf16[264,384]{1,0:T(8,128)(2,1)S(1)}, u32[]{:S(2)}, u32[]{:S(2)}) collective-permute-start(bf16[264,384]{1,0:T(8,128)(2,1)S(1)} %get-tuple-element.43), channel_id=1, source_target_pairs={{0,4},{1,5},{2,6},{3,7},{4,0},{5,1},{6,2},{7,3},{8,12},{9,13},{10,... | collective-permute-start | bytes 608264 | tf_op jit(solution)/shard_map/ppermute | solution.py:204
  32.9 8.1 %collective-permute-start.9 = (bf16[264,384]{1,0:T(8,128)(2,1)S(1)}, bf16[264,384]{1,0:T(8,128)(2,1)S(1)}, u32[]{:S(2)}, u32[]{:S(2)}) collective-permute-start(bf16[264,384]{1,0:T(8,128)(2,1)S(1)} %get-tuple-element.58), channel_id=1, source_target_pairs={{0,2},{1,3},{2,0},{3,1},{4,6},{5,7},{6,4},{7,5},{8,10},{9,11},{10,... | collective-permute-start | bytes 608264 | tf_op jit(solution)/shard_map/ppermute | solution.py:204
  37.2 5.8 %collective-permute-start.6 = (bf16[264,256]{1,0:T(8,128)(2,1)S(1)}, bf16[264,256]{1,0:T(8,128)(2,1)S(1)}, u32[]{:S(2)}, u32[]{:S(2)}) collective-permute-start(bf16[264,256]{1,0:T(8,128)(2,1)S(1)} %get-tuple-element.52), channel_id=1, source_target_pairs={{0,4},{1,5},{2,6},{3,7},{4,0},{5,1},{6,2},{7,3},{8,12},{9,13},{10,... | collective-permute-start | bytes 405512 | tf_op jit(solution)/shard_map/ppermute | solution.py:204
  38.3 11.6 %collective-permute-start.3 = (bf16[136,384]{1,0:T(8,128)(2,1)S(1)}, bf16[136,384]{1,0:T(8,128)(2,1)S(1)}, u32[]{:S(2)}, u32[]{:S(2)}) collective-permute-start(bf16[136,384]{1,0:T(8,128)(2,1)S(1)} %get-tuple-element.45), channel_id=1, source_target_pairs={{0,8},{1,9},{2,10},{3,11},{4,12},{5,13},{6,14},{7,15},{8,0},{9,1},... | collective-permute-start | bytes 313352 | tf_op jit(solution)/shard_map/ppermute | solution.py:204
  41.7 10.8 %collective-permute-start.10 = (bf16[136,384]{1,0:T(8,128)(2,1)S(1)}, bf16[136,384]{1,0:T(8,128)(2,1)S(1)}, u32[]{:S(2)}, u32[]{:S(2)}) collective-permute-start(bf16[136,384]{1,0:T(8,128)(2,1)S(1)} %get-tuple-element.60), channel_id=1, source_target_pairs={{0,8},{1,9},{2,10},{3,11},{4,12},{5,13},{6,14},{7,15},{8,0},{9,1},... | collective-permute-start | bytes 313352 | tf_op jit(solution)/shard_map/ppermute | solution.py:204
  43.7 8.8 %collective-permute-start.7 = (bf16[136,256]{1,0:T(8,128)(2,1)S(1)}, bf16[136,256]{1,0:T(8,128)(2,1)S(1)}, u32[]{:S(2)}, u32[]{:S(2)}) collective-permute-start(bf16[136,256]{1,0:T(8,128)(2,1)S(1)} %get-tuple-element.54), channel_id=1, source_target_pairs={{0,8},{1,9},{2,10},{3,11},{4,12},{5,13},{6,14},{7,15},{8,0},{9,1},... | collective-permute-start | bytes 208904 | tf_op jit(solution)/shard_map/ppermute | solution.py:204
  53.4 1.2 %collective-permute-start.11 = (f32[2,16,64]{2,1,0:T(8,128)S(1)}, f32[2,16,64]{2,1,0:T(8,128)S(1)}, u32[]{:S(2)}, u32[]{:S(2)}) collective-permute-start(f32[2,16,64]{2,1,0:T(8,128)S(1)} %get-tuple-element.63), channel_id=1, source_target_pairs={{0,1},{1,0},{2,3},{3,2},{4,5},{5,4},{6,7},{7,6},{8,9},{9,8},{10,11... | collective-permute-start | bytes 24584 | tf_op jit(solution)/shard_map/ppermute | solution.py:204
  54.7 3.7 %collective-permute-start.12 = (f32[16,64]{1,0:T(8,128)S(1)}, f32[16,64]{1,0:T(8,128)S(1)}, u32[]{:S(2)}, u32[]{:S(2)}) collective-permute-start(f32[16,64]{1,0:T(8,128)S(1)} %dynamic-slice_bitcast_fusion), channel_id=1, source_target_pairs={{0,2},{1,3},{2,0},{3,1},{4,6},{5,7},{6,4},{7,5},{8,10},{9,11},{10,... | collective-permute-start | bytes 12296 | tf_op jit(solution)/shard_map/ppermute | solution.py:204
  59.1 1.2 %collective-permute-start.13 = (f32[2,1024]{1,0:T(2,128)S(1)}, f32[2,1024]{1,0:T(2,128)S(1)}, u32[]{:S(2)}, u32[]{:S(2)}) collective-permute-start(f32[2,1024]{1,0:T(2,128)S(1)} %scores.1), channel_id=1, source_target_pairs={{0,1},{1,0},{2,3},{3,2},{4,5},{5,4},{6,7},{7,6},{8,9},{9,8},{10,11... | collective-permute-start | bytes 24584 | tf_op jit(solution)/shard_map/ppermute | solution.py:204
  60.3 3.7 %collective-permute-start.14 = (f32[2,1024]{1,0:T(2,128)S(1)}, f32[2,1024]{1,0:T(2,128)S(1)}, u32[]{:S(2)}, u32[]{:S(2)}) collective-permute-start(f32[2,1024]{1,0:T(2,128)S(1)} %add.42), channel_id=1, source_target_pairs={{0,2},{1,3},{2,0},{3,1},{4,6},{5,7},{6,4},{7,5},{8,10},{9,11},{10,... | collective-permute-start | bytes 24584 | tf_op jit(solution)/shard_map/ppermute | solution.py:204
  64.0 3.7 %collective-permute-start.15 = (f32[2,1024]{1,0:T(2,128)S(1)}, f32[2,1024]{1,0:T(2,128)S(1)}, u32[]{:S(2)}, u32[]{:S(2)}) collective-permute-start(f32[2,1024]{1,0:T(2,128)S(1)} %add.43), channel_id=1, source_target_pairs={{0,4},{1,5},{2,6},{3,7},{4,0},{5,1},{6,2},{7,3},{8,12},{9,13},{10,... | collective-permute-start | bytes 24584 | tf_op jit(solution)/shard_map/ppermute | solution.py:204
  67.7 4.5 %collective-permute-start.16 = (f32[2,1024]{1,0:T(2,128)S(1)}, f32[2,1024]{1,0:T(2,128)S(1)}, u32[]{:S(2)}, u32[]{:S(2)}) collective-permute-start(f32[2,1024]{1,0:T(2,128)S(1)} %add.44), channel_id=1, source_target_pairs={{0,8},{1,9},{2,10},{3,11},{4,12},{5,13},{6,14},{7,15},{8,0},{9,1},... | collective-permute-start | bytes 24584 | tf_op jit(solution)/shard_map/ppermute | solution.py:204

commit v5 on v4

--- a/solution.py
+++ b/solution.py
@@ -169,18 +169,42 @@
         copy.wait()
 
 
-def join_kernel(dim, at, where_ref, own_ref, got_ref, codes_ref, kept_ref, scales_ref, total_ref):
-    span, width = own_ref.shape[-1] // 2, total_ref.shape[-1] // 2
-    for s in range(2):
-        lanes = slice(s * span + at, s * span + at + width)
-        total_ref[:, :, :, s * width : (s + 1) * width] = own_ref[:, :, :, lanes] + got_ref[:, :, :, lanes]
-    split(dim, total_ref, codes_ref, kept_ref, scales_ref, where_ref)
+def join_kernel(dim, at, width, where_ref, own_ref, got_ref, codes_ref, kept_ref, scales_ref):
+    span = own_ref.shape[-1] // 2
+    layers, modules = own_ref.shape[:2]
+    scales_ref[...] = jnp.zeros_like(scales_ref)
+
+    def total(l, m, w, lanes):
+        rows = slice(w * K, w * K + K)
+        return own_ref[l, m, rows, lanes] + got_ref[l, m, rows, lanes]
+
+    if dim == "s":
+        mine = where_ref[1]
+        leave = pl.ds(pl.multiple_of((1 - mine) * span + at, 128), width)
+        stay = pl.ds(pl.multiple_of(mine * span + at, 128), width)
+        groups = [(l, m, w) for l in range(layers) for m in range(modules) for w in range(2)]
+        for index, (l, m, w) in enumerate(groups):
+            encode(total(l, m, w, leave), codes_ref, index * K, scales_ref, index)
+        for l, m, w in groups:
+            kept_ref[l, m, w * K : w * K + K, :] = total(l, m, w, stay)
+    else:
+        mine = where_ref[2]
+        for s in range(2):
+            lanes, place = slice(s * span + at, s * span + at + width), slice(s * width, (s + 1) * width)
+            for l in range(layers):
+                for w in range(2):
+                    index = l * 2 + w
+                    encode(
+                        total(l, 1 - mine, w, lanes), codes_ref.at[:, place], index * K, scales_ref.at[:, place], index
+                    )
+                    kept_ref[l, 0, w * K : w * K + K, place] = total(l, mine, w, lanes)
+    codes_ref[codes_ref.shape[0] - scales_ref.shape[0] :, :] = scales_ref[...].astype(BF16)
 
 
 CHUNKS = ((384, 'sml'), (384, 'msl'), (256, 'sml'))
 GROUPS = ((0,), (1, 2))
 PLAN = (('send', 0, (0, 1, 2)), ('own', 0, (0, 1, 2)), ('k', 0, 0), ('x', 0, 0), ('k', 1, 0), ('x', 1, 0), ('k', 2, 0), ('x', 2, 0), ('k', 0, 1), ('x', 0, 1), ('k', 1, 1), ('x', 1, 1), ('k', 2, 1), ('x', 2, 1), ('k', 0, 2), ('x', 0, 2), ('k', 2, 2), ('x', 2, 2), ('k', 1, 2), ('x', 1, 2))
-AFTER = 4
+AFTER = 5
 EARLY = 1
 FINISH = tuple(i for kind, i, stage in PLAN if kind == "x" and stage == 2)
 BITS = {"s": 2, "m": 4, "l": 8}
@@ -243,7 +267,7 @@
         shape = (*own.shape[:3], 2 * CHUNKS[index][0])
         outs, scales = outputs(dim, shape)
         return call(
-            functools.partial(join_kernel, dim, at), (own, got), [vmem] * 2, outs, [scales, pltpu.VMEM(shape, F32)],
+            functools.partial(join_kernel, dim, at, CHUNKS[index][0]), (own, got), [vmem] * 2, outs, [scales],
             4 << 20, 12,
         )
 

time: 72.9 us -> 72.7 us (level)
  transfers between devices with their start and end apart: 17 -> 17, of which waited for: 11 -> 11; matrix products, arithmetic and copies ran while one was open for 0% -> 0% of each run, Pallas kernels for 22% -> 21%
where the time goes in v5:
time: 72.7 us; the launch traced here: 72.6 us
  waiting for transfers between devices  28.6 us (39%)
  Pallas kernels  24.1 us (33%)
  starting transfers between devices  18.8 us (26%)
    ppermute x17, waiting for transfers between devices, swap(): return lax.ppermute(value, 'tp', [(i, i ^ bit) for i in range(16)])  28.6 us
    pallas_call x13, Pallas kernels, call(): pl.pallas_call(kernel, out_shape=outs, in_specs=[smem] + in_specs, out_sp...  23.4 us
    ppermute x17, starting transfers between devices, swap(): return lax.ppermute(value, 'tp', [(i, i ^ bit) for i in range(16)])  18.8 us
  transfers between devices with their start and end apart: 17, of which 11 were waited for; matrix products, arithmetic and copies ran while one was open for 0% of the time, Pallas kernels for 21%

profile of v5, /device:TPU:0, one launch (start us, length us, event | category | flops | bytes accessed | tf_op | source)
XLA Modules:
  0.0 72.6 jit_solution(15187279523622422438)
XLA Ops:
  0.0 0.1 pad_add_fusion.where_ref
  0.1 7.0 %shard_map.91 = (f32[2,2,128,768]{3,2,1,0:T(8,128)S(1)}, f32[2,2,128,1280]{3,2,1,0:T(8,128)S(1)}, bf16[256,1024]{1,0:T(8,128)(2,1)S(1)}, bf16[256,1024]{1,0:T(8,...) custom-call(s32[4]{0:T(128)S(1)} %pad_add_fusion.where_ref, ...), custom_call_target="tpu_custom_call" | custom-call | bytes 16777216 | tf_op jit(solution)/shard_map/pallas_call | solution.py:234
  7.1 0.6 collective-permute-start.4
  7.7 0.1 collective-permute-start
  7.7 5.6 %shard_map.92 = (f32[2,2,128,768]{3,2,1,0:T(8,128)S(1)}, f32[2,2,128,1280]{3,2,1,0:T(8,128)S(1)}) custom-call(s32[4]{0:T(128)S(1)} %pad_add_fusion.where_ref, bf16[2,256,4096]{2,1,0:T(8,128)(2,1)} %refs_0_.3, bf16[2,256,4096]{2,1,0:T(8,128)(2,1)} %refs_1_.3, bf16[2,256,4096]{2,1,0:T(8,128)(2,1)} %refs_2_.3, bf16[2,896,4096]{2,1,0:T(8,128)(2,1)} %refs_3_.3, ...), custom_call_target="tpu_custom_call" | custom-call | bytes 16777216 | tf_op jit(solution)/shard_map/pallas_call | solution.py:234
  13.3 0.0 collective-permute-done.4.got_ref
  13.3 0.9 %shard_map.100 = (bf16[264,768]{1,0:T(8,128)(2,1)S(1)}, f32[2,1,128,768]{3,2,1,0:T(8,128)S(1)}) custom-call(s32[4]{0:T(128)S(1)} %pad_add_fusion.where_ref, f32[2,2,128,1280]{3,2,1,0:T(8,128)S(1)} %get-tuple-element.50.own_ref, f32[2,2,128,1280]{3,2,1,0:T(8,128)S(1)} %collective-permute-done.4.got_ref), custom_call_target="tpu_custom_call" | custom-call | bytes 4194304 | tf_op jit(solution)/shard_map/pallas_call | solution.py:234
  14.3 3.1 %collective-permute-start.8 = (bf16[264,768]{1,0:T(8,128)(2,1)S(1)}, bf16[264,768]{1,0:T(8,128)(2,1)S(1)}, u32[]{:S(2)}, u32[]{:S(2)}) collective-permute-start(bf16[264,768]{1,0:T(8,128)(2,1)S(1)} %get-tuple-element.58), channel_id=1, source_target_pairs={{0,4},{1,5},{2,6},{3,7},{4,0},{5,1},{6,2},{7,3},{8,12},{9,13},{10,... | collective-permute-start | bytes 1216520 | tf_op jit(solution)/shard_map/ppermute | solution.py:228
  17.3 0.0 collective-permute-done.got_ref
  17.3 0.9 %shard_map.93 = (bf16[520,384]{1,0:T(8,128)(2,1)S(1)}, f32[2,2,128,384]{3,2,1,0:T(8,128)S(1)}) custom-call(s32[4]{0:T(128)S(1)} %pad_add_fusion.where_ref, f32[2,2,128,768]{3,2,1,0:T(8,128)S(1)} %get-tuple-element.41.own_ref, f32[2,2,128,768]{3,2,1,0:T(8,128)S(1)} %collective-permute-done.got_ref), custom_call_target="tpu_custom_call" | custom-call | bytes 4194304 | tf_op jit(solution)/shard_map/pallas_call | solution.py:234
  18.3 1.6 %collective-permute-start.1 = (bf16[520,384]{1,0:T(8,128)(2,1)S(1)}, bf16[520,384]{1,0:T(8,128)(2,1)S(1)}, u32[]{:S(2)}, u32[]{:S(2)}) collective-permute-start(bf16[520,384]{1,0:T(8,128)(2,1)S(1)} %get-tuple-element.43), channel_id=1, source_target_pairs={{0,2},{1,3},{2,0},{3,1},{4,6},{5,7},{6,4},{7,5},{8,10},{9,11},{10,... | collective-permute-start | bytes 1198088 | tf_op jit(solution)/shard_map/ppermute | solution.py:228
  19.9 0.8 %shard_map.97 = (bf16[520,256]{1,0:T(8,128)(2,1)S(1)}, f32[2,2,128,256]{3,2,1,0:T(8,128)S(1)}) custom-call(s32[4]{0:T(128)S(1)} %pad_add_fusion.where_ref, f32[2,2,128,1280]{3,2,1,0:T(8,128)S(1)} %get-tuple-element.50.own_ref, f32[2,2,128,1280]{3,2,1,0:T(8,128)S(1)} %collective-permute-done.4.got_ref), custom_call_target="tpu_custom_call" | custom-call | bytes 4194304 | tf_op jit(solution)/shard_map/pallas_call | solution.py:234
  20.7 0.6 collective-permute-start.5
  21.2 9.2 %collective-permute-done.1.codes_in = bf16[520,384]{1,0:T(8,128)(2,1)S(1)} collective-permute-done((bf16[520,384]{1,0:T(8,128)(2,1)S(1)}, bf16[520,384]{1,0:T(8,128)(2,1)S(1)}, u32[]{:S(2)}, u32[]{:S(2)}) %collective-permute-start.1) | collective-permute-done | bytes 399392 | tf_op jit(solution)/shard_map/ppermute | solution.py:228
  30.5 1.0 %shard_map.94 = (bf16[264,384]{1,0:T(8,128)(2,1)S(1)}, f32[2,1,128,384]{3,2,1,0:T(8,128)S(1)}) custom-call(s32[4]{0:T(128)S(1)} %pad_add_fusion.where_ref, bf16[520,384]{1,0:T(8,128)(2,1)S(1)} %collective-permute-done.1.codes_in, f32[2,2,128,384]{3,2,1,0:T(8,128)S(1)} %get-tuple-element.44.kept_in), custom_call_target="tpu_custom_call" | custom-call | bytes 4194304 | tf_op jit(solution)/shard_map/pallas_call | solution.py:234
  31.5 0.1 collective-permute-start.2
  31.6 1.1 %shard_map.101 = (bf16[264,384]{1,0:T(8,128)(2,1)S(1)}, f32[2,1,128,384]{3,2,1,0:T(8,128)S(1)}) custom-call(s32[4]{0:T(128)S(1)} %pad_add_fusion.where_ref, bf16[264,768]{1,0:T(8,128)(2,1)S(1)} %collective-permute-done.8.codes_in, f32[2,1,128,768]{3,2,1,0:T(8,128)S(1)} %get-tuple-element.59.kept_in), custom_call_target="tpu_custom_call" | custom-call | bytes 4194304 | tf_op jit(solution)/shard_map/pallas_call | solution.py:234
  32.6 2.0 %collective-permute-start.9 = (bf16[264,384]{1,0:T(8,128)(2,1)S(1)}, bf16[264,384]{1,0:T(8,128)(2,1)S(1)}, u32[]{:S(2)}, u32[]{:S(2)}) collective-permute-start(bf16[264,384]{1,0:T(8,128)(2,1)S(1)} %get-tuple-element.60), channel_id=1, source_target_pairs={{0,2},{1,3},{2,0},{3,1},{4,6},{5,7},{6,4},{7,5},{8,10},{9,11},{10,... | collective-permute-start | bytes 608264 | tf_op jit(solution)/shard_map/ppermute | solution.py:228
  34.6 1.5 %collective-permute-done.5.codes_in = bf16[520,256]{1,0:T(8,128)(2,1)S(1)} collective-permute-done((bf16[520,256]{1,0:T(8,128)(2,1)S(1)}, bf16[520,256]{1,0:T(8,128)(2,1)S(1)}, u32[]{:S(2)}, u32[]{:S(2)}) %collective-permute-start.5) | collective-permute-done | bytes 266272 | tf_op jit(solution)/shard_map/ppermute | solution.py:228
  36.2 0.8 %shard_map.98 = (bf16[264,256]{1,0:T(8,128)(2,1)S(1)}, f32[2,1,128,256]{3,2,1,0:T(8,128)S(1)}) custom-call(s32[4]{0:T(128)S(1)} %pad_add_fusion.where_ref, bf16[520,256]{1,0:T(8,128)(2,1)S(1)} %collective-permute-done.5.codes_in, f32[2,2,128,256]{3,2,1,0:T(8,128)S(1)} %get-tuple-element.53.kept_in), custom_call_target="tpu_custom_call" | custom-call | bytes 4194304 | tf_op jit(solution)/shard_map/pallas_call | solution.py:234
  37.0 0.1 collective-permute-start.6
  37.1 0.2 collective-permute-done.2.codes_in
  37.3 0.8 %shard_map.95 = (bf16[136,384]{1,0:T(8,128)(2,1)S(1)}, f32[1,1,128,384]{3,2,1,0:T(8,128)S(1)}) custom-call(s32[4]{0:T(128)S(1)} %pad_add_fusion.where_ref, bf16[264,384]{1,0:T(8,128)(2,1)S(1)} %collective-permute-done.2.codes_in, f32[2,1,128,384]{3,2,1,0:T(8,128)S(1)} %get-tuple-element.46.kept_in), custom_call_target="tpu_custom_call" | custom-call | bytes 4194304 | tf_op jit(solution)/shard_map/pallas_call | solution.py:234
  38.0 2.7 %collective-permute-start.3 = (bf16[136,384]{1,0:T(8,128)(2,1)S(1)}, bf16[136,384]{1,0:T(8,128)(2,1)S(1)}, u32[]{:S(2)}, u32[]{:S(2)}) collective-permute-start(bf16[136,384]{1,0:T(8,128)(2,1)S(1)} %get-tuple-element.47), channel_id=1, source_target_pairs={{0,8},{1,9},{2,10},{3,11},{4,12},{5,13},{6,14},{7,15},{8,0},{9,1},... | collective-permute-start | bytes 313352 | tf_op jit(solution)/shard_map/ppermute | solution.py:228
  40.7 0.8 %shard_map.102 = (bf16[136,384]{1,0:T(8,128)(2,1)S(1)}, f32[1,1,128,384]{3,2,1,0:T(8,128)S(1)}) custom-call(s32[4]{0:T(128)S(1)} %pad_add_fusion.where_ref, bf16[264,384]{1,0:T(8,128)(2,1)S(1)} %collective-permute-done.9.codes_in, f32[2,1,128,384]{3,2,1,0:T(8,128)S(1)} %get-tuple-element.61.kept_in), custom_call_target="tpu_custom_call" | custom-call | bytes 4194304 | tf_op jit(solution)/shard_map/pallas_call | solution.py:234
  41.5 1.3 %collective-permute-start.10 = (bf16[136,384]{1,0:T(8,128)(2,1)S(1)}, bf16[136,384]{1,0:T(8,128)(2,1)S(1)}, u32[]{:S(2)}, u32[]{:S(2)}) collective-permute-start(bf16[136,384]{1,0:T(8,128)(2,1)S(1)} %get-tuple-element.62), channel_id=1, source_target_pairs={{0,8},{1,9},{2,10},{3,11},{4,12},{5,13},{6,14},{7,15},{8,0},{9,1},... | collective-permute-start | bytes 313352 | tf_op jit(solution)/shard_map/ppermute | solution.py:228
  42.8 0.7 shard_map.99
  43.5 2.5 %collective-permute-start.7 = (bf16[136,256]{1,0:T(8,128)(2,1)S(1)}, bf16[136,256]{1,0:T(8,128)(2,1)S(1)}, u32[]{:S(2)}, u32[]{:S(2)}) collective-permute-start(bf16[136,256]{1,0:T(8,128)(2,1)S(1)} %get-tuple-element.56), channel_id=1, source_target_pairs={{0,8},{1,9},{2,10},{3,11},{4,12},{5,13},{6,14},{7,15},{8,0},{9,1},... | collective-permute-start | bytes 208904 | tf_op jit(solution)/shard_map/ppermute | solution.py:228
  46.0 3.6 %collective-permute-done.3.refs_0_ = bf16[136,384]{1,0:T(8,128)(2,1)S(1)} collective-permute-done((bf16[136,384]{1,0:T(8,128)(2,1)S(1)}, bf16[136,384]{1,0:T(8,128)(2,1)S(1)}, u32[]{:S(2)}, u32[]{:S(2)}) %collective-permute-start.3) | collective-permute-done | bytes 104480 | tf_op jit(solution)/shard_map/ppermute | solution.py:228
  49.6 2.1 %shard_map.96 = (f32[64,64]{1,0:T(8,128)S(1)}, bf16[1024,1024]{1,0:T(8,128)(2,1)S(1)}) custom-call(s32[4]{0:T(128)S(1)} %pad_add_fusion.where_ref, bf16[1024,1024]{1,0:T(8,128)(2,1)} %tests_in.1, bf16[136,384]{1,0:T(8,128)(2,1)S(1)} %collective-permute-done.3.refs_0_, f32[1,1,128,384]{3,2,1,0:T(8,128)S(1)} %get-tuple-element.48.refs_1_), custom_call_target="tpu_custom_call" | custom-call | bytes 4194304 | tf_op jit(solution)/shard_map/pallas_call | solution.py:234
  51.8 0.4 collective-permute-done.7.refs_0_
  52.2 0.9 %shard_map.103 = (f32[2,16,64]{2,1,0:T(8,128)S(1)}, f32[2,16,64]{2,1,0:T(8,128)S(1)}) custom-call(s32[4]{0:T(128)S(1)} %pad_add_fusion.where_ref, f32[64,64]{1,0:T(8,128)S(1)} %get-tuple-element.49.early_ref, bf16[136,256]{1,0:T(8,128)(2,1)S(1)} %collective-permute-done.7.refs_0_, f32[1,1,128,256]{3,2,1,0:T(8,128)S(1)} %get-tuple-element.57.refs_1_, ...), custom_call_target="tpu_custom_call" | custom-call | bytes 2097152 | tf_op jit(solution)/shard_map/pallas_call | solution.py:234
  53.1 0.1 collective-permute-start.11
  53.2 1.2 %collective-permute-done.11 = f32[2,16,64]{2,1,0:T(8,128)S(1)} collective-permute-done((f32[2,16,64]{2,1,0:T(8,128)S(1)}, f32[2,16,64]{2,1,0:T(8,128)S(1)}, u32[]{:S(2)}, u32[]{:S(2)}) %collective-permute-start.11) | collective-permute-done | bytes 8224 | tf_op jit(solution)/shard_map/ppermute | solution.py:228
  54.4 1.5 %collective-permute-start.12 = (f32[16,64]{1,0:T(8,128)S(1)}, f32[16,64]{1,0:T(8,128)S(1)}, u32[]{:S(2)}, u32[]{:S(2)}) collective-permute-start(f32[16,64]{1,0:T(8,128)S(1)} %dynamic-slice_bitcast_fusion), channel_id=1, source_target_pairs={{0,2},{1,3},{2,0},{3,1},{4,6},{5,7},{6,4},{7,5},{8,10},{9,11},{10,... | collective-permute-start | bytes 12296 | tf_op jit(solution)/shard_map/ppermute | solution.py:228
  55.9 2.2 %collective-permute-done.12 = f32[16,64]{1,0:T(8,128)S(1)} collective-permute-done((f32[16,64]{1,0:T(8,128)S(1)}, f32[16,64]{1,0:T(8,128)S(1)}, u32[]{:S(2)}, u32[]{:S(2)}) %collective-permute-start.12) | collective-permute-done | bytes 4128 | tf_op jit(solution)/shard_map/ppermute | solution.py:228
  58.1 0.1 stack.29
  58.1 0.1 stack.30
  58.2 0.7 scores.1
  58.9 0.0 collective-permute-start.13
  58.9 1.2 %collective-permute-done.13 = f32[2,1024]{1,0:T(2,128)S(1)} collective-permute-done((f32[2,1024]{1,0:T(2,128)S(1)}, f32[2,1024]{1,0:T(2,128)S(1)}, u32[]{:S(2)}, u32[]{:S(2)}) %collective-permute-start.13) | collective-permute-done | bytes 8224 | tf_op jit(solution)/shard_map/ppermute | solution.py:228
  60.1 1.5 %collective-permute-start.14 = (f32[2,1024]{1,0:T(2,128)S(1)}, f32[2,1024]{1,0:T(2,128)S(1)}, u32[]{:S(2)}, u32[]{:S(2)}) collective-permute-start(f32[2,1024]{1,0:T(2,128)S(1)} %add.42), channel_id=1, source_target_pairs={{0,2},{1,3},{2,0},{3,1},{4,6},{5,7},{6,4},{7,5},{8,10},{9,11},{10,... | collective-permute-start | bytes 24584 | tf_op jit(solution)/shard_map/ppermute | solution.py:228
  61.6 2.2 %collective-permute-done.14 = f32[2,1024]{1,0:T(2,128)S(1)} collective-permute-done((f32[2,1024]{1,0:T(2,128)S(1)}, f32[2,1024]{1,0:T(2,128)S(1)}, u32[]{:S(2)}, u32[]{:S(2)}) %collective-permute-start.14) | collective-permute-done | bytes 8224 | tf_op jit(solution)/shard_map/ppermute | solution.py:228
  63.7 0.0 collective-permute-start.15
  63.8 3.6 %collective-permute-done.15 = f32[2,1024]{1,0:T(2,128)S(1)} collective-permute-done((f32[2,1024]{1,0:T(2,128)S(1)}, f32[2,1024]{1,0:T(2,128)S(1)}, u32[]{:S(2)}, u32[]{:S(2)}) %collective-permute-start.15) | collective-permute-done | bytes 8224 | tf_op jit(solution)/shard_map/ppermute | solution.py:228
  67.4 1.3 %collective-permute-start.16 = (f32[2,1024]{1,0:T(2,128)S(1)}, f32[2,1024]{1,0:T(2,128)S(1)}, u32[]{:S(2)}, u32[]{:S(2)}) collective-permute-start(f32[2,1024]{1,0:T(2,128)S(1)} %add.44), channel_id=1, source_target_pairs={{0,8},{1,9},{2,10},{3,11},{4,12},{5,13},{6,14},{7,15},{8,0},{9,1},... | collective-permute-start | bytes 24584 | tf_op jit(solution)/shard_map/ppermute | solution.py:228
  68.7 3.3 %collective-permute-done.16 = f32[2,1024]{1,0:T(2,128)S(1)} collective-permute-done((f32[2,1024]{1,0:T(2,128)S(1)}, f32[2,1024]{1,0:T(2,128)S(1)}, u32[]{:S(2)}, u32[]{:S(2)}) %collective-permute-start.16) | collective-permute-done | bytes 8224 | tf_op jit(solution)/shard_map/ppermute | solution.py:228
  72.0 0.6 add.45
  (11 shorter events, 0.1 us)
Async XLA Ops:
  7.1 6.2 %collective-permute-start.4 = (f32[2,2,128,1280]{3,2,1,0:T(8,128)S(1)}, f32[2,2,128,1280]{3,2,1,0:T(8,128)S(1)}, u32[]{:S(2)}, u32[]{:S(2)}) collective-permute-start(f32[2,2,128,1280]{3,2,1,0:T(8,128)S(1)} %get-tuple-element.51), channel_id=1, source_target_pairs={{0,1},{1,0},{2,3},{3,2},{4,5},{5,4},{6,7},{7,6},{8,9},{9,8},{10,11... | collective-permute-start | bytes 7864328 | tf_op jit(solution)/shard_map/ppermute | solution.py:228
  7.7 9.7 %collective-permute-start = (f32[2,2,128,768]{3,2,1,0:T(8,128)S(1)}, f32[2,2,128,768]{3,2,1,0:T(8,128)S(1)}, u32[]{:S(2)}, u32[]{:S(2)}) collective-permute-start(f32[2,2,128,768]{3,2,1,0:T(8,128)S(1)} %get-tuple-element.42), channel_id=1, source_target_pairs={{0,1},{1,0},{2,3},{3,2},{4,5},{5,4},{6,7},{7,6},{8,9},{9,8},{10,11... | collective-permute-start | bytes 4718600 | tf_op jit(solution)/shard_map/ppermute | solution.py:228
  14.3 17.3 %collective-permute-start.8 = (bf16[264,768]{1,0:T(8,128)(2,1)S(1)}, bf16[264,768]{1,0:T(8,128)(2,1)S(1)}, u32[]{:S(2)}, u32[]{:S(2)}) collective-permute-start(bf16[264,768]{1,0:T(8,128)(2,1)S(1)} %get-tuple-element.58), channel_id=1, source_target_pairs={{0,4},{1,5},{2,6},{3,7},{4,0},{5,1},{6,2},{7,3},{8,12},{9,13},{10,... | collective-permute-start | bytes 1216520 | tf_op jit(solution)/shard_map/ppermute | solution.py:228
  18.3 12.2 %collective-permute-start.1 = (bf16[520,384]{1,0:T(8,128)(2,1)S(1)}, bf16[520,384]{1,0:T(8,128)(2,1)S(1)}, u32[]{:S(2)}, u32[]{:S(2)}) collective-permute-start(bf16[520,384]{1,0:T(8,128)(2,1)S(1)} %get-tuple-element.43), channel_id=1, source_target_pairs={{0,2},{1,3},{2,0},{3,1},{4,6},{5,7},{6,4},{7,5},{8,10},{9,11},{10,... | collective-permute-start | bytes 1198088 | tf_op jit(solution)/shard_map/ppermute | solution.py:228
  20.7 15.5 %collective-permute-start.5 = (bf16[520,256]{1,0:T(8,128)(2,1)S(1)}, bf16[520,256]{1,0:T(8,128)(2,1)S(1)}, u32[]{:S(2)}, u32[]{:S(2)}) collective-permute-start(bf16[520,256]{1,0:T(8,128)(2,1)S(1)} %get-tuple-element.52), channel_id=1, source_target_pairs={{0,2},{1,3},{2,0},{3,1},{4,6},{5,7},{6,4},{7,5},{8,10},{9,11},{10,... | collective-permute-start | bytes 798728 | tf_op jit(solution)/shard_map/ppermute | solution.py:228
  31.5 5.8 %collective-permute-start.2 = (bf16[264,384]{1,0:T(8,128)(2,1)S(1)}, bf16[264,384]{1,0:T(8,128)(2,1)S(1)}, u32[]{:S(2)}, u32[]{:S(2)}) collective-permute-start(bf16[264,384]{1,0:T(8,128)(2,1)S(1)} %get-tuple-element.45), channel_id=1, source_target_pairs={{0,4},{1,5},{2,6},{3,7},{4,0},{5,1},{6,2},{7,3},{8,12},{9,13},{10,... | collective-permute-start | bytes 608264 | tf_op jit(solution)/shard_map/ppermute | solution.py:228
  32.6 8.0 %collective-permute-start.9 = (bf16[264,384]{1,0:T(8,128)(2,1)S(1)}, bf16[264,384]{1,0:T(8,128)(2,1)S(1)}, u32[]{:S(2)}, u32[]{:S(2)}) collective-permute-start(bf16[264,384]{1,0:T(8,128)(2,1)S(1)} %get-tuple-element.60), channel_id=1, source_target_pairs={{0,2},{1,3},{2,0},{3,1},{4,6},{5,7},{6,4},{7,5},{8,10},{9,11},{10,... | collective-permute-start | bytes 608264 | tf_op jit(solution)/shard_map/ppermute | solution.py:228
  37.0 5.8 %collective-permute-start.6 = (bf16[264,256]{1,0:T(8,128)(2,1)S(1)}, bf16[264,256]{1,0:T(8,128)(2,1)S(1)}, u32[]{:S(2)}, u32[]{:S(2)}) collective-permute-start(bf16[264,256]{1,0:T(8,128)(2,1)S(1)} %get-tuple-element.54), channel_id=1, source_target_pairs={{0,4},{1,5},{2,6},{3,7},{4,0},{5,1},{6,2},{7,3},{8,12},{9,13},{10,... | collective-permute-start | bytes 405512 | tf_op jit(solution)/shard_map/ppermute | solution.py:228
  38.0 11.6 %collective-permute-start.3 = (bf16[136,384]{1,0:T(8,128)(2,1)S(1)}, bf16[136,384]{1,0:T(8,128)(2,1)S(1)}, u32[]{:S(2)}, u32[]{:S(2)}) collective-permute-start(bf16[136,384]{1,0:T(8,128)(2,1)S(1)} %get-tuple-element.47), channel_id=1, source_target_pairs={{0,8},{1,9},{2,10},{3,11},{4,12},{5,13},{6,14},{7,15},{8,0},{9,1},... | collective-permute-start | bytes 313352 | tf_op jit(solution)/shard_map/ppermute | solution.py:228
  41.5 10.8 %collective-permute-start.10 = (bf16[136,384]{1,0:T(8,128)(2,1)S(1)}, bf16[136,384]{1,0:T(8,128)(2,1)S(1)}, u32[]{:S(2)}, u32[]{:S(2)}) collective-permute-start(bf16[136,384]{1,0:T(8,128)(2,1)S(1)} %get-tuple-element.62), channel_id=1, source_target_pairs={{0,8},{1,9},{2,10},{3,11},{4,12},{5,13},{6,14},{7,15},{8,0},{9,1},... | collective-permute-start | bytes 313352 | tf_op jit(solution)/shard_map/ppermute | solution.py:228
  43.5 8.8 %collective-permute-start.7 = (bf16[136,256]{1,0:T(8,128)(2,1)S(1)}, bf16[136,256]{1,0:T(8,128)(2,1)S(1)}, u32[]{:S(2)}, u32[]{:S(2)}) collective-permute-start(bf16[136,256]{1,0:T(8,128)(2,1)S(1)} %get-tuple-element.56), channel_id=1, source_target_pairs={{0,8},{1,9},{2,10},{3,11},{4,12},{5,13},{6,14},{7,15},{8,0},{9,1},... | collective-permute-start | bytes 208904 | tf_op jit(solution)/shard_map/ppermute | solution.py:228
  53.1 1.2 %collective-permute-start.11 = (f32[2,16,64]{2,1,0:T(8,128)S(1)}, f32[2,16,64]{2,1,0:T(8,128)S(1)}, u32[]{:S(2)}, u32[]{:S(2)}) collective-permute-start(f32[2,16,64]{2,1,0:T(8,128)S(1)} %get-tuple-element.65), channel_id=1, source_target_pairs={{0,1},{1,0},{2,3},{3,2},{4,5},{5,4},{6,7},{7,6},{8,9},{9,8},{10,11... | collective-permute-start | bytes 24584 | tf_op jit(solution)/shard_map/ppermute | solution.py:228
  54.4 3.7 %collective-permute-start.12 = (f32[16,64]{1,0:T(8,128)S(1)}, f32[16,64]{1,0:T(8,128)S(1)}, u32[]{:S(2)}, u32[]{:S(2)}) collective-permute-start(f32[16,64]{1,0:T(8,128)S(1)} %dynamic-slice_bitcast_fusion), channel_id=1, source_target_pairs={{0,2},{1,3},{2,0},{3,1},{4,6},{5,7},{6,4},{7,5},{8,10},{9,11},{10,... | collective-permute-start | bytes 12296 | tf_op jit(solution)/shard_map/ppermute | solution.py:228
  58.9 1.2 %collective-permute-start.13 = (f32[2,1024]{1,0:T(2,128)S(1)}, f32[2,1024]{1,0:T(2,128)S(1)}, u32[]{:S(2)}, u32[]{:S(2)}) collective-permute-start(f32[2,1024]{1,0:T(2,128)S(1)} %scores.1), channel_id=1, source_target_pairs={{0,1},{1,0},{2,3},{3,2},{4,5},{5,4},{6,7},{7,6},{8,9},{9,8},{10,11... | collective-permute-start | bytes 24584 | tf_op jit(solution)/shard_map/ppermute | solution.py:228
  60.1 3.7 %collective-permute-start.14 = (f32[2,1024]{1,0:T(2,128)S(1)}, f32[2,1024]{1,0:T(2,128)S(1)}, u32[]{:S(2)}, u32[]{:S(2)}) collective-permute-start(f32[2,1024]{1,0:T(2,128)S(1)} %add.42), channel_id=1, source_target_pairs={{0,2},{1,3},{2,0},{3,1},{4,6},{5,7},{6,4},{7,5},{8,10},{9,11},{10,... | collective-permute-start | bytes 24584 | tf_op jit(solution)/shard_map/ppermute | solution.py:228
  63.7 3.7 %collective-permute-start.15 = (f32[2,1024]{1,0:T(2,128)S(1)}, f32[2,1024]{1,0:T(2,128)S(1)}, u32[]{:S(2)}, u32[]{:S(2)}) collective-permute-start(f32[2,1024]{1,0:T(2,128)S(1)} %add.43), channel_id=1, source_target_pairs={{0,4},{1,5},{2,6},{3,7},{4,0},{5,1},{6,2},{7,3},{8,12},{9,13},{10,... | collective-permute-start | bytes 24584 | tf_op jit(solution)/shard_map/ppermute | solution.py:228
  67.4 4.5 %collective-permute-start.16 = (f32[2,1024]{1,0:T(2,128)S(1)}, f32[2,1024]{1,0:T(2,128)S(1)}, u32[]{:S(2)}, u32[]{:S(2)}) collective-permute-start(f32[2,1024]{1,0:T(2,128)S(1)} %add.44), channel_id=1, source_target_pairs={{0,8},{1,9},{2,10},{3,11},{4,12},{5,13},{6,14},{7,15},{8,0},{9,1},... | collective-permute-start | bytes 24584 | tf_op jit(solution)/shard_map/ppermute | solution.py:228
